TPU v7x, 256 devices: a whole 4x4x8 slice. The times are simulated.
256 devices in a mesh: seq: 32 (over z, y), tp: 8 (over x, core).
Axes of the slice: x: 4, y: 4, z: 8, core: 2. Of those that a mesh axis runs over, the one named last changes fastest.
Arguments:
- gate: bfloat16 [8192, 8192], P('seq', 'tp'), may hold values from -6 to 6
- conv_input: bfloat16 [8192, 8192], P('seq', 'tp'), may hold values from -6 to 6
- filters: bfloat16 [512, 128], P('tp'), may hold values from -0.5 to 0.5
- out_weight: bfloat16 [4096, 8192], P('seq', 'tp'), may hold values from -0.0625 to 0.0625
- upstream: bfloat16 [8192, 4096], P('seq', 'tp'), may hold values from -12 to 12
Outputs:
- grad_gate: bfloat16 [8192, 8192], P('seq', 'tp')
- grad_input: bfloat16 [8192, 8192], P('seq', 'tp')
- grad_filter: float32 [512, 128], P('tp')
- grad_weight: bfloat16 [4096, 8192], P('seq', 'tp')
All inputs are finite; a program needn't handle non-finite values.
Results may differ from a plain program's by a relative error of at most 0.018.
Values may be sent and summed in bfloat16 or wider, within the bound.
No kernel may reach another device: no remote copies, remote signals or barrier semaphores. Data moves between devices by JAX's collectives and lax.ppermute only.
A program may use at most 128 MiB of HBM per device.

v0:
```python
import jax
import jax.numpy as jnp
from jax import lax
from jax.experimental import pallas as pl
from jax.experimental.pallas import tpu as pltpu
from jax.sharding import Mesh
from jax.sharding import PartitionSpec as P

GROUP = 16
TAPS = 128
LANES = 128
F32 = jnp.float32
BF16 = jnp.bfloat16
SIZES = {"z": 8, "y": 4, "x": 4, "c": 2}
SEQ = ("z", "y")
GRANT = pltpu.CompilerParams(vmem_limit_bytes=20 << 20)
TP = ("x", "c")


def shift(block, axis, distance):
    size = SIZES[axis]
    route = [(i, (i + distance) % size) for i in range(size)]
    return lax.ppermute(block, axis, route)


def exchanged(blocks, axis):
    return lax.all_to_all(blocks, axis, split_axis=0, concat_axis=0, tiled=True)


def from_behind(block, distance):
    devices = range(SIZES["z"] * SIZES["y"])
    route = [(i - distance, i) for i in devices if i - distance in devices]
    return lax.ppermute(block, SEQ, route)


def rows_and_cols():
    row = lax.broadcasted_iota(jnp.int32, (TAPS, TAPS), 0)
    col = lax.broadcasted_iota(jnp.int32, (TAPS, TAPS), 1)
    return row, col


def lane_group(shape):
    return lax.broadcasted_iota(jnp.int32, shape, len(shape) - 1) % LANES // GROUP


def pick_groups(stacked):
    lanes = lane_group((TAPS, 2 * LANES))
    out = stacked[:TAPS]
    for g in range(1, LANES // GROUP):
        out = jnp.where(lanes == g, stacked[g * TAPS : (g + 1) * TAPS], out)
    return out


STEP = 512


def tiles():
    return [slice(at, at + LANES) for at in range(0, STEP, LANES)]


def group_rows(at):
    return slice(at // GROUP, (at + LANES) // GROUP)


def banded(rings, first):
    bands = []
    for ring in rings:
        left = jnp.where(first, ring, 0.0)
        right = jnp.where(first, 0.0, ring)
        bands.append(jnp.concatenate([left, right], axis=1).astype(BF16))
    return jnp.concatenate(bands, axis=0)


def rings_of(taps, turn):
    out = []
    for g in range(LANES // GROUP):
        wide = jnp.broadcast_to(taps[g : g + 1], (TAPS, TAPS))
        out.append(pltpu.roll(wide, turn, 1, stride=1, stride_axis=0))
    return out


def conv_kernel(prev_ref, x_ref, gate_ref, taps_ref, mixed_ref, out_ref):
    row, col = rows_and_cols()
    flip = jnp.where(row + col == TAPS - 1, 1.0, 0.0).astype(BF16)
    taps = jnp.dot(taps_ref[...], flip, preferred_element_type=F32)
    for at in tiles():
        band = banded(rings_of(taps[group_rows(at.start)], 1), col > row)
        x0, x1 = x_ref[:TAPS, at], x_ref[TAPS:, at]
        first = jnp.concatenate([prev_ref[:, at], x0], axis=0)
        second = jnp.concatenate([x0, x1], axis=0)
        window = jnp.concatenate([first, second], axis=1)
        conv = pick_groups(jnp.dot(band, window, preferred_element_type=F32))
        conv = jnp.concatenate([conv[:, :LANES], conv[:, LANES:]], axis=0)
        out_ref[:, at] = conv
        mixed_ref[:, at] = (gate_ref[:, at].astype(F32) * conv).astype(BF16)


def tile(rows):
    return pl.BlockSpec((rows, STEP), lambda i: (0, i))


def taps_tile():
    return pl.BlockSpec((STEP // GROUP, TAPS), lambda i: (i, 0))


def conv_forward(prev, x, gate, filters):
    rows, channels = x.shape
    return pl.pallas_call(
        conv_kernel,
        grid=(channels // STEP,),
        in_specs=[tile(TAPS), tile(rows), tile(rows), taps_tile()],
        out_specs=[tile(rows), tile(rows)],
        out_shape=[
            jax.ShapeDtypeStruct(x.shape, BF16),
            jax.ShapeDtypeStruct(x.shape, F32),
        ],
        name="conv_forward",
        compiler_params=GRANT,
    )(prev, x, gate, filters)


def back_kernel(d_ref, next_ref, taps_ref, out_ref):
    row, col = rows_and_cols()
    taps = taps_ref[...].astype(F32)
    for at in tiles():
        band = banded(rings_of(taps[group_rows(at.start)], 0), col >= row)
        d0, d1 = d_ref[:TAPS, at], d_ref[TAPS:, at]
        first = jnp.concatenate([d0, d1], axis=0)
        second = jnp.concatenate([d1, next_ref[:, at]], axis=0)
        window = jnp.concatenate([first, second], axis=1)
        conv = pick_groups(jnp.dot(band, window, preferred_element_type=F32))
        out_ref[:TAPS, at] = conv[:, :LANES].astype(BF16)
        out_ref[TAPS:, at] = conv[:, LANES:].astype(BF16)


def conv_backward(d_conv, following, filters):
    rows, channels = d_conv.shape
    return pl.pallas_call(
        back_kernel,
        grid=(channels // STEP,),
        in_specs=[tile(rows), tile(TAPS), taps_tile()],
        out_specs=tile(rows),
        out_shape=jax.ShapeDtypeStruct(d_conv.shape, BF16),
        name="conv_backward",
        compiler_params=GRANT,
    )(d_conv, following, filters)


def gradient_kernel(*refs):
    terms, (conv_ref, gate_ref, prev_ref, x_ref) = refs[:4], refs[4:8]
    grad_gate_ref, d_ref, head_ref, out_ref = refs[8:]
    row, col = rows_and_cols()
    flip = jnp.where(row + col == TAPS - 1, 1.0, 0.0).astype(BF16)
    keep = col + row >= TAPS - 1

    def flipped(block):
        return jnp.dot(flip, block, preferred_element_type=F32).astype(BF16)

    prev, x0, x1 = flipped(prev_ref[...]), flipped(x_ref[:TAPS]), flipped(x_ref[TAPS:])
    for at in tiles():
        d_out = sum(term[:, at].astype(F32) for term in terms)
        grad_gate_ref[:, at] = (d_out * conv_ref[:, at]).astype(BF16)
        d_conv = (d_out * gate_ref[:, at].astype(F32)).astype(BF16)
        d_ref[:, at] = d_conv
        head_ref[:, at] = d_conv[:TAPS]
        first = jnp.concatenate([prev[:, at], x0[:, at]], axis=0)
        second = jnp.concatenate([x0[:, at], x1[:, at]], axis=0)
        window = jnp.concatenate([first, second], axis=1)
        both = jnp.concatenate([d_conv[:TAPS], d_conv[TAPS:]], axis=1)
        lanes = lane_group(both.shape)
        zero = jnp.zeros_like(both)
        left = [jnp.where(lanes == g, both, zero) for g in range(LANES // GROUP)]
        left = jnp.concatenate(left, axis=0)
        table = lax.dot_general(
            left, window, (((1,), (1,)), ((), ())), preferred_element_type=F32
        )
        sums = []
        for g in range(LANES // GROUP):
            part = table[g * TAPS : (g + 1) * TAPS]
            ring = jnp.where(keep, part[:, TAPS:], part[:, :TAPS])
            ring = pltpu.roll(ring, 1, 1, stride=1, stride_axis=0)
            sums.append(jnp.sum(ring, axis=0, keepdims=True))
        out_ref[group_rows(at.start)] = jnp.concatenate(sums, axis=0)


def output_gradients(terms, conv_out, gate, prev, x):
    rows, channels = x.shape
    return pl.pallas_call(
        gradient_kernel,
        grid=(channels // STEP,),
        in_specs=[tile(rows)] * 6 + [tile(TAPS), tile(rows)],
        out_specs=[tile(rows), tile(rows), tile(TAPS), taps_tile()],
        out_shape=[
            jax.ShapeDtypeStruct(x.shape, BF16),
            jax.ShapeDtypeStruct(x.shape, BF16),
            jax.ShapeDtypeStruct(prev.shape, BF16),
            jax.ShapeDtypeStruct((channels // GROUP, TAPS), F32),
        ],
        name="output_gradients",
        compiler_params=GRANT,
    )(*terms, conv_out, gate, prev, x)


ANY = pl.BlockSpec(memory_space=pl.ANY)
VMEM = pl.BlockSpec(memory_space=pltpu.VMEM)


def on_chip(block):
    return pltpu.with_memory_space_constraint(block, pltpu.VMEM)


def place_features(pieces, scratch):
    x, c = lax.axis_index("x"), lax.axis_index("c")
    out = []
    for at, piece in enumerate(pieces):
        owner_c = c if at < 4 else 1 - c
        owner = 2 * lax.rem(x - at % 4 + 4, 4) + owner_c
        start = pl.multiple_of(owner * LANES, LANES)
        out.append((piece, scratch.at[:, pl.ds(start, LANES)]))
    return out


def run_copies(pairs, sems):
    copies = [
        pltpu.make_async_copy(source, target, sems.at[at])
        for at, (source, target) in enumerate(pairs)
    ]
    for copy in copies:
        copy.start()
    for copy in copies:
        copy.wait()


def output_kernel(*refs):
    u_refs, w_refs, outs = refs[:8], refs[8:17], refs[17:21]
    u_all, w_all, sems = refs[21:]
    z, y = lax.axis_index("z"), lax.axis_index("y")
    pairs = place_features(u_refs, u_all)
    for at, k in enumerate((0, 1, 2, 3, -1, -2, -3)):
        start = pl.multiple_of(lax.rem(z - k + 8, 8) * LANES, LANES)
        pairs.append((w_refs[at], w_all.at[pl.ds(start, LANES)]))
    far = pl.multiple_of(lax.rem(z + 4, 8) * LANES, LANES)
    half = LANES // 2
    pairs.append((w_refs[7], w_all.at[pl.ds(far, half)]))
    pairs.append((w_refs[8], w_all.at[pl.ds(pl.multiple_of(far + half, half), half)]))
    run_copies(pairs, sems)
    rows = outs[0].shape[0]
    for d, out in enumerate(outs):
        start = pl.multiple_of(lax.rem(y + d, 4) * rows, rows)
        out[...] = jnp.dot(
            u_all[pl.ds(start, rows)], w_all[...], preferred_element_type=F32
        ).astype(BF16)


def output_partials(features, weights):
    tokens, channels = features[0].shape[0], weights[0].shape[1]
    shape = jax.ShapeDtypeStruct((tokens // 4, channels), BF16)
    return pl.pallas_call(
        output_kernel,
        in_specs=[VMEM] * 17,
        out_specs=[VMEM] * 4,
        out_shape=[shape] * 4,
        scratch_shapes=[
            pltpu.VMEM((tokens, 8 * LANES), BF16),
            pltpu.VMEM((8 * LANES, channels), BF16),
            pltpu.SemaphoreType.DMA((17,)),
        ],
        name="output_partials",
        compiler_params=GRANT,
    )(*map(on_chip, (*features, *weights)))


HOPS = (3, -3, 2, -2, 1, -1, 0)


def weight_kernel(*refs):
    u_refs, m_refs, far_refs, outs = refs[:8], refs[8:12], refs[13:15], refs[15:22]
    u_all, m_all, sems = refs[22:]
    z, y = lax.axis_index("z"), lax.axis_index("y")
    pairs = place_features(u_refs, u_all)
    rows = m_refs[0].shape[0]
    for d, m_ref in enumerate(m_refs):
        start = pl.multiple_of(lax.rem(y - d + 4, 4) * rows, rows)
        pairs.append((m_ref, m_all.at[pl.ds(start, rows)]))
    run_copies(pairs, sems)

    def block(hop):
        start = pl.multiple_of(lax.rem(z + hop + 8, 8) * LANES, LANES)
        return lax.dot_general(
            u_all[:, pl.ds(start, LANES)],
            m_all[...],
            (((0,), (0,)), ((), ())),
            preferred_element_type=F32,
        ).astype(BF16)

    far = block(4)
    half = LANES // 2
    far_refs[0][...] = far[:half]
    far_refs[1][...] = far[half:]
    for out, hop in zip(outs, HOPS):
        out[...] = block(hop)


def weight_partials(features, mixed, after):
    tokens, channels = features[0].shape[0], mixed[0].shape[1]
    shape = jax.ShapeDtypeStruct((LANES, channels), BF16)
    short = jax.ShapeDtypeStruct((LANES // 2, channels), BF16)
    return pl.pallas_call(
        weight_kernel,
        in_specs=[VMEM] * 12 + [ANY],
        out_specs=[VMEM] * 9,
        out_shape=[short] * 2 + [shape] * 7,
        scratch_shapes=[
            pltpu.VMEM((tokens, 8 * LANES), BF16),
            pltpu.VMEM((tokens, channels), BF16),
            pltpu.SemaphoreType.DMA((12,)),
        ],
        name="weight_partials",
        compiler_params=GRANT,
    )(*map(on_chip, (*features, *mixed)), after)


def add_kernel(ahead_ref, behind_ref, first_ref, last_ref, ahead_out, behind_out):
    rows, half = ahead_ref.shape[0], LANES // 2
    for got, own, out, start in (
        (ahead_ref, first_ref, ahead_out, 0),
        (behind_ref, last_ref, behind_out, LANES - rows),
    ):
        if rows == half:
            other = slice(half - start, LANES - start)
            out[other] = own[other]
        span = slice(start, start + rows)
        out[span] = (got[...].astype(F32) + own[span].astype(F32)).astype(BF16)


def add_pair(ahead, behind, first, last):
    shape = jax.ShapeDtypeStruct(first.shape, BF16)
    return pl.pallas_call(
        add_kernel,
        in_specs=[VMEM] * 4,
        out_specs=[VMEM] * 2,
        out_shape=[shape] * 2,
        compiler_params=GRANT,
    )(*map(on_chip, (ahead, behind, first, last)))


def block_backward(gate, conv_input, filters, out_weight, upstream):
    rows, _ = conv_input.shape
    half = LANES // 2
    factor = (rows * SIZES["z"] * SIZES["y"]) ** (-0.5)

    ahead, behind = out_weight, out_weight
    forward, backward = [], []
    for _ in range(3):
        ahead = shift(ahead, "z", 1)
        behind = shift(behind, "z", -1)
        forward.append(ahead)
        backward.append(behind)
    weights = [out_weight] + forward + backward
    weights.append(shift(ahead[:half], "z", 1))
    weights.append(shift(behind[half:], "z", -1))

    split = jnp.moveaxis(upstream.reshape(rows, 4, LANES), 1, 0)
    own = exchanged(split, "y").reshape(4 * rows, LANES)
    near = [own] + [shift(own, "x", k) for k in (1, 2, 3)]
    features = near + [shift(near[k], "c", 1) for k in range(4)]

    prior = from_behind(conv_input[rows - TAPS :], 1)
    mixed, conv_out = conv_forward(prior, conv_input, gate, filters)
    mixed = [mixed] + [shift(mixed, "y", d) for d in (1, 2, 3)]

    partials = output_partials(features, weights)
    terms = [partials[0]] + [shift(partials[d], "y", d) for d in (1, 2, 3)]

    ahead, behind, *blocks = weight_partials(features, mixed, partials[0])
    for step in (1, 2, 3):
        ahead = shift(ahead, "z", 1)
        behind = shift(behind, "z", -1)
        pair = blocks[2 * step - 2], blocks[2 * step - 1]
        ahead, behind = add_pair(ahead, behind, *pair)
    ahead, behind = shift(ahead, "z", 1), shift(behind, "z", -1)
    summed = sum(term.astype(F32) for term in (blocks[6], ahead, behind))
    grad_weight = (summed * factor).astype(BF16)

    grad_gate, d_conv, head, local = output_gradients(
        terms, conv_out, gate, prior, conv_input
    )
    following = from_behind(head, -1)
    local = local + sum(shift(local, "y", d) for d in (1, 2, 3))
    below, above = shift(local, "z", 1), shift(local, "z", -1)
    pair = local + above
    local = pair + below
    local = local + shift(local, "z", -3) + shift(pair, "z", 3)
    grad_filter = local * factor
    grad_input = conv_backward(d_conv, following, filters)
    return (grad_gate, grad_input, grad_filter, grad_weight)


def solution(mesh):
    finer = Mesh(mesh.devices.reshape(8, 4, 4, 2), ("z", "y", "x", "c"))
    return jax.shard_map(
        block_backward,
        mesh=finer,
        in_specs=(P(SEQ, TP), P(SEQ, TP), P(TP, None), P(SEQ, TP), P(SEQ, TP)),
        out_specs=(P(SEQ, TP), P(SEQ, TP), P(TP, None), P(SEQ, TP)),
        check_vma=False,
    )
```

profile of v0, /device:TPU:32, one launch (start us, length us, event | category | flops | bytes accessed | tf_op | source)
XLA Modules:
  0.0 127.9 jit_solution(14583036440615006739)
XLA Ops:
  0.7 2.0 %collective-permute-start.7 = (bf16[128,1024]{1,0:T(8,128)(2,1)}, bf16[128,1024]{1,0:T(8,128)(2,1)S(1)}, u32[]{:S(2)}, u32[]{:S(2)}) collective-permute-start(bf16[128,1024]{1,0:T(8,128)(2,1)} %refs_8_.1), channel_id=1, source_target_pairs={{0,32},{32,64},{64,96},{96,128},{128,160},{160,192},{192,224},{224... | collective-permute-start | bytes 786440 | tf_op jit(solution)/shard_map/ppermute | solution.py:23
  3.5 4.6 %all-to-all-start = ((bf16[4,256,128]{2,1,0:T(8,128)(2,1)}), bf16[4,256,128]{2,1,0:T(8,128)(2,1)S(1)}, u32[]{:S(2)}, u32[]{:S(2)}) async-start(bf16[4,256,128]{2,1,0:T(8,128)(2,1)} %bitcast_bitcast_fusion), calls=%async_computation | async-start | bytes 524288 | tf_op jit(solution)/shard_map/all_to_all | solution.py:27
  8.1 3.9 %collective-permute-start.18 = (bf16[128,1024]{1,0:T(8,128)(2,1)S(1)}, bf16[128,1024]{1,0:T(8,128)(2,1)S(1)}, u32[]{:S(2)}, u32[]{:S(2)}) collective-permute-start(bf16[128,1024]{1,0:T(8,128)(2,1)S(1)} %slice.11), channel_id=1, source_target_pairs={{0,8},{8,16},{16,24},{24,32},{32,40},{40,48},{48,56},{56,64},{64,7... | collective-permute-start | bytes 786440 | tf_op jit(solution)/shard_map/ppermute | solution.py:33
  12.1 3.3 %all-to-all-done = bf16[4,256,128]{2,1,0:T(8,128)(2,1)S(1)} async-done(((bf16[4,256,128]{2,1,0:T(8,128)(2,1)}), bf16[4,256,128]{2,1,0:T(8,128)(2,1)S(1)}, u32[]{:S(2)}, u32[]{:S(2)}) %all-to-all-start) | async-done | bytes 262176 | tf_op jit(solution)/shard_map/all_to_all | solution.py:27
  15.4 2.8 %collective-permute-start.2 = (bf16[1024,128]{1,0:T(8,128)(2,1)S(1)}, bf16[1024,128]{1,0:T(8,128)(2,1)S(1)}, u32[]{:S(2)}, u32[]{:S(2)}) collective-permute-start(bf16[1024,128]{1,0:T(8,128)(2,1)S(1)} %bitcast.9), channel_id=1, source_target_pairs={{0,6},{2,0},{4,2},{6,4},{1,7},{3,1},{5,3},{7,5},{8,14},{10,8},{12,... | collective-permute-start | bytes 786440 | tf_op jit(solution)/shard_map/ppermute | solution.py:23
  18.2 2.5 %collective-permute-start.8 = (bf16[128,1024]{1,0:T(8,128)(2,1)S(1)}, bf16[128,1024]{1,0:T(8,128)(2,1)S(1)}, u32[]{:S(2)}, u32[]{:S(2)}) collective-permute-start(bf16[128,1024]{1,0:T(8,128)(2,1)S(1)} %collective-permute-done.7.refs_9_), channel_id=1, source_target_pairs={{0,32},{32,64},{64,96},{96,128},{128,160},{160,192},{192,224},{224... | collective-permute-start | bytes 786440 | tf_op jit(solution)/shard_map/ppermute | solution.py:23
  22.2 4.2 %collective-permute-start.1 = (bf16[1024,128]{1,0:T(8,128)(2,1)S(1)}, bf16[1024,128]{1,0:T(8,128)(2,1)S(1)}, u32[]{:S(2)}, u32[]{:S(2)}) collective-permute-start(bf16[1024,128]{1,0:T(8,128)(2,1)S(1)} %bitcast.10), channel_id=1, source_target_pairs={{0,4},{2,6},{4,0},{6,2},{1,5},{3,7},{5,1},{7,3},{8,12},{10,14},{12... | collective-permute-start | bytes 786440 | tf_op jit(solution)/shard_map/ppermute | solution.py:23
  27.2 1.5 %collective-permute-done.8.refs_10_ = bf16[128,1024]{1,0:T(8,128)(2,1)S(1)} collective-permute-done((bf16[128,1024]{1,0:T(8,128)(2,1)S(1)}, bf16[128,1024]{1,0:T(8,128)(2,1)S(1)}, u32[]{:S(2)}, u32[]{:S(2)}) %collective-permute-start.8) | collective-permute-done | bytes 262176 | tf_op jit(solution)/shard_map/ppermute | solution.py:23
  28.8 3.8 %collective-permute-start.9 = (bf16[128,1024]{1,0:T(8,128)(2,1)S(1)}, bf16[128,1024]{1,0:T(8,128)(2,1)S(1)}, u32[]{:S(2)}, u32[]{:S(2)}) collective-permute-start(bf16[128,1024]{1,0:T(8,128)(2,1)S(1)} %collective-permute-done.8.refs_10_), channel_id=1, source_target_pairs={{0,32},{32,64},{64,96},{96,128},{128,160},{160,192},{192,224},{224... | collective-permute-start | bytes 786440 | tf_op jit(solution)/shard_map/ppermute | solution.py:23
  34.1 2.1 %conv_forward.1 = (bf16[256,1024]{1,0:T(8,128)(2,1)S(1)}, f32[256,1024]{1,0:T(8,128)S(1)}) custom-call(bf16[128,1024]{1,0:T(8,128)(2,1)S(1)} %collective-permute-done.18.prev_ref.refs_6_, bf16[256,1024]{1,0:T(8,128)(2,1)S(1)} %copy-done.1, bf16[256,1024]{1,0:T(8,128)(2,1)S(1)} %copy-done.2, bf16[64,128]{1,0:T(8,128)(2,1)S(1)} %copy-done.4), custom_call_target="tpu_custom_call" | custom-call | tf_op jit(solution)/shard_map/conv_forward/pallas_call | solution.py:108
  38.0 3.0 %collective-permute-done.9.refs_11_ = bf16[128,1024]{1,0:T(8,128)(2,1)S(1)} collective-permute-done((bf16[128,1024]{1,0:T(8,128)(2,1)S(1)}, bf16[128,1024]{1,0:T(8,128)(2,1)S(1)}, u32[]{:S(2)}, u32[]{:S(2)}) %collective-permute-start.9) | collective-permute-done | bytes 262176 | tf_op jit(solution)/shard_map/ppermute | solution.py:23
  42.5 3.0 %collective-permute-start.13 = (bf16[64,1024]{1,0:T(8,128)(2,1)S(1)}, bf16[64,1024]{1,0:T(8,128)(2,1)S(1)}, u32[]{:S(2)}, u32[]{:S(2)}) collective-permute-start(bf16[64,1024]{1,0:T(8,128)(2,1)S(1)} %slice.12), channel_id=1, source_target_pairs={{0,32},{32,64},{64,96},{96,128},{128,160},{160,192},{192,224},{224... | collective-permute-start | bytes 393224 | tf_op jit(solution)/shard_map/ppermute | solution.py:23
  45.7 2.8 %collective-permute-done.13.refs_15_ = bf16[64,1024]{1,0:T(8,128)(2,1)S(1)} collective-permute-done((bf16[64,1024]{1,0:T(8,128)(2,1)S(1)}, bf16[64,1024]{1,0:T(8,128)(2,1)S(1)}, u32[]{:S(2)}, u32[]{:S(2)}) %collective-permute-start.13) | collective-permute-done | bytes 131104 | tf_op jit(solution)/shard_map/ppermute | solution.py:23
  48.5 2.9 %collective-permute-done.14.refs_16_ = bf16[64,1024]{1,0:T(8,128)(2,1)S(1)} collective-permute-done((bf16[64,1024]{1,0:T(8,128)(2,1)S(1)}, bf16[64,1024]{1,0:T(8,128)(2,1)S(1)}, u32[]{:S(2)}, u32[]{:S(2)}) %collective-permute-start.14) | collective-permute-done | bytes 131104 | tf_op jit(solution)/shard_map/ppermute | solution.py:23
  51.4 3.7 %output_partials.1 = (bf16[256,1024]{1,0:T(8,128)(2,1)S(1)}, bf16[256,1024]{1,0:T(8,128)(2,1)S(1)}, bf16[256,1024]{1,0:T(8,128)(2,1)S(1)}, bf16[256,1024]{1,0:T(8,128)(2,1)S(1)}) custom-call(bf16[1024,128]{1,0:T(8,128)(2,1)S(1)} %bitcast.12, bf16[1024,128]{1,0:T(8,128)(2,1)S(1)} %collective-permute-done.refs_1_, ...), custom_call_target="tpu_custom_call" | custom-call | tf_op jit(solution)/shard_map/output_partials/pallas_call | solution.py:258
  55.3 4.6 %collective-permute-start.16 = (bf16[256,1024]{1,0:T(8,128)(2,1)S(1)}, bf16[256,1024]{1,0:T(8,128)(2,1)S(1)}, u32[]{:S(2)}, u32[]{:S(2)}) collective-permute-start(bf16[256,1024]{1,0:T(8,128)(2,1)S(1)} %get-tuple-element.31), channel_id=1, source_target_pairs={{0,16},{8,24},{16,0},{24,8},{1,17},{9,25},{17,1},{25,9},{2,18},{10... | collective-permute-start | bytes 1572872 | tf_op jit(solution)/shard_map/ppermute | solution.py:23
  59.9 7.6 %collective-permute-done.27.refs_9_ = bf16[256,1024]{1,0:T(8,128)(2,1)S(1)} collective-permute-done((bf16[256,1024]{1,0:T(8,128)(2,1)S(1)}, bf16[256,1024]{1,0:T(8,128)(2,1)S(1)}, u32[]{:S(2)}, u32[]{:S(2)}) %collective-permute-start.27) | collective-permute-done | bytes 524320 | tf_op jit(solution)/shard_map/ppermute | solution.py:23
  67.5 3.4 %weight_partials.1 = (bf16[64,1024]{1,0:T(8,128)(2,1)S(1)}, bf16[64,1024]{1,0:T(8,128)(2,1)S(1)}, bf16[128,1024]{1,0:T(8,128)(2,1)S(1)}, bf16[128,1024]{1,0:T(8,...) custom-call(bf16[1024,128]{1,0:T(8,128)(2,1)S(1)} %bitcast.13, ...), custom_call_target="tpu_custom_call" | custom-call | tf_op jit(solution)/shard_map/weight_partials/pallas_call | solution.py:308
  71.5 2.3 %collective-permute-start.31 = (bf16[64,1024]{1,0:T(8,128)(2,1)S(1)}, bf16[64,1024]{1,0:T(8,128)(2,1)S(1)}, u32[]{:S(2)}, u32[]{:S(2)}) collective-permute-start(bf16[64,1024]{1,0:T(8,128)(2,1)S(1)} %get-tuple-element.41), channel_id=1, source_target_pairs={{0,224},{32,0},{64,32},{96,64},{128,96},{160,128},{192,160},{224,1... | collective-permute-start | bytes 393224 | tf_op jit(solution)/shard_map/ppermute | solution.py:23
  73.8 2.9 %collective-permute-done.30.ahead_ref = bf16[64,1024]{1,0:T(8,128)(2,1)S(1)} collective-permute-done((bf16[64,1024]{1,0:T(8,128)(2,1)S(1)}, bf16[64,1024]{1,0:T(8,128)(2,1)S(1)}, u32[]{:S(2)}, u32[]{:S(2)}) %collective-permute-start.30) | collective-permute-done | bytes 131104 | tf_op jit(solution)/shard_map/ppermute | solution.py:23
  78.1 3.4 %collective-permute-start.32 = (bf16[128,1024]{1,0:T(8,128)(2,1)S(1)}, bf16[128,1024]{1,0:T(8,128)(2,1)S(1)}, u32[]{:S(2)}, u32[]{:S(2)}) collective-permute-start(bf16[128,1024]{1,0:T(8,128)(2,1)S(1)} %get-tuple-element.44), channel_id=1, source_target_pairs={{0,32},{32,64},{64,96},{96,128},{128,160},{160,192},{192,224},{224... | collective-permute-start | bytes 786440 | tf_op jit(solution)/shard_map/ppermute | solution.py:23
  81.6 8.4 %collective-permute-done.16.refs_2_ = bf16[256,1024]{1,0:T(8,128)(2,1)S(1)} collective-permute-done((bf16[256,1024]{1,0:T(8,128)(2,1)S(1)}, bf16[256,1024]{1,0:T(8,128)(2,1)S(1)}, u32[]{:S(2)}, u32[]{:S(2)}) %collective-permute-start.16) | collective-permute-done | bytes 524320 | tf_op jit(solution)/shard_map/ppermute | solution.py:23
  90.0 3.3 %output_gradients.1 = (bf16[256,1024]{1,0:T(8,128)(2,1)}, bf16[256,1024]{1,0:T(8,128)(2,1)S(1)}, bf16[128,1024]{1,0:T(8,128)(2,1)S(1)}, f32[64,128]{1,0:T(8,128)S(1)}) custom-call(bf16[256,1024]{1,0:T(8,128)(2,1)S(1)} %get-tuple-element.29.refs_0_.refs_12_, bf16[256,1024]{1,0:T(8,128)(2,1)S(1)} %collective-permute-done.15.refs_1_, ...), custom_call_target="tpu_custom_call" | custom-call | tf_op jit(solution)/shard_map/output_gradients/pallas_call | solution.py:188
  93.5 1.7 %collective-permute-start.20 = (f32[64,128]{1,0:T(8,128)S(1)}, f32[64,128]{1,0:T(8,128)S(1)}, u32[]{:S(2)}, u32[]{:S(2)}) collective-permute-start(f32[64,128]{1,0:T(8,128)S(1)} %get-tuple-element.37), channel_id=1, source_target_pairs={{0,8},{8,16},{16,24},{24,0},{1,9},{9,17},{17,25},{25,1},{2,10},{10... | collective-permute-start | bytes 98312 | tf_op jit(solution)/shard_map/ppermute | solution.py:23
  95.4 1.6 %collective-permute-start.34 = (bf16[128,1024]{1,0:T(8,128)(2,1)S(1)}, bf16[128,1024]{1,0:T(8,128)(2,1)S(1)}, u32[]{:S(2)}, u32[]{:S(2)}) collective-permute-start(bf16[128,1024]{1,0:T(8,128)(2,1)S(1)} %get-tuple-element.48), channel_id=1, source_target_pairs={{0,32},{32,64},{64,96},{96,128},{128,160},{160,192},{192,224},{224... | collective-permute-start | bytes 786440 | tf_op jit(solution)/shard_map/ppermute | solution.py:23
  100.6 2.1 %collective-permute-start.23 = (f32[64,128]{1,0:T(8,128)S(1)}, f32[64,128]{1,0:T(8,128)S(1)}, u32[]{:S(2)}, u32[]{:S(2)}) collective-permute-start(f32[64,128]{1,0:T(8,128)S(1)} %add_add_fusion), channel_id=1, source_target_pairs={{0,224},{32,0},{64,32},{96,64},{128,96},{160,128},{192,160},{224,1... | collective-permute-start | bytes 98312 | tf_op jit(solution)/shard_map/ppermute | solution.py:23
  102.7 6.5 %collective-permute-start.19 = (bf16[128,1024]{1,0:T(8,128)(2,1)S(1)}, bf16[128,1024]{1,0:T(8,128)(2,1)S(1)}, u32[]{:S(2)}, u32[]{:S(2)}) collective-permute-start(bf16[128,1024]{1,0:T(8,128)(2,1)S(1)} %get-tuple-element.36), channel_id=1, source_target_pairs={{8,0},{16,8},{24,16},{32,24},{40,32},{48,40},{56,48},{64,56},{72,6... | collective-permute-start | bytes 786440 | tf_op jit(solution)/shard_map/ppermute | solution.py:33
  109.4 2.0 %collective-permute-start.37 = (bf16[128,1024]{1,0:T(8,128)(2,1)S(1)}, bf16[128,1024]{1,0:T(8,128)(2,1)S(1)}, u32[]{:S(2)}, u32[]{:S(2)}) collective-permute-start(bf16[128,1024]{1,0:T(8,128)(2,1)S(1)} %get-tuple-element.53), channel_id=1, source_target_pairs={{0,224},{32,0},{64,32},{96,64},{128,96},{160,128},{192,160},{224,1... | collective-permute-start | bytes 786440 | tf_op jit(solution)/shard_map/ppermute | solution.py:23
  111.4 4.9 %collective-permute-start.26 = (f32[64,128]{1,0:T(8,128)S(1)}, f32[64,128]{1,0:T(8,128)S(1)}, u32[]{:S(2)}, u32[]{:S(2)}) collective-permute-start(f32[64,128]{1,0:T(8,128)S(1)} %get-tuple-element.55), channel_id=1, source_target_pairs={{0,96},{32,128},{64,160},{96,192},{128,224},{160,0},{192,32},{224,... | collective-permute-start | bytes 98312 | tf_op jit(solution)/shard_map/ppermute | solution.py:23
  116.6 1.9 %collective-permute-done.26 = f32[64,128]{1,0:T(8,128)S(1)} collective-permute-done((f32[64,128]{1,0:T(8,128)S(1)}, f32[64,128]{1,0:T(8,128)S(1)}, u32[]{:S(2)}, u32[]{:S(2)}) %collective-permute-start.26) | collective-permute-done | bytes 32800 | tf_op jit(solution)/shard_map/ppermute | solution.py:23
  118.4 5.7 %collective-permute-done.25 = f32[64,128]{1,0:T(8,128)S(1)} collective-permute-done((f32[64,128]{1,0:T(8,128)S(1)}, f32[64,128]{1,0:T(8,128)S(1)}, u32[]{:S(2)}, u32[]{:S(2)}) %collective-permute-start.25) | collective-permute-done | bytes 32800 | tf_op jit(solution)/shard_map/ppermute | solution.py:23
  124.7 2.3 %conv_backward.1 = bf16[256,1024]{1,0:T(8,128)(2,1)} custom-call(bf16[256,1024]{1,0:T(8,128)(2,1)S(1)} %get-tuple-element.35.d_ref, bf16[128,1024]{1,0:T(8,128)(2,1)S(1)} %collective-permute-done.19.next_ref, bf16[64,128]{1,0:T(8,128)(2,1)S(1)} %copy-done.4), custom_call_target="tpu_custom_call" | custom-call | tf_op jit(solution)/shard_map/conv_backward/pallas_call | solution.py:138
  (72 shorter events, 16.3 us)
Async XLA Ops:
  0.7 17.5 %collective-permute-start.7 = (bf16[128,1024]{1,0:T(8,128)(2,1)}, bf16[128,1024]{1,0:T(8,128)(2,1)S(1)}, u32[]{:S(2)}, u32[]{:S(2)}) collective-permute-start(bf16[128,1024]{1,0:T(8,128)(2,1)} %refs_8_.1), channel_id=1, source_target_pairs={{0,32},{32,64},{64,96},{96,128},{128,160},{160,192},{192,224},{224... | collective-permute-start | bytes 786440 | tf_op jit(solution)/shard_map/ppermute | solution.py:23
  2.7 18.0 %collective-permute-start.10 = (bf16[128,1024]{1,0:T(8,128)(2,1)}, bf16[128,1024]{1,0:T(8,128)(2,1)S(1)}, u32[]{:S(2)}, u32[]{:S(2)}) collective-permute-start(bf16[128,1024]{1,0:T(8,128)(2,1)} %refs_8_.1), channel_id=1, source_target_pairs={{0,224},{32,0},{64,32},{96,64},{128,96},{160,128},{192,160},{224,1... | collective-permute-start | bytes 786440 | tf_op jit(solution)/shard_map/ppermute | solution.py:23
  3.5 11.9 %all-to-all-start = ((bf16[4,256,128]{2,1,0:T(8,128)(2,1)}), bf16[4,256,128]{2,1,0:T(8,128)(2,1)S(1)}, u32[]{:S(2)}, u32[]{:S(2)}) async-start(bf16[4,256,128]{2,1,0:T(8,128)(2,1)} %bitcast_bitcast_fusion), calls=%async_computation | async-start | bytes 524288 | tf_op jit(solution)/shard_map/all_to_all | solution.py:27
  8.1 14.1 %collective-permute-start.18 = (bf16[128,1024]{1,0:T(8,128)(2,1)S(1)}, bf16[128,1024]{1,0:T(8,128)(2,1)S(1)}, u32[]{:S(2)}, u32[]{:S(2)}) collective-permute-start(bf16[128,1024]{1,0:T(8,128)(2,1)S(1)} %slice.11), channel_id=1, source_target_pairs={{0,8},{8,16},{16,24},{24,32},{32,40},{40,48},{48,56},{56,64},{64,7... | collective-permute-start | bytes 786440 | tf_op jit(solution)/shard_map/ppermute | solution.py:33
  15.4 11.0 %collective-permute-start.3 = (bf16[1024,128]{1,0:T(8,128)(2,1)S(1)}, bf16[1024,128]{1,0:T(8,128)(2,1)S(1)}, u32[]{:S(2)}, u32[]{:S(2)}) collective-permute-start(bf16[1024,128]{1,0:T(8,128)(2,1)S(1)} %bitcast.8), channel_id=1, source_target_pairs={{0,1},{1,0},{2,3},{3,2},{4,5},{5,4},{6,7},{7,6},{8,9},{9,8},{10,11... | collective-permute-start | bytes 786440 | tf_op jit(solution)/shard_map/ppermute | solution.py:23
  15.4 11.8 %collective-permute-start.2 = (bf16[1024,128]{1,0:T(8,128)(2,1)S(1)}, bf16[1024,128]{1,0:T(8,128)(2,1)S(1)}, u32[]{:S(2)}, u32[]{:S(2)}) collective-permute-start(bf16[1024,128]{1,0:T(8,128)(2,1)S(1)} %bitcast.9), channel_id=1, source_target_pairs={{0,6},{2,0},{4,2},{6,4},{1,7},{3,1},{5,3},{7,5},{8,14},{10,8},{12,... | collective-permute-start | bytes 786440 | tf_op jit(solution)/shard_map/ppermute | solution.py:23
  18.2 10.6 %collective-permute-start.8 = (bf16[128,1024]{1,0:T(8,128)(2,1)S(1)}, bf16[128,1024]{1,0:T(8,128)(2,1)S(1)}, u32[]{:S(2)}, u32[]{:S(2)}) collective-permute-start(bf16[128,1024]{1,0:T(8,128)(2,1)S(1)} %collective-permute-done.7.refs_9_), channel_id=1, source_target_pairs={{0,32},{32,64},{64,96},{96,128},{128,160},{160,192},{192,224},{224... | collective-permute-start | bytes 786440 | tf_op jit(solution)/shard_map/ppermute | solution.py:23
  20.7 11.9 %collective-permute-start.11 = (bf16[128,1024]{1,0:T(8,128)(2,1)S(1)}, bf16[128,1024]{1,0:T(8,128)(2,1)S(1)}, u32[]{:S(2)}, u32[]{:S(2)}) collective-permute-start(bf16[128,1024]{1,0:T(8,128)(2,1)S(1)} %collective-permute-done.10.refs_12_), channel_id=1, source_target_pairs={{0,224},{32,0},{64,32},{96,64},{128,96},{160,128},{192,160},{224,1... | collective-permute-start | bytes 786440 | tf_op jit(solution)/shard_map/ppermute | solution.py:23
  22.2 14.0 %collective-permute-start.1 = (bf16[1024,128]{1,0:T(8,128)(2,1)S(1)}, bf16[1024,128]{1,0:T(8,128)(2,1)S(1)}, u32[]{:S(2)}, u32[]{:S(2)}) collective-permute-start(bf16[1024,128]{1,0:T(8,128)(2,1)S(1)} %bitcast.10), channel_id=1, source_target_pairs={{0,4},{2,6},{4,0},{6,2},{1,5},{3,7},{5,1},{7,3},{8,12},{10,14},{12... | collective-permute-start | bytes 786440 | tf_op jit(solution)/shard_map/ppermute | solution.py:23
  26.4 11.1 %collective-permute-start = (bf16[1024,128]{1,0:T(8,128)(2,1)S(1)}, bf16[1024,128]{1,0:T(8,128)(2,1)S(1)}, u32[]{:S(2)}, u32[]{:S(2)}) collective-permute-start(bf16[1024,128]{1,0:T(8,128)(2,1)S(1)} %bitcast.11), channel_id=1, source_target_pairs={{0,2},{2,4},{4,6},{6,0},{1,3},{3,5},{5,7},{7,1},{8,10},{10,12},{12... | collective-permute-start | bytes 786440 | tf_op jit(solution)/shard_map/ppermute | solution.py:23
  27.2 10.2 %collective-permute-start.6 = (bf16[1024,128]{1,0:T(8,128)(2,1)S(1)}, bf16[1024,128]{1,0:T(8,128)(2,1)S(1)}, u32[]{:S(2)}, u32[]{:S(2)}) collective-permute-start(bf16[1024,128]{1,0:T(8,128)(2,1)S(1)} %collective-permute-done.2.refs_3_), channel_id=1, source_target_pairs={{0,1},{1,0},{2,3},{3,2},{4,5},{5,4},{6,7},{7,6},{8,9},{9,8},{10,11... | collective-permute-start | bytes 786440 | tf_op jit(solution)/shard_map/ppermute | solution.py:23
  28.8 12.2 %collective-permute-start.9 = (bf16[128,1024]{1,0:T(8,128)(2,1)S(1)}, bf16[128,1024]{1,0:T(8,128)(2,1)S(1)}, u32[]{:S(2)}, u32[]{:S(2)}) collective-permute-start(bf16[128,1024]{1,0:T(8,128)(2,1)S(1)} %collective-permute-done.8.refs_10_), channel_id=1, source_target_pairs={{0,32},{32,64},{64,96},{96,128},{128,160},{160,192},{192,224},{224... | collective-permute-start | bytes 786440 | tf_op jit(solution)/shard_map/ppermute | solution.py:23
  32.6 9.6 %collective-permute-start.12 = (bf16[128,1024]{1,0:T(8,128)(2,1)S(1)}, bf16[128,1024]{1,0:T(8,128)(2,1)S(1)}, u32[]{:S(2)}, u32[]{:S(2)}) collective-permute-start(bf16[128,1024]{1,0:T(8,128)(2,1)S(1)} %collective-permute-done.11.refs_13_), channel_id=1, source_target_pairs={{0,224},{32,0},{64,32},{96,64},{128,96},{160,128},{192,160},{224,1... | collective-permute-start | bytes 786440 | tf_op jit(solution)/shard_map/ppermute | solution.py:23
  36.2 23.7 %collective-permute-start.29 = (bf16[256,1024]{1,0:T(8,128)(2,1)S(1)}, bf16[256,1024]{1,0:T(8,128)(2,1)S(1)}, u32[]{:S(2)}, u32[]{:S(2)}) collective-permute-start(bf16[256,1024]{1,0:T(8,128)(2,1)S(1)} %get-tuple-element.38.refs_8_), channel_id=1, source_target_pairs={{0,24},{8,0},{16,8},{24,16},{1,25},{9,1},{17,9},{25,17},{2,26},{10... | collective-permute-start | bytes 1572872 | tf_op jit(solution)/shard_map/ppermute | solution.py:23
  37.5 8.1 %collective-permute-start.4 = (bf16[1024,128]{1,0:T(8,128)(2,1)S(1)}, bf16[1024,128]{1,0:T(8,128)(2,1)S(1)}, u32[]{:S(2)}, u32[]{:S(2)}) collective-permute-start(bf16[1024,128]{1,0:T(8,128)(2,1)S(1)} %collective-permute-done.refs_1_), channel_id=1, source_target_pairs={{0,1},{1,0},{2,3},{3,2},{4,5},{5,4},{6,7},{7,6},{8,9},{9,8},{10,11... | collective-permute-start | bytes 786440 | tf_op jit(solution)/shard_map/ppermute | solution.py:23
  40.9 19.0 %collective-permute-start.28 = (bf16[256,1024]{1,0:T(8,128)(2,1)S(1)}, bf16[256,1024]{1,0:T(8,128)(2,1)S(1)}, u32[]{:S(2)}, u32[]{:S(2)}) collective-permute-start(bf16[256,1024]{1,0:T(8,128)(2,1)S(1)} %get-tuple-element.38.refs_8_), channel_id=1, source_target_pairs={{0,16},{8,24},{16,0},{24,8},{1,17},{9,25},{17,1},{25,9},{2,18},{10... | collective-permute-start | bytes 1572872 | tf_op jit(solution)/shard_map/ppermute | solution.py:23
  42.2 25.3 %collective-permute-start.27 = (bf16[256,1024]{1,0:T(8,128)(2,1)S(1)}, bf16[256,1024]{1,0:T(8,128)(2,1)S(1)}, u32[]{:S(2)}, u32[]{:S(2)}) collective-permute-start(bf16[256,1024]{1,0:T(8,128)(2,1)S(1)} %get-tuple-element.38.refs_8_), channel_id=1, source_target_pairs={{0,8},{8,16},{16,24},{24,0},{1,9},{9,17},{17,25},{25,1},{2,10},{10... | collective-permute-start | bytes 1572872 | tf_op jit(solution)/shard_map/ppermute | solution.py:23
  55.1 26.4 %collective-permute-start.15 = (bf16[256,1024]{1,0:T(8,128)(2,1)S(1)}, bf16[256,1024]{1,0:T(8,128)(2,1)S(1)}, u32[]{:S(2)}, u32[]{:S(2)}) collective-permute-start(bf16[256,1024]{1,0:T(8,128)(2,1)S(1)} %get-tuple-element.30), channel_id=1, source_target_pairs={{0,8},{8,16},{16,24},{24,0},{1,9},{9,17},{17,25},{25,1},{2,10},{10... | collective-permute-start | bytes 1572872 | tf_op jit(solution)/shard_map/ppermute | solution.py:23
  55.3 34.7 %collective-permute-start.16 = (bf16[256,1024]{1,0:T(8,128)(2,1)S(1)}, bf16[256,1024]{1,0:T(8,128)(2,1)S(1)}, u32[]{:S(2)}, u32[]{:S(2)}) collective-permute-start(bf16[256,1024]{1,0:T(8,128)(2,1)S(1)} %get-tuple-element.31), channel_id=1, source_target_pairs={{0,16},{8,24},{16,0},{24,8},{1,17},{9,25},{17,1},{25,9},{2,18},{10... | collective-permute-start | bytes 1572872 | tf_op jit(solution)/shard_map/ppermute | solution.py:23
  59.9 30.0 %collective-permute-start.17 = (bf16[256,1024]{1,0:T(8,128)(2,1)S(1)}, bf16[256,1024]{1,0:T(8,128)(2,1)S(1)}, u32[]{:S(2)}, u32[]{:S(2)}) collective-permute-start(bf16[256,1024]{1,0:T(8,128)(2,1)S(1)} %get-tuple-element.32), channel_id=1, source_target_pairs={{0,24},{8,0},{16,8},{24,16},{1,25},{9,1},{17,9},{25,17},{2,26},{10... | collective-permute-start | bytes 1572872 | tf_op jit(solution)/shard_map/ppermute | solution.py:23
  71.5 6.5 %collective-permute-start.31 = (bf16[64,1024]{1,0:T(8,128)(2,1)S(1)}, bf16[64,1024]{1,0:T(8,128)(2,1)S(1)}, u32[]{:S(2)}, u32[]{:S(2)}) collective-permute-start(bf16[64,1024]{1,0:T(8,128)(2,1)S(1)} %get-tuple-element.41), channel_id=1, source_target_pairs={{0,224},{32,0},{64,32},{96,64},{128,96},{160,128},{192,160},{224,1... | collective-permute-start | bytes 393224 | tf_op jit(solution)/shard_map/ppermute | solution.py:23
  78.1 17.1 %collective-permute-start.32 = (bf16[128,1024]{1,0:T(8,128)(2,1)S(1)}, bf16[128,1024]{1,0:T(8,128)(2,1)S(1)}, u32[]{:S(2)}, u32[]{:S(2)}) collective-permute-start(bf16[128,1024]{1,0:T(8,128)(2,1)S(1)} %get-tuple-element.44), channel_id=1, source_target_pairs={{0,32},{32,64},{64,96},{96,128},{128,160},{160,192},{192,224},{224... | collective-permute-start | bytes 786440 | tf_op jit(solution)/shard_map/ppermute | solution.py:23
  81.6 13.7 %collective-permute-start.33 = (bf16[128,1024]{1,0:T(8,128)(2,1)S(1)}, bf16[128,1024]{1,0:T(8,128)(2,1)S(1)}, u32[]{:S(2)}, u32[]{:S(2)}) collective-permute-start(bf16[128,1024]{1,0:T(8,128)(2,1)S(1)} %get-tuple-element.45), channel_id=1, source_target_pairs={{0,224},{32,0},{64,32},{96,64},{128,96},{160,128},{192,160},{224,1... | collective-permute-start | bytes 786440 | tf_op jit(solution)/shard_map/ppermute | solution.py:23
  95.4 13.8 %collective-permute-start.34 = (bf16[128,1024]{1,0:T(8,128)(2,1)S(1)}, bf16[128,1024]{1,0:T(8,128)(2,1)S(1)}, u32[]{:S(2)}, u32[]{:S(2)}) collective-permute-start(bf16[128,1024]{1,0:T(8,128)(2,1)S(1)} %get-tuple-element.48), channel_id=1, source_target_pairs={{0,32},{32,64},{64,96},{96,128},{128,160},{160,192},{192,224},{224... | collective-permute-start | bytes 786440 | tf_op jit(solution)/shard_map/ppermute | solution.py:23
  97.0 12.2 %collective-permute-start.35 = (bf16[128,1024]{1,0:T(8,128)(2,1)S(1)}, bf16[128,1024]{1,0:T(8,128)(2,1)S(1)}, u32[]{:S(2)}, u32[]{:S(2)}) collective-permute-start(bf16[128,1024]{1,0:T(8,128)(2,1)S(1)} %get-tuple-element.49), channel_id=1, source_target_pairs={{0,224},{32,0},{64,32},{96,64},{128,96},{160,128},{192,160},{224,1... | collective-permute-start | bytes 786440 | tf_op jit(solution)/shard_map/ppermute | solution.py:23
  99.8 11.6 %collective-permute-start.24 = (f32[64,128]{1,0:T(8,128)S(1)}, f32[64,128]{1,0:T(8,128)S(1)}, u32[]{:S(2)}, u32[]{:S(2)}) collective-permute-start(f32[64,128]{1,0:T(8,128)S(1)} %add_add_fusion), channel_id=1, source_target_pairs={{0,32},{32,64},{64,96},{96,128},{128,160},{160,192},{192,224},{224... | collective-permute-start | bytes 98312 | tf_op jit(solution)/shard_map/ppermute | solution.py:23
  100.6 10.9 %collective-permute-start.23 = (f32[64,128]{1,0:T(8,128)S(1)}, f32[64,128]{1,0:T(8,128)S(1)}, u32[]{:S(2)}, u32[]{:S(2)}) collective-permute-start(f32[64,128]{1,0:T(8,128)S(1)} %add_add_fusion), channel_id=1, source_target_pairs={{0,224},{32,0},{64,32},{96,64},{128,96},{160,128},{192,160},{224,1... | collective-permute-start | bytes 98312 | tf_op jit(solution)/shard_map/ppermute | solution.py:23
  102.7 22.1 %collective-permute-start.19 = (bf16[128,1024]{1,0:T(8,128)(2,1)S(1)}, bf16[128,1024]{1,0:T(8,128)(2,1)S(1)}, u32[]{:S(2)}, u32[]{:S(2)}) collective-permute-start(bf16[128,1024]{1,0:T(8,128)(2,1)S(1)} %get-tuple-element.36), channel_id=1, source_target_pairs={{8,0},{16,8},{24,16},{32,24},{40,32},{48,40},{56,48},{64,56},{72,6... | collective-permute-start | bytes 786440 | tf_op jit(solution)/shard_map/ppermute | solution.py:33
  109.3 17.7 %collective-permute-start.36 = (bf16[128,1024]{1,0:T(8,128)(2,1)S(1)}, bf16[128,1024]{1,0:T(8,128)(2,1)S(1)}, u32[]{:S(2)}, u32[]{:S(2)}) collective-permute-start(bf16[128,1024]{1,0:T(8,128)(2,1)S(1)} %get-tuple-element.52), channel_id=1, source_target_pairs={{0,32},{32,64},{64,96},{96,128},{128,160},{160,192},{192,224},{224... | collective-permute-start | bytes 786440 | tf_op jit(solution)/shard_map/ppermute | solution.py:23
  109.4 17.7 %collective-permute-start.37 = (bf16[128,1024]{1,0:T(8,128)(2,1)S(1)}, bf16[128,1024]{1,0:T(8,128)(2,1)S(1)}, u32[]{:S(2)}, u32[]{:S(2)}) collective-permute-start(bf16[128,1024]{1,0:T(8,128)(2,1)S(1)} %get-tuple-element.53), channel_id=1, source_target_pairs={{0,224},{32,0},{64,32},{96,64},{128,96},{160,128},{192,160},{224,1... | collective-permute-start | bytes 786440 | tf_op jit(solution)/shard_map/ppermute | solution.py:23
  111.4 7.0 %collective-permute-start.26 = (f32[64,128]{1,0:T(8,128)S(1)}, f32[64,128]{1,0:T(8,128)S(1)}, u32[]{:S(2)}, u32[]{:S(2)}) collective-permute-start(f32[64,128]{1,0:T(8,128)S(1)} %get-tuple-element.55), channel_id=1, source_target_pairs={{0,96},{32,128},{64,160},{96,192},{128,224},{160,0},{192,32},{224,... | collective-permute-start | bytes 98312 | tf_op jit(solution)/shard_map/ppermute | solution.py:23
  116.3 7.8 %collective-permute-start.25 = (f32[64,128]{1,0:T(8,128)S(1)}, f32[64,128]{1,0:T(8,128)S(1)}, u32[]{:S(2)}, u32[]{:S(2)}) collective-permute-start(f32[64,128]{1,0:T(8,128)S(1)} %get-tuple-element.54), channel_id=1, source_target_pairs={{0,160},{32,192},{64,224},{96,0},{128,32},{160,64},{192,96},{224,1... | collective-permute-start | bytes 98312 | tf_op jit(solution)/shard_map/ppermute | solution.py:23
  (12 other events, 121.0 us)
where the time goes:
time: 129 us; the launch traced here: 128 us
  starting transfers between devices  64.6 us (50%)
  waiting for transfers between devices  45.1 us (35%)
  Pallas kernels  15.1 us (12%)
  other arithmetic  1.47 us (1%)
    ppermute x36, starting transfers between devices, shift(): return lax.ppermute(block, axis, route)  49.6 us
    ppermute x36, waiting for transfers between devices, shift(): return lax.ppermute(block, axis, route)  41.8 us
    ppermute x2, starting transfers between devices, from_behind(): return lax.ppermute(block, SEQ, route)  10.4 us
    all_to_all x1, starting transfers between devices, exchanged(): return lax.all_to_all(blocks, axis, split_axis=0, concat_axis=0, tiled=True)  4.59 us
    pallas_call x1, Pallas kernels, output_partials(): pl.pallas_call(output_kernel, in_specs=[VMEM] * 17, out_specs=[VMEM] * 4,...  3.7 us
    pallas_call x1, Pallas kernels, weight_partials(): pl.pallas_call(weight_kernel, in_specs=[VMEM] * 12 + [ANY], out_specs=[VM...  3.39 us
    all_to_all x1, waiting for transfers between devices, exchanged(): return lax.all_to_all(blocks, axis, split_axis=0, concat_axis=0, tiled=True)  3.32 us
    pallas_call x1, Pallas kernels, output_gradients(): pl.pallas_call(gradient_kernel, grid=(channels // STEP,), in_specs=[tile(...  3.25 us
  transfers between devices with their start and end apart: 39, of which 16 were waited for; matrix products, arithmetic and copies ran while one was open for 1% of the time, Pallas kernels for 12%

commit v1 on v0

--- a/solution.py
+++ b/solution.py
@@ -13,7 +13,9 @@
 BF16 = jnp.bfloat16
 SIZES = {"z": 8, "y": 4, "x": 4, "c": 2}
 SEQ = ("z", "y")
-GRANT = pltpu.CompilerParams(vmem_limit_bytes=20 << 20)
+MiB = 1 << 20
+SMALL = pltpu.CompilerParams(vmem_limit_bytes=10 * MiB)
+LARGE = pltpu.CompilerParams(vmem_limit_bytes=16 * MiB)
 TP = ("x", "c")
 
 
@@ -54,12 +56,9 @@
 STEP = 512
 
 
-def tiles():
-    return [slice(at, at + LANES) for at in range(0, STEP, LANES)]
-
-
-def group_rows(at):
-    return slice(at // GROUP, (at + LANES) // GROUP)
+def for_tiles(body):
+    for at in range(0, STEP, LANES):
+        body(slice(at, at + LANES), slice(at // GROUP, (at + LANES) // GROUP))
 
 
 def banded(rings, first):
@@ -83,8 +82,9 @@
     row, col = rows_and_cols()
     flip = jnp.where(row + col == TAPS - 1, 1.0, 0.0).astype(BF16)
     taps = jnp.dot(taps_ref[...], flip, preferred_element_type=F32)
-    for at in tiles():
-        band = banded(rings_of(taps[group_rows(at.start)], 1), col > row)
+
+    def body(at, groups):
+        band = banded(rings_of(taps[groups], 1), col > row)
         x0, x1 = x_ref[:TAPS, at], x_ref[TAPS:, at]
         first = jnp.concatenate([prev_ref[:, at], x0], axis=0)
         second = jnp.concatenate([x0, x1], axis=0)
@@ -93,6 +93,8 @@
         conv = jnp.concatenate([conv[:, :LANES], conv[:, LANES:]], axis=0)
         out_ref[:, at] = conv
         mixed_ref[:, at] = (gate_ref[:, at].astype(F32) * conv).astype(BF16)
+
+    for_tiles(body)
 
 
 def tile(rows):
@@ -115,15 +117,16 @@
             jax.ShapeDtypeStruct(x.shape, F32),
         ],
         name="conv_forward",
-        compiler_params=GRANT,
+        compiler_params=SMALL,
     )(prev, x, gate, filters)
 
 
 def back_kernel(d_ref, next_ref, taps_ref, out_ref):
     row, col = rows_and_cols()
-    taps = taps_ref[...].astype(F32)
-    for at in tiles():
-        band = banded(rings_of(taps[group_rows(at.start)], 0), col >= row)
+
+    def body(at, groups):
+        taps = taps_ref[groups].astype(F32)
+        band = banded(rings_of(taps, 0), col >= row)
         d0, d1 = d_ref[:TAPS, at], d_ref[TAPS:, at]
         first = jnp.concatenate([d0, d1], axis=0)
         second = jnp.concatenate([d1, next_ref[:, at]], axis=0)
@@ -132,6 +135,8 @@
         out_ref[:TAPS, at] = conv[:, :LANES].astype(BF16)
         out_ref[TAPS:, at] = conv[:, LANES:].astype(BF16)
 
+    for_tiles(body)
+
 
 def conv_backward(d_conv, following, filters):
     rows, channels = d_conv.shape
@@ -142,13 +147,13 @@
         out_specs=tile(rows),
         out_shape=jax.ShapeDtypeStruct(d_conv.shape, BF16),
         name="conv_backward",
-        compiler_params=GRANT,
+        compiler_params=SMALL,
     )(d_conv, following, filters)
 
 
 def gradient_kernel(*refs):
-    terms, (conv_ref, gate_ref, prev_ref, x_ref) = refs[:4], refs[4:8]
-    grad_gate_ref, d_ref, head_ref, out_ref = refs[8:]
+    own_ref, terms, (conv_ref, gate_ref, prev_ref, x_ref) = refs[0], refs[1:5], refs[5:9]
+    grad_gate_ref, d_ref, head_ref, out_ref = refs[9:]
     row, col = rows_and_cols()
     flip = jnp.where(row + col == TAPS - 1, 1.0, 0.0).astype(BF16)
     keep = col + row >= TAPS - 1
@@ -156,15 +161,20 @@
     def flipped(block):
         return jnp.dot(flip, block, preferred_element_type=F32).astype(BF16)
 
-    prev, x0, x1 = flipped(prev_ref[...]), flipped(x_ref[:TAPS]), flipped(x_ref[TAPS:])
-    for at in tiles():
-        d_out = sum(term[:, at].astype(F32) for term in terms)
+    blocks = flipped(prev_ref[...]), flipped(x_ref[:TAPS]), flipped(x_ref[TAPS:])
+
+    def body(at, groups):
+        prev, x0, x1 = (block[:, at] for block in blocks)
+        above, below = (
+            terms[k][:, at].astype(F32) + terms[k + 1][:, at].astype(F32) for k in (0, 2)
+        )
+        d_out = own_ref[:, at].astype(F32) + jnp.concatenate([above, below], axis=0)
         grad_gate_ref[:, at] = (d_out * conv_ref[:, at]).astype(BF16)
         d_conv = (d_out * gate_ref[:, at].astype(F32)).astype(BF16)
         d_ref[:, at] = d_conv
         head_ref[:, at] = d_conv[:TAPS]
-        first = jnp.concatenate([prev[:, at], x0[:, at]], axis=0)
-        second = jnp.concatenate([x0[:, at], x1[:, at]], axis=0)
+        first = jnp.concatenate([prev, x0], axis=0)
+        second = jnp.concatenate([x0, x1], axis=0)
         window = jnp.concatenate([first, second], axis=1)
         both = jnp.concatenate([d_conv[:TAPS], d_conv[TAPS:]], axis=1)
         lanes = lane_group(both.shape)
@@ -180,15 +190,18 @@
             ring = jnp.where(keep, part[:, TAPS:], part[:, :TAPS])
             ring = pltpu.roll(ring, 1, 1, stride=1, stride_axis=0)
             sums.append(jnp.sum(ring, axis=0, keepdims=True))
-        out_ref[group_rows(at.start)] = jnp.concatenate(sums, axis=0)
-
-
-def output_gradients(terms, conv_out, gate, prev, x):
+        out_ref[groups] = jnp.concatenate(sums, axis=0)
+
+    for_tiles(body)
+
+
+def output_gradients(own, terms, conv_out, gate, prev, x):
     rows, channels = x.shape
     return pl.pallas_call(
         gradient_kernel,
         grid=(channels // STEP,),
-        in_specs=[tile(rows)] * 6 + [tile(TAPS), tile(rows)],
+        in_specs=[tile(rows)] + [tile(TAPS)] * 4
+        + [tile(rows)] * 2 + [tile(TAPS), tile(rows)],
         out_specs=[tile(rows), tile(rows), tile(TAPS), taps_tile()],
         out_shape=[
             jax.ShapeDtypeStruct(x.shape, BF16),
@@ -197,27 +210,27 @@
             jax.ShapeDtypeStruct((channels // GROUP, TAPS), F32),
         ],
         name="output_gradients",
-        compiler_params=GRANT,
-    )(*terms, conv_out, gate, prev, x)
+        compiler_params=SMALL,
+    )(own, *terms, conv_out, gate, prev, x)
 
 
 ANY = pl.BlockSpec(memory_space=pl.ANY)
 VMEM = pl.BlockSpec(memory_space=pltpu.VMEM)
 
 
-def on_chip(block):
-    return pltpu.with_memory_space_constraint(block, pltpu.VMEM)
-
-
-def place_features(pieces, scratch):
+def on_chip(blocks):
+    return [pltpu.with_memory_space_constraint(b, pltpu.VMEM) for b in blocks]
+
+
+def owners():
     x, c = lax.axis_index("x"), lax.axis_index("c")
-    out = []
-    for at, piece in enumerate(pieces):
-        owner_c = c if at < 4 else 1 - c
-        owner = 2 * lax.rem(x - at % 4 + 4, 4) + owner_c
-        start = pl.multiple_of(owner * LANES, LANES)
-        out.append((piece, scratch.at[:, pl.ds(start, LANES)]))
-    return out
+    for at in range(8):
+        yield 2 * lax.rem(x - at % 4 + 4, 4) + (c if at < 4 else 1 - c)
+
+
+def for_columns(body, channels):
+    for at in range(0, channels, 2 * LANES):
+        body(pl.ds(at, 2 * LANES))
 
 
 def run_copies(pairs, sems):
@@ -232,42 +245,54 @@
 
 
 def output_kernel(*refs):
-    u_refs, w_refs, outs = refs[:8], refs[8:17], refs[17:21]
-    u_all, w_all, sems = refs[21:]
+    u_refs, w_refs, own_ref, outs = refs[:8], refs[8:17], refs[17], refs[18:24]
+    u_all, w_all, total, sems = refs[24:]
     z, y = lax.axis_index("z"), lax.axis_index("y")
-    pairs = place_features(u_refs, u_all)
+    rows = own_ref.shape[0]
+    half = rows // 2
+    pairs = []
+    for u_ref, owner in zip(u_refs, owners()):
+        lanes = pl.ds(pl.multiple_of(owner * LANES, LANES), LANES)
+        pairs.append((u_ref, u_all.at[:, lanes]))
     for at, k in enumerate((0, 1, 2, 3, -1, -2, -3)):
         start = pl.multiple_of(lax.rem(z - k + 8, 8) * LANES, LANES)
         pairs.append((w_refs[at], w_all.at[pl.ds(start, LANES)]))
     far = pl.multiple_of(lax.rem(z + 4, 8) * LANES, LANES)
-    half = LANES // 2
-    pairs.append((w_refs[7], w_all.at[pl.ds(far, half)]))
-    pairs.append((w_refs[8], w_all.at[pl.ds(pl.multiple_of(far + half, half), half)]))
+    later = pl.multiple_of(far + LANES // 2, LANES // 2)
+    pairs.append((w_refs[7], w_all.at[pl.ds(far, LANES // 2)]))
+    pairs.append((w_refs[8], w_all.at[pl.ds(later, LANES // 2)]))
     run_copies(pairs, sems)
-    rows = outs[0].shape[0]
-    for d, out in enumerate(outs):
-        start = pl.multiple_of(lax.rem(y + d, 4) * rows, rows)
-        out[...] = jnp.dot(
-            u_all[pl.ds(start, rows)], w_all[...], preferred_element_type=F32
-        ).astype(BF16)
+    places = ((2, 0), (2, half), (1, half), (3, 0), (1, 0), (3, half))
+
+    def body(lanes):
+        sums = jnp.dot(u_all[...], w_all[:, lanes], preferred_element_type=F32)
+        total[:, lanes] = sums.astype(BF16)
+
+    for_columns(body, own_ref.shape[1])
+    own_ref[...] = total[pl.ds(pl.multiple_of(y * rows, rows), rows)]
+    for out, (d, at) in zip(outs, places):
+        start = pl.multiple_of(lax.rem(y + d, 4) * rows + at, half)
+        out[...] = total[pl.ds(start, half)]
 
 
 def output_partials(features, weights):
     tokens, channels = features[0].shape[0], weights[0].shape[1]
     shape = jax.ShapeDtypeStruct((tokens // 4, channels), BF16)
+    short = jax.ShapeDtypeStruct((tokens // 8, channels), BF16)
     return pl.pallas_call(
         output_kernel,
-        in_specs=[VMEM] * 17,
-        out_specs=[VMEM] * 4,
-        out_shape=[shape] * 4,
+        in_specs=[ANY] + [VMEM] * 7 + [ANY] + [VMEM] * 8,
+        out_specs=[VMEM] * 7,
+        out_shape=[shape] + [short] * 6,
         scratch_shapes=[
             pltpu.VMEM((tokens, 8 * LANES), BF16),
             pltpu.VMEM((8 * LANES, channels), BF16),
+            pltpu.VMEM((tokens, channels), BF16),
             pltpu.SemaphoreType.DMA((17,)),
         ],
         name="output_partials",
-        compiler_params=GRANT,
-    )(*map(on_chip, (*features, *weights)))
+        compiler_params=LARGE,
+    )(features[0], *on_chip(features[1:]), weights[0], *on_chip(weights[1:]))
 
 
 HOPS = (3, -3, 2, -2, 1, -1, 0)
@@ -275,30 +300,31 @@
 
 def weight_kernel(*refs):
     u_refs, m_refs, far_refs, outs = refs[:8], refs[8:12], refs[13:15], refs[15:22]
-    u_all, m_all, sems = refs[22:]
+    u_all, m_all, flipped, sems = refs[22:]
     z, y = lax.axis_index("z"), lax.axis_index("y")
-    pairs = place_features(u_refs, u_all)
+    pairs = []
+    for u_ref, owner in zip(u_refs, owners()):
+        start = pl.multiple_of(lax.rem(owner - z + 8, 8) * LANES, LANES)
+        pairs.append((u_ref, u_all.at[:, pl.ds(start, LANES)]))
     rows = m_refs[0].shape[0]
     for d, m_ref in enumerate(m_refs):
         start = pl.multiple_of(lax.rem(y - d + 4, 4) * rows, rows)
         pairs.append((m_ref, m_all.at[pl.ds(start, rows)]))
     run_copies(pairs, sems)
-
-    def block(hop):
-        start = pl.multiple_of(lax.rem(z + hop + 8, 8) * LANES, LANES)
-        return lax.dot_general(
-            u_all[:, pl.ds(start, LANES)],
-            m_all[...],
-            (((0,), (0,)), ((), ())),
-            preferred_element_type=F32,
-        ).astype(BF16)
-
-    far = block(4)
+    flipped[...] = u_all[...].T
     half = LANES // 2
-    far_refs[0][...] = far[:half]
-    far_refs[1][...] = far[half:]
-    for out, hop in zip(outs, HOPS):
-        out[...] = block(hop)
+
+    def body(lanes):
+        sums = jnp.dot(flipped[...], m_all[:, lanes], preferred_element_type=F32)
+        sums = sums.astype(BF16)
+        far = 4 * LANES
+        far_refs[0][:, lanes] = sums[far : far + half]
+        far_refs[1][:, lanes] = sums[far + half : far + LANES]
+        for out, hop in zip(outs, HOPS):
+            start = hop % 8 * LANES
+            out[:, lanes] = sums[start : start + LANES]
+
+    for_columns(body, m_all.shape[1])
 
 
 def weight_partials(features, mixed, after):
@@ -307,17 +333,18 @@
     short = jax.ShapeDtypeStruct((LANES // 2, channels), BF16)
     return pl.pallas_call(
         weight_kernel,
-        in_specs=[VMEM] * 12 + [ANY],
+        in_specs=[ANY] + [VMEM] * 7 + [ANY] + [VMEM] * 3 + [ANY],
         out_specs=[VMEM] * 9,
         out_shape=[short] * 2 + [shape] * 7,
         scratch_shapes=[
             pltpu.VMEM((tokens, 8 * LANES), BF16),
             pltpu.VMEM((tokens, channels), BF16),
+            pltpu.VMEM((8 * LANES, tokens), BF16),
             pltpu.SemaphoreType.DMA((12,)),
         ],
         name="weight_partials",
-        compiler_params=GRANT,
-    )(*map(on_chip, (*features, *mixed)), after)
+        compiler_params=LARGE,
+    )(features[0], *on_chip(features[1:]), mixed[0], *on_chip(mixed[1:]), after)
 
 
 def add_kernel(ahead_ref, behind_ref, first_ref, last_ref, ahead_out, behind_out):
@@ -340,8 +367,8 @@
         in_specs=[VMEM] * 4,
         out_specs=[VMEM] * 2,
         out_shape=[shape] * 2,
-        compiler_params=GRANT,
-    )(*map(on_chip, (ahead, behind, first, last)))
+        compiler_params=SMALL,
+    )(*on_chip((ahead, behind, first, last)))
 
 
 def block_backward(gate, conv_input, filters, out_weight, upstream):
@@ -369,10 +396,16 @@
     mixed, conv_out = conv_forward(prior, conv_input, gate, filters)
     mixed = [mixed] + [shift(mixed, "y", d) for d in (1, 2, 3)]
 
-    partials = output_partials(features, weights)
-    terms = [partials[0]] + [shift(partials[d], "y", d) for d in (1, 2, 3)]
-
-    ahead, behind, *blocks = weight_partials(features, mixed, partials[0])
+    own_sum, far_top, far_low, up_low, down_top, up_top, down_low = output_partials(
+        features, weights
+    )
+    top, low = shift(far_top, "y", 1), shift(far_low, "y", -1)
+    from_below, from_above = shift(up_low, "y", 1), shift(down_top, "y", -1)
+    top, low = add_pair(top, low, up_top, down_low)
+    top, low = shift(top, "y", 1), shift(low, "y", -1)
+    terms = top, from_above, from_below, low
+
+    ahead, behind, *blocks = weight_partials(features, mixed, own_sum)
     for step in (1, 2, 3):
         ahead = shift(ahead, "z", 1)
         behind = shift(behind, "z", -1)
@@ -383,10 +416,12 @@
     grad_weight = (summed * factor).astype(BF16)
 
     grad_gate, d_conv, head, local = output_gradients(
-        terms, conv_out, gate, prior, conv_input
+        own_sum, terms, conv_out, gate, prior, conv_input
     )
     following = from_behind(head, -1)
-    local = local + sum(shift(local, "y", d) for d in (1, 2, 3))
+    for step in (1, 2):
+        other = shift(local, "y", step)
+        local = local + other
     below, above = shift(local, "z", 1), shift(local, "z", -1)
     pair = local + above
     local = pair + below

time: 129 us -> 132 us (1.023)
  waiting for transfers between devices: 45.1 us -> 52.3 us
  starting transfers between devices: 64.6 us -> 59.2 us
    ppermute x36 -> x38, waiting for transfers between devices: 41.8 us -> 47.1 us  [shift(): return lax.ppermute(block, axis, route)]
    ppermute x2, waiting for transfers between devices: 0.04 us -> 4.54 us  [from_behind(): return lax.ppermute(block, SEQ, route)]
    ppermute x36 -> x38, starting transfers between devices: 49.6 us -> 46.5 us  [shift(): return lax.ppermute(block, axis, route)]
    all_to_all x1, waiting for transfers between devices: 3.32 us -> 0.68 us  [exchanged(): return lax.all_to_all(blocks, axis, split_axis=0, concat_axis=0, tiled=True)]
    ppermute x2, starting transfers between devices: 10.4 us -> 8.12 us  [from_behind(): return lax.ppermute(block, SEQ, route)]
  transfers between devices with their start and end apart: 39 -> 41, of which waited for: 16 -> 19; matrix products, arithmetic and copies ran while one was open for 1% -> 1% of each run, Pallas kernels for 12% -> 9%
where the time goes in v1:
time: 132 us; the launch traced here: 131 us
  starting transfers between devices  59.2 us (45%)
  waiting for transfers between devices  52.3 us (40%)
  Pallas kernels  15.3 us (12%)
  local copies, waits for them, and re-layouts  1.74 us (1%)
  other arithmetic  1.48 us (1%)
    ppermute x38, waiting for transfers between devices, shift(): return lax.ppermute(block, axis, route)  47.1 us
    ppermute x38, starting transfers between devices, shift(): return lax.ppermute(block, axis, route)  46.5 us
    ppermute x2, starting transfers between devices, from_behind(): return lax.ppermute(block, SEQ, route)  8.12 us
    all_to_all x1, starting transfers between devices, exchanged(): return lax.all_to_all(blocks, axis, split_axis=0, concat_axis=0, tiled=True)  4.59 us
    ppermute x2, waiting for transfers between devices, from_behind(): return lax.ppermute(block, SEQ, route)  4.54 us
    pallas_call x1, Pallas kernels, output_partials(): pl.pallas_call(output_kernel, in_specs=[ANY] + [VMEM] * 7 + [ANY] + [VMEM...  3.96 us
    pallas_call x1, Pallas kernels, weight_partials(): pl.pallas_call(weight_kernel, in_specs=[ANY] + [VMEM] * 7 + [ANY] + [VMEM...  3.28 us
    pallas_call x1, Pallas kernels, output_gradients(): pl.pallas_call(gradient_kernel, grid=(channels // STEP,), in_specs=[tile(...  3.18 us
  transfers between devices with their start and end apart: 41, of which 19 were waited for; matrix products, arithmetic and copies ran while one was open for 1% of the time, Pallas kernels for 9%

profile of v1, /device:TPU:32, one launch (start us, length us, event | category | flops | bytes accessed | tf_op | source)
XLA Modules:
  0.0 130.9 jit_solution(18129492951762388432)
XLA Ops:
  2.3 4.6 %all-to-all-start = ((bf16[4,256,128]{2,1,0:T(8,128)(2,1)}), bf16[4,256,128]{2,1,0:T(8,128)(2,1)S(1)}, u32[]{:S(2)}, u32[]{:S(2)}) async-start(bf16[4,256,128]{2,1,0:T(8,128)(2,1)} %bitcast_bitcast_fusion), calls=%async_computation | async-start | bytes 524288 | tf_op jit(solution)/shard_map/all_to_all | solution.py:29
  6.9 1.9 %collective-permute-start.7 = (bf16[128,1024]{1,0:T(8,128)(2,1)S(1)}, bf16[128,1024]{1,0:T(8,128)(2,1)S(1)}, u32[]{:S(2)}, u32[]{:S(2)}) collective-permute-start(bf16[128,1024]{1,0:T(8,128)(2,1)S(1)} %copy-done.3), channel_id=1, source_target_pairs={{0,32},{32,64},{64,96},{96,128},{128,160},{160,192},{192,224},{224... | collective-permute-start | bytes 786440 | tf_op jit(solution)/shard_map/ppermute | solution.py:25
  9.0 3.9 %collective-permute-start.21 = (bf16[128,1024]{1,0:T(8,128)(2,1)S(1)}, bf16[128,1024]{1,0:T(8,128)(2,1)S(1)}, u32[]{:S(2)}, u32[]{:S(2)}) collective-permute-start(bf16[128,1024]{1,0:T(8,128)(2,1)S(1)} %slice.11), channel_id=1, source_target_pairs={{0,8},{8,16},{16,24},{24,32},{32,40},{40,48},{48,56},{56,64},{64,7... | collective-permute-start | bytes 786440 | tf_op jit(solution)/shard_map/ppermute | solution.py:35
  13.6 2.8 %collective-permute-start.2 = (bf16[1024,128]{1,0:T(8,128)(2,1)S(1)}, bf16[1024,128]{1,0:T(8,128)(2,1)S(1)}, u32[]{:S(2)}, u32[]{:S(2)}) collective-permute-start(bf16[1024,128]{1,0:T(8,128)(2,1)S(1)} %bitcast.9), channel_id=1, source_target_pairs={{0,6},{2,0},{4,2},{6,4},{1,7},{3,1},{5,3},{7,5},{8,14},{10,8},{12,... | collective-permute-start | bytes 786440 | tf_op jit(solution)/shard_map/ppermute | solution.py:25
  16.4 1.9 %collective-permute-start.8 = (bf16[128,1024]{1,0:T(8,128)(2,1)S(1)}, bf16[128,1024]{1,0:T(8,128)(2,1)S(1)}, u32[]{:S(2)}, u32[]{:S(2)}) collective-permute-start(bf16[128,1024]{1,0:T(8,128)(2,1)S(1)} %collective-permute-done.7.refs_9_), channel_id=1, source_target_pairs={{0,32},{32,64},{64,96},{96,128},{128,160},{160,192},{192,224},{224... | collective-permute-start | bytes 786440 | tf_op jit(solution)/shard_map/ppermute | solution.py:25
  20.0 4.5 %collective-permute-done.21.prev_ref.refs_7_ = bf16[128,1024]{1,0:T(8,128)(2,1)S(1)} collective-permute-done((bf16[128,1024]{1,0:T(8,128)(2,1)S(1)}, bf16[128,1024]{1,0:T(8,128)(2,1)S(1)}, u32[]{:S(2)}, u32[]{:S(2)}) %collective-permute-start.21) | collective-permute-done | bytes 262176 | tf_op jit(solution)/shard_map/ppermute | solution.py:35
  24.5 3.2 %collective-permute-start.1 = (bf16[1024,128]{1,0:T(8,128)(2,1)S(1)}, bf16[1024,128]{1,0:T(8,128)(2,1)S(1)}, u32[]{:S(2)}, u32[]{:S(2)}) collective-permute-start(bf16[1024,128]{1,0:T(8,128)(2,1)S(1)} %bitcast.10), channel_id=1, source_target_pairs={{0,4},{2,6},{4,0},{6,2},{1,5},{3,7},{5,1},{7,3},{8,12},{10,14},{12... | collective-permute-start | bytes 786440 | tf_op jit(solution)/shard_map/ppermute | solution.py:25
  30.0 1.8 %collective-permute-start.12 = (bf16[128,1024]{1,0:T(8,128)(2,1)S(1)}, bf16[128,1024]{1,0:T(8,128)(2,1)S(1)}, u32[]{:S(2)}, u32[]{:S(2)}) collective-permute-start(bf16[128,1024]{1,0:T(8,128)(2,1)S(1)} %collective-permute-done.11.refs_13_), channel_id=1, source_target_pairs={{0,224},{32,0},{64,32},{96,64},{128,96},{160,128},{192,160},{224,1... | collective-permute-start | bytes 786440 | tf_op jit(solution)/shard_map/ppermute | solution.py:25
  31.8 2.1 %conv_forward.1 = (bf16[256,1024]{1,0:T(8,128)(2,1)S(1)}, f32[256,1024]{1,0:T(8,128)S(1)}) custom-call(bf16[128,1024]{1,0:T(8,128)(2,1)S(1)} %collective-permute-done.21.prev_ref.refs_7_, bf16[256,1024]{1,0:T(8,128)(2,1)S(1)} %copy-done.1, bf16[256,1024]{1,0:T(8,128)(2,1)S(1)} %copy-done.2, bf16[64,128]{1,0:T(8,128)(2,1)S(1)} %copy-done.4), custom_call_target="tpu_custom_call" | custom-call | tf_op jit(solution)/shard_map/conv_forward/pallas_call | solution.py:110
  40.2 2.4 %collective-permute-start.13 = (bf16[64,1024]{1,0:T(8,128)(2,1)S(1)}, bf16[64,1024]{1,0:T(8,128)(2,1)S(1)}, u32[]{:S(2)}, u32[]{:S(2)}) collective-permute-start(bf16[64,1024]{1,0:T(8,128)(2,1)S(1)} %slice.12), channel_id=1, source_target_pairs={{0,32},{32,64},{64,96},{96,128},{128,160},{160,192},{192,224},{224... | collective-permute-start | bytes 393224 | tf_op jit(solution)/shard_map/ppermute | solution.py:25
  43.6 3.4 %collective-permute-done.13.refs_15_ = bf16[64,1024]{1,0:T(8,128)(2,1)S(1)} collective-permute-done((bf16[64,1024]{1,0:T(8,128)(2,1)S(1)}, bf16[64,1024]{1,0:T(8,128)(2,1)S(1)}, u32[]{:S(2)}, u32[]{:S(2)}) %collective-permute-start.13) | collective-permute-done | bytes 131104 | tf_op jit(solution)/shard_map/ppermute | solution.py:25
  47.0 2.5 %collective-permute-done.14.refs_16_ = bf16[64,1024]{1,0:T(8,128)(2,1)S(1)} collective-permute-done((bf16[64,1024]{1,0:T(8,128)(2,1)S(1)}, bf16[64,1024]{1,0:T(8,128)(2,1)S(1)}, u32[]{:S(2)}, u32[]{:S(2)}) %collective-permute-start.14) | collective-permute-done | bytes 131104 | tf_op jit(solution)/shard_map/ppermute | solution.py:25
  49.5 4.0 %output_partials.1 = (bf16[256,1024]{1,0:T(8,128)(2,1)S(1)}, bf16[128,1024]{1,0:T(8,128)(2,1)S(1)}, bf16[128,1024]{1,0:T(8,128)(2,1)S(1)}, bf16[128,1024]{1,0:T(...) custom-call(bf16[1024,128]{1,0:T(8,128)(2,1)S(1)} %bitcast.12, ...), custom_call_target="tpu_custom_call" | custom-call | tf_op jit(solution)/shard_map/output_partials/pallas_call | solution.py:282
  53.5 8.5 %collective-permute-done.29.refs_9_ = bf16[256,1024]{1,0:T(8,128)(2,1)S(1)} collective-permute-done((bf16[256,1024]{1,0:T(8,128)(2,1)S(1)}, bf16[256,1024]{1,0:T(8,128)(2,1)S(1)}, u32[]{:S(2)}, u32[]{:S(2)}) %collective-permute-start.29) | collective-permute-done | bytes 524320 | tf_op jit(solution)/shard_map/ppermute | solution.py:25
  62.0 3.3 %weight_partials.1 = (bf16[64,1024]{1,0:T(8,128)(2,1)S(1)}, bf16[64,1024]{1,0:T(8,128)(2,1)S(1)}, bf16[128,1024]{1,0:T(8,128)(2,1)S(1)}, bf16[128,1024]{1,0:T(8,...) custom-call(bf16[1024,128]{1,0:T(8,128)(2,1)S(1)} %bitcast.13, ...), custom_call_target="tpu_custom_call" | custom-call | tf_op jit(solution)/shard_map/weight_partials/pallas_call | solution.py:334
  65.3 3.1 %collective-permute-start.32 = (bf16[64,1024]{1,0:T(8,128)(2,1)S(1)}, bf16[64,1024]{1,0:T(8,128)(2,1)S(1)}, u32[]{:S(2)}, u32[]{:S(2)}) collective-permute-start(bf16[64,1024]{1,0:T(8,128)(2,1)S(1)} %get-tuple-element.50), channel_id=1, source_target_pairs={{0,32},{32,64},{64,96},{96,128},{128,160},{160,192},{192,224},{224... | collective-permute-start | bytes 393224 | tf_op jit(solution)/shard_map/ppermute | solution.py:25
  69.3 2.3 %collective-permute-start.16 = (bf16[128,1024]{1,0:T(8,128)(2,1)S(1)}, bf16[128,1024]{1,0:T(8,128)(2,1)S(1)}, u32[]{:S(2)}, u32[]{:S(2)}) collective-permute-start(bf16[128,1024]{1,0:T(8,128)(2,1)S(1)} %get-tuple-element.36), channel_id=1, source_target_pairs={{0,24},{8,0},{16,8},{24,16},{1,25},{9,1},{17,9},{25,17},{2,26},{10... | collective-permute-start | bytes 786440 | tf_op jit(solution)/shard_map/ppermute | solution.py:25
  71.7 2.0 %collective-permute-done.33.behind_ref = bf16[64,1024]{1,0:T(8,128)(2,1)S(1)} collective-permute-done((bf16[64,1024]{1,0:T(8,128)(2,1)S(1)}, bf16[64,1024]{1,0:T(8,128)(2,1)S(1)}, u32[]{:S(2)}, u32[]{:S(2)}) %collective-permute-start.33) | collective-permute-done | bytes 131104 | tf_op jit(solution)/shard_map/ppermute | solution.py:25
  73.8 2.8 %collective-permute-start.34 = (bf16[128,1024]{1,0:T(8,128)(2,1)S(1)}, bf16[128,1024]{1,0:T(8,128)(2,1)S(1)}, u32[]{:S(2)}, u32[]{:S(2)}) collective-permute-start(bf16[128,1024]{1,0:T(8,128)(2,1)S(1)} %get-tuple-element.54), channel_id=1, source_target_pairs={{0,32},{32,64},{64,96},{96,128},{128,160},{160,192},{192,224},{224... | collective-permute-start | bytes 786440 | tf_op jit(solution)/shard_map/ppermute | solution.py:25
  78.9 2.6 %collective-permute-done.34.ahead_ref = bf16[128,1024]{1,0:T(8,128)(2,1)S(1)} collective-permute-done((bf16[128,1024]{1,0:T(8,128)(2,1)S(1)}, bf16[128,1024]{1,0:T(8,128)(2,1)S(1)}, u32[]{:S(2)}, u32[]{:S(2)}) %collective-permute-start.34) | collective-permute-done | bytes 262176 | tf_op jit(solution)/shard_map/ppermute | solution.py:25
  82.1 2.5 %collective-permute-done.35.behind_ref = bf16[128,1024]{1,0:T(8,128)(2,1)S(1)} collective-permute-done((bf16[128,1024]{1,0:T(8,128)(2,1)S(1)}, bf16[128,1024]{1,0:T(8,128)(2,1)S(1)}, u32[]{:S(2)}, u32[]{:S(2)}) %collective-permute-start.35) | collective-permute-done | bytes 262176 | tf_op jit(solution)/shard_map/ppermute | solution.py:25
  84.8 1.8 %collective-permute-start.36 = (bf16[128,1024]{1,0:T(8,128)(2,1)S(1)}, bf16[128,1024]{1,0:T(8,128)(2,1)S(1)}, u32[]{:S(2)}, u32[]{:S(2)}) collective-permute-start(bf16[128,1024]{1,0:T(8,128)(2,1)S(1)} %get-tuple-element.58), channel_id=1, source_target_pairs={{0,32},{32,64},{64,96},{96,128},{128,160},{160,192},{192,224},{224... | collective-permute-start | bytes 786440 | tf_op jit(solution)/shard_map/ppermute | solution.py:25
  87.8 3.3 %collective-permute-done.17.refs_1_ = bf16[128,1024]{1,0:T(8,128)(2,1)S(1)} collective-permute-done((bf16[128,1024]{1,0:T(8,128)(2,1)S(1)}, bf16[128,1024]{1,0:T(8,128)(2,1)S(1)}, u32[]{:S(2)}, u32[]{:S(2)}) %collective-permute-start.17) | collective-permute-done | bytes 262176 | tf_op jit(solution)/shard_map/ppermute | solution.py:25
  91.1 3.2 %output_gradients.1 = (bf16[256,1024]{1,0:T(8,128)(2,1)}, bf16[256,1024]{1,0:T(8,128)(2,1)S(1)}, bf16[128,1024]{1,0:T(8,128)(2,1)S(1)}, f32[64,128]{1,0:T(8,128)S(1)}) custom-call(bf16[256,1024]{1,0:T(8,128)(2,1)S(1)} %get-tuple-element.34.refs_0_.refs_12_, bf16[128,1024]{1,0:T(8,128)(2,1)S(1)} %collective-permute-done.17.refs_1_, ...), custom_call_target="tpu_custom_call" | custom-call | tf_op jit(solution)/shard_map/output_gradients/pallas_call | solution.py:200
  94.3 5.1 %collective-permute-done.23 = f32[64,128]{1,0:T(8,128)S(1)} collective-permute-done((f32[64,128]{1,0:T(8,128)S(1)}, f32[64,128]{1,0:T(8,128)S(1)}, u32[]{:S(2)}, u32[]{:S(2)}) %collective-permute-start.23) | collective-permute-done | bytes 32800 | tf_op jit(solution)/shard_map/ppermute | solution.py:25
  99.4 5.4 %collective-permute-done.24 = f32[64,128]{1,0:T(8,128)S(1)} collective-permute-done((f32[64,128]{1,0:T(8,128)S(1)}, f32[64,128]{1,0:T(8,128)S(1)}, u32[]{:S(2)}, u32[]{:S(2)}) %collective-permute-start.24) | collective-permute-done | bytes 32800 | tf_op jit(solution)/shard_map/ppermute | solution.py:25
  104.8 2.4 %collective-permute-start.26 = (f32[64,128]{1,0:T(8,128)S(1)}, f32[64,128]{1,0:T(8,128)S(1)}, u32[]{:S(2)}, u32[]{:S(2)}) collective-permute-start(f32[64,128]{1,0:T(8,128)S(1)} %add.25), channel_id=1, source_target_pairs={{0,32},{32,64},{64,96},{96,128},{128,160},{160,192},{192,224},{224... | collective-permute-start | bytes 98312 | tf_op jit(solution)/shard_map/ppermute | solution.py:25
  107.6 4.2 %collective-permute-start.22 = (bf16[128,1024]{1,0:T(8,128)(2,1)S(1)}, bf16[128,1024]{1,0:T(8,128)(2,1)S(1)}, u32[]{:S(2)}, u32[]{:S(2)}) collective-permute-start(bf16[128,1024]{1,0:T(8,128)(2,1)S(1)} %get-tuple-element.46), channel_id=1, source_target_pairs={{8,0},{16,8},{24,16},{32,24},{40,32},{48,40},{56,48},{64,56},{72,6... | collective-permute-start | bytes 786440 | tf_op jit(solution)/shard_map/ppermute | solution.py:35
  112.0 2.0 %collective-permute-start.39 = (bf16[128,1024]{1,0:T(8,128)(2,1)S(1)}, bf16[128,1024]{1,0:T(8,128)(2,1)S(1)}, u32[]{:S(2)}, u32[]{:S(2)}) collective-permute-start(bf16[128,1024]{1,0:T(8,128)(2,1)S(1)} %get-tuple-element.63), channel_id=1, source_target_pairs={{0,224},{32,0},{64,32},{96,64},{128,96},{160,128},{192,160},{224,1... | collective-permute-start | bytes 786440 | tf_op jit(solution)/shard_map/ppermute | solution.py:25
  114.1 6.1 %collective-permute-start.28 = (f32[64,128]{1,0:T(8,128)S(1)}, f32[64,128]{1,0:T(8,128)S(1)}, u32[]{:S(2)}, u32[]{:S(2)}) collective-permute-start(f32[64,128]{1,0:T(8,128)S(1)} %get-tuple-element.65), channel_id=1, source_target_pairs={{0,96},{32,128},{64,160},{96,192},{128,224},{160,0},{192,32},{224,... | collective-permute-start | bytes 98312 | tf_op jit(solution)/shard_map/ppermute | solution.py:25
  121.7 5.3 %collective-permute-done.27 = f32[64,128]{1,0:T(8,128)S(1)} collective-permute-done((f32[64,128]{1,0:T(8,128)S(1)}, f32[64,128]{1,0:T(8,128)S(1)}, u32[]{:S(2)}, u32[]{:S(2)}) %collective-permute-start.27) | collective-permute-done | bytes 32800 | tf_op jit(solution)/shard_map/ppermute | solution.py:25
  127.7 2.3 %conv_backward.1 = bf16[256,1024]{1,0:T(8,128)(2,1)} custom-call(bf16[256,1024]{1,0:T(8,128)(2,1)S(1)} %get-tuple-element.45.d_ref, bf16[128,1024]{1,0:T(8,128)(2,1)S(1)} %collective-permute-done.22.next_ref, bf16[64,128]{1,0:T(8,128)(2,1)S(1)} %copy-done.4), custom_call_target="tpu_custom_call" | custom-call | tf_op jit(solution)/shard_map/conv_backward/pallas_call | solution.py:143
  (78 shorter events, 22.5 us)
Async XLA Ops:
  2.3 11.3 %all-to-all-start = ((bf16[4,256,128]{2,1,0:T(8,128)(2,1)}), bf16[4,256,128]{2,1,0:T(8,128)(2,1)S(1)}, u32[]{:S(2)}, u32[]{:S(2)}) async-start(bf16[4,256,128]{2,1,0:T(8,128)(2,1)} %bitcast_bitcast_fusion), calls=%async_computation | async-start | bytes 524288 | tf_op jit(solution)/shard_map/all_to_all | solution.py:29
  6.9 9.4 %collective-permute-start.7 = (bf16[128,1024]{1,0:T(8,128)(2,1)S(1)}, bf16[128,1024]{1,0:T(8,128)(2,1)S(1)}, u32[]{:S(2)}, u32[]{:S(2)}) collective-permute-start(bf16[128,1024]{1,0:T(8,128)(2,1)S(1)} %copy-done.3), channel_id=1, source_target_pairs={{0,32},{32,64},{64,96},{96,128},{128,160},{160,192},{192,224},{224... | collective-permute-start | bytes 786440 | tf_op jit(solution)/shard_map/ppermute | solution.py:25
  8.9 9.4 %collective-permute-start.10 = (bf16[128,1024]{1,0:T(8,128)(2,1)S(1)}, bf16[128,1024]{1,0:T(8,128)(2,1)S(1)}, u32[]{:S(2)}, u32[]{:S(2)}) collective-permute-start(bf16[128,1024]{1,0:T(8,128)(2,1)S(1)} %copy-done.3), channel_id=1, source_target_pairs={{0,224},{32,0},{64,32},{96,64},{128,96},{160,128},{192,160},{224,1... | collective-permute-start | bytes 786440 | tf_op jit(solution)/shard_map/ppermute | solution.py:25
  9.0 15.5 %collective-permute-start.21 = (bf16[128,1024]{1,0:T(8,128)(2,1)S(1)}, bf16[128,1024]{1,0:T(8,128)(2,1)S(1)}, u32[]{:S(2)}, u32[]{:S(2)}) collective-permute-start(bf16[128,1024]{1,0:T(8,128)(2,1)S(1)} %slice.11), channel_id=1, source_target_pairs={{0,8},{8,16},{16,24},{24,32},{32,40},{40,48},{48,56},{56,64},{64,7... | collective-permute-start | bytes 786440 | tf_op jit(solution)/shard_map/ppermute | solution.py:35
  13.6 14.2 %collective-permute-start.3 = (bf16[1024,128]{1,0:T(8,128)(2,1)S(1)}, bf16[1024,128]{1,0:T(8,128)(2,1)S(1)}, u32[]{:S(2)}, u32[]{:S(2)}) collective-permute-start(bf16[1024,128]{1,0:T(8,128)(2,1)S(1)} %bitcast.8), channel_id=1, source_target_pairs={{0,1},{1,0},{2,3},{3,2},{4,5},{5,4},{6,7},{7,6},{8,9},{9,8},{10,11... | collective-permute-start | bytes 786440 | tf_op jit(solution)/shard_map/ppermute | solution.py:25
  13.6 14.7 %collective-permute-start.2 = (bf16[1024,128]{1,0:T(8,128)(2,1)S(1)}, bf16[1024,128]{1,0:T(8,128)(2,1)S(1)}, u32[]{:S(2)}, u32[]{:S(2)}) collective-permute-start(bf16[1024,128]{1,0:T(8,128)(2,1)S(1)} %bitcast.9), channel_id=1, source_target_pairs={{0,6},{2,0},{4,2},{6,4},{1,7},{3,1},{5,3},{7,5},{8,14},{10,8},{12,... | collective-permute-start | bytes 786440 | tf_op jit(solution)/shard_map/ppermute | solution.py:25
  16.4 12.0 %collective-permute-start.8 = (bf16[128,1024]{1,0:T(8,128)(2,1)S(1)}, bf16[128,1024]{1,0:T(8,128)(2,1)S(1)}, u32[]{:S(2)}, u32[]{:S(2)}) collective-permute-start(bf16[128,1024]{1,0:T(8,128)(2,1)S(1)} %collective-permute-done.7.refs_9_), channel_id=1, source_target_pairs={{0,32},{32,64},{64,96},{96,128},{128,160},{160,192},{192,224},{224... | collective-permute-start | bytes 786440 | tf_op jit(solution)/shard_map/ppermute | solution.py:25
  18.3 11.7 %collective-permute-start.11 = (bf16[128,1024]{1,0:T(8,128)(2,1)S(1)}, bf16[128,1024]{1,0:T(8,128)(2,1)S(1)}, u32[]{:S(2)}, u32[]{:S(2)}) collective-permute-start(bf16[128,1024]{1,0:T(8,128)(2,1)S(1)} %collective-permute-done.10.refs_12_), channel_id=1, source_target_pairs={{0,224},{32,0},{64,32},{96,64},{128,96},{160,128},{192,160},{224,1... | collective-permute-start | bytes 786440 | tf_op jit(solution)/shard_map/ppermute | solution.py:25
  24.5 9.5 %collective-permute-start.1 = (bf16[1024,128]{1,0:T(8,128)(2,1)S(1)}, bf16[1024,128]{1,0:T(8,128)(2,1)S(1)}, u32[]{:S(2)}, u32[]{:S(2)}) collective-permute-start(bf16[1024,128]{1,0:T(8,128)(2,1)S(1)} %bitcast.10), channel_id=1, source_target_pairs={{0,4},{2,6},{4,0},{6,2},{1,5},{3,7},{5,1},{7,3},{8,12},{10,14},{12... | collective-permute-start | bytes 786440 | tf_op jit(solution)/shard_map/ppermute | solution.py:25
  27.8 9.0 %collective-permute-start = (bf16[1024,128]{1,0:T(8,128)(2,1)S(1)}, bf16[1024,128]{1,0:T(8,128)(2,1)S(1)}, u32[]{:S(2)}, u32[]{:S(2)}) collective-permute-start(bf16[1024,128]{1,0:T(8,128)(2,1)S(1)} %bitcast.11), channel_id=1, source_target_pairs={{0,2},{2,4},{4,6},{6,0},{1,3},{3,5},{5,7},{7,1},{8,10},{10,12},{12... | collective-permute-start | bytes 786440 | tf_op jit(solution)/shard_map/ppermute | solution.py:25
  28.4 9.5 %collective-permute-start.6 = (bf16[1024,128]{1,0:T(8,128)(2,1)S(1)}, bf16[1024,128]{1,0:T(8,128)(2,1)S(1)}, u32[]{:S(2)}, u32[]{:S(2)}) collective-permute-start(bf16[1024,128]{1,0:T(8,128)(2,1)S(1)} %collective-permute-done.2.refs_3_), channel_id=1, source_target_pairs={{0,1},{1,0},{2,3},{3,2},{4,5},{5,4},{6,7},{7,6},{8,9},{9,8},{10,11... | collective-permute-start | bytes 786440 | tf_op jit(solution)/shard_map/ppermute | solution.py:25
  28.4 10.3 %collective-permute-start.9 = (bf16[128,1024]{1,0:T(8,128)(2,1)S(1)}, bf16[128,1024]{1,0:T(8,128)(2,1)S(1)}, u32[]{:S(2)}, u32[]{:S(2)}) collective-permute-start(bf16[128,1024]{1,0:T(8,128)(2,1)S(1)} %collective-permute-done.8.refs_10_), channel_id=1, source_target_pairs={{0,32},{32,64},{64,96},{96,128},{128,160},{160,192},{192,224},{224... | collective-permute-start | bytes 786440 | tf_op jit(solution)/shard_map/ppermute | solution.py:25
  30.0 8.7 %collective-permute-start.12 = (bf16[128,1024]{1,0:T(8,128)(2,1)S(1)}, bf16[128,1024]{1,0:T(8,128)(2,1)S(1)}, u32[]{:S(2)}, u32[]{:S(2)}) collective-permute-start(bf16[128,1024]{1,0:T(8,128)(2,1)S(1)} %collective-permute-done.11.refs_13_), channel_id=1, source_target_pairs={{0,224},{32,0},{64,32},{96,64},{128,96},{160,128},{192,160},{224,1... | collective-permute-start | bytes 786440 | tf_op jit(solution)/shard_map/ppermute | solution.py:25
  34.1 19.4 %collective-permute-start.31 = (bf16[256,1024]{1,0:T(8,128)(2,1)S(1)}, bf16[256,1024]{1,0:T(8,128)(2,1)S(1)}, u32[]{:S(2)}, u32[]{:S(2)}) collective-permute-start(bf16[256,1024]{1,0:T(8,128)(2,1)S(1)} %get-tuple-element.48.refs_8_), channel_id=1, source_target_pairs={{0,24},{8,0},{16,8},{24,16},{1,25},{9,1},{17,9},{25,17},{2,26},{10... | collective-permute-start | bytes 1572872 | tf_op jit(solution)/shard_map/ppermute | solution.py:25
  36.8 16.7 %collective-permute-start.30 = (bf16[256,1024]{1,0:T(8,128)(2,1)S(1)}, bf16[256,1024]{1,0:T(8,128)(2,1)S(1)}, u32[]{:S(2)}, u32[]{:S(2)}) collective-permute-start(bf16[256,1024]{1,0:T(8,128)(2,1)S(1)} %get-tuple-element.48.refs_8_), channel_id=1, source_target_pairs={{0,16},{8,24},{16,0},{24,8},{1,17},{9,25},{17,1},{25,9},{2,18},{10... | collective-permute-start | bytes 1572872 | tf_op jit(solution)/shard_map/ppermute | solution.py:25
  37.9 24.2 %collective-permute-start.29 = (bf16[256,1024]{1,0:T(8,128)(2,1)S(1)}, bf16[256,1024]{1,0:T(8,128)(2,1)S(1)}, u32[]{:S(2)}, u32[]{:S(2)}) collective-permute-start(bf16[256,1024]{1,0:T(8,128)(2,1)S(1)} %get-tuple-element.48.refs_8_), channel_id=1, source_target_pairs={{0,8},{8,16},{16,24},{24,0},{1,9},{9,17},{17,25},{25,1},{2,10},{10... | collective-permute-start | bytes 1572872 | tf_op jit(solution)/shard_map/ppermute | solution.py:25
  68.4 8.9 %collective-permute-start.15 = (bf16[128,1024]{1,0:T(8,128)(2,1)S(1)}, bf16[128,1024]{1,0:T(8,128)(2,1)S(1)}, u32[]{:S(2)}, u32[]{:S(2)}) collective-permute-start(bf16[128,1024]{1,0:T(8,128)(2,1)S(1)} %get-tuple-element.35), channel_id=1, source_target_pairs={{0,8},{8,16},{16,24},{24,0},{1,9},{9,17},{17,25},{25,1},{2,10},{10... | collective-permute-start | bytes 786440 | tf_op jit(solution)/shard_map/ppermute | solution.py:25
  69.3 9.3 %collective-permute-start.16 = (bf16[128,1024]{1,0:T(8,128)(2,1)S(1)}, bf16[128,1024]{1,0:T(8,128)(2,1)S(1)}, u32[]{:S(2)}, u32[]{:S(2)}) collective-permute-start(bf16[128,1024]{1,0:T(8,128)(2,1)S(1)} %get-tuple-element.36), channel_id=1, source_target_pairs={{0,24},{8,0},{16,8},{24,16},{1,25},{9,1},{17,9},{25,17},{2,26},{10... | collective-permute-start | bytes 786440 | tf_op jit(solution)/shard_map/ppermute | solution.py:25
  73.8 7.7 %collective-permute-start.34 = (bf16[128,1024]{1,0:T(8,128)(2,1)S(1)}, bf16[128,1024]{1,0:T(8,128)(2,1)S(1)}, u32[]{:S(2)}, u32[]{:S(2)}) collective-permute-start(bf16[128,1024]{1,0:T(8,128)(2,1)S(1)} %get-tuple-element.54), channel_id=1, source_target_pairs={{0,32},{32,64},{64,96},{96,128},{128,160},{160,192},{192,224},{224... | collective-permute-start | bytes 786440 | tf_op jit(solution)/shard_map/ppermute | solution.py:25
  76.6 8.0 %collective-permute-start.35 = (bf16[128,1024]{1,0:T(8,128)(2,1)S(1)}, bf16[128,1024]{1,0:T(8,128)(2,1)S(1)}, u32[]{:S(2)}, u32[]{:S(2)}) collective-permute-start(bf16[128,1024]{1,0:T(8,128)(2,1)S(1)} %get-tuple-element.55), channel_id=1, source_target_pairs={{0,224},{32,0},{64,32},{96,64},{128,96},{160,128},{192,160},{224,1... | collective-permute-start | bytes 786440 | tf_op jit(solution)/shard_map/ppermute | solution.py:25
  76.6 10.0 %collective-permute-start.18 = (bf16[128,1024]{1,0:T(8,128)(2,1)S(1)}, bf16[128,1024]{1,0:T(8,128)(2,1)S(1)}, u32[]{:S(2)}, u32[]{:S(2)}) collective-permute-start(bf16[128,1024]{1,0:T(8,128)(2,1)S(1)} %get-tuple-element.40), channel_id=1, source_target_pairs={{0,24},{8,0},{16,8},{24,16},{1,25},{9,1},{17,9},{25,17},{2,26},{10... | collective-permute-start | bytes 786440 | tf_op jit(solution)/shard_map/ppermute | solution.py:25
  77.4 10.4 %collective-permute-start.19 = (bf16[128,1024]{1,0:T(8,128)(2,1)S(1)}, bf16[128,1024]{1,0:T(8,128)(2,1)S(1)}, u32[]{:S(2)}, u32[]{:S(2)}) collective-permute-start(bf16[128,1024]{1,0:T(8,128)(2,1)S(1)} %get-tuple-element.41), channel_id=1, source_target_pairs={{0,8},{8,16},{16,24},{24,0},{1,9},{9,17},{17,25},{25,1},{2,10},{10... | collective-permute-start | bytes 786440 | tf_op jit(solution)/shard_map/ppermute | solution.py:25
  78.8 12.3 %collective-permute-start.17 = (bf16[128,1024]{1,0:T(8,128)(2,1)S(1)}, bf16[128,1024]{1,0:T(8,128)(2,1)S(1)}, u32[]{:S(2)}, u32[]{:S(2)}) collective-permute-start(bf16[128,1024]{1,0:T(8,128)(2,1)S(1)} %get-tuple-element.39), channel_id=1, source_target_pairs={{0,8},{8,16},{16,24},{24,0},{1,9},{9,17},{17,25},{25,1},{2,10},{10... | collective-permute-start | bytes 786440 | tf_op jit(solution)/shard_map/ppermute | solution.py:25
  81.5 9.6 %collective-permute-start.20 = (bf16[128,1024]{1,0:T(8,128)(2,1)S(1)}, bf16[128,1024]{1,0:T(8,128)(2,1)S(1)}, u32[]{:S(2)}, u32[]{:S(2)}) collective-permute-start(bf16[128,1024]{1,0:T(8,128)(2,1)S(1)} %get-tuple-element.42), channel_id=1, source_target_pairs={{0,24},{8,0},{16,8},{24,16},{1,25},{9,1},{17,9},{25,17},{2,26},{10... | collective-permute-start | bytes 786440 | tf_op jit(solution)/shard_map/ppermute | solution.py:25
  84.8 27.0 %collective-permute-start.36 = (bf16[128,1024]{1,0:T(8,128)(2,1)S(1)}, bf16[128,1024]{1,0:T(8,128)(2,1)S(1)}, u32[]{:S(2)}, u32[]{:S(2)}) collective-permute-start(bf16[128,1024]{1,0:T(8,128)(2,1)S(1)} %get-tuple-element.58), channel_id=1, source_target_pairs={{0,32},{32,64},{64,96},{96,128},{128,160},{160,192},{192,224},{224... | collective-permute-start | bytes 786440 | tf_op jit(solution)/shard_map/ppermute | solution.py:25
  86.6 25.2 %collective-permute-start.37 = (bf16[128,1024]{1,0:T(8,128)(2,1)S(1)}, bf16[128,1024]{1,0:T(8,128)(2,1)S(1)}, u32[]{:S(2)}, u32[]{:S(2)}) collective-permute-start(bf16[128,1024]{1,0:T(8,128)(2,1)S(1)} %get-tuple-element.59), channel_id=1, source_target_pairs={{0,224},{32,0},{64,32},{96,64},{128,96},{160,128},{192,160},{224,1... | collective-permute-start | bytes 786440 | tf_op jit(solution)/shard_map/ppermute | solution.py:25
  104.8 9.2 %collective-permute-start.26 = (f32[64,128]{1,0:T(8,128)S(1)}, f32[64,128]{1,0:T(8,128)S(1)}, u32[]{:S(2)}, u32[]{:S(2)}) collective-permute-start(f32[64,128]{1,0:T(8,128)S(1)} %add.25), channel_id=1, source_target_pairs={{0,32},{32,64},{64,96},{96,128},{128,160},{160,192},{192,224},{224... | collective-permute-start | bytes 98312 | tf_op jit(solution)/shard_map/ppermute | solution.py:25
  107.6 20.1 %collective-permute-start.22 = (bf16[128,1024]{1,0:T(8,128)(2,1)S(1)}, bf16[128,1024]{1,0:T(8,128)(2,1)S(1)}, u32[]{:S(2)}, u32[]{:S(2)}) collective-permute-start(bf16[128,1024]{1,0:T(8,128)(2,1)S(1)} %get-tuple-element.46), channel_id=1, source_target_pairs={{8,0},{16,8},{24,16},{32,24},{40,32},{48,40},{56,48},{64,56},{72,6... | collective-permute-start | bytes 786440 | tf_op jit(solution)/shard_map/ppermute | solution.py:35
  112.0 18.1 %collective-permute-start.38 = (bf16[128,1024]{1,0:T(8,128)(2,1)S(1)}, bf16[128,1024]{1,0:T(8,128)(2,1)S(1)}, u32[]{:S(2)}, u32[]{:S(2)}) collective-permute-start(bf16[128,1024]{1,0:T(8,128)(2,1)S(1)} %get-tuple-element.62), channel_id=1, source_target_pairs={{0,32},{32,64},{64,96},{96,128},{128,160},{160,192},{192,224},{224... | collective-permute-start | bytes 786440 | tf_op jit(solution)/shard_map/ppermute | solution.py:25
  112.0 18.0 %collective-permute-start.39 = (bf16[128,1024]{1,0:T(8,128)(2,1)S(1)}, bf16[128,1024]{1,0:T(8,128)(2,1)S(1)}, u32[]{:S(2)}, u32[]{:S(2)}) collective-permute-start(bf16[128,1024]{1,0:T(8,128)(2,1)S(1)} %get-tuple-element.63), channel_id=1, source_target_pairs={{0,224},{32,0},{64,32},{96,64},{128,96},{160,128},{192,160},{224,1... | collective-permute-start | bytes 786440 | tf_op jit(solution)/shard_map/ppermute | solution.py:25
  114.1 7.7 %collective-permute-start.28 = (f32[64,128]{1,0:T(8,128)S(1)}, f32[64,128]{1,0:T(8,128)S(1)}, u32[]{:S(2)}, u32[]{:S(2)}) collective-permute-start(f32[64,128]{1,0:T(8,128)S(1)} %get-tuple-element.65), channel_id=1, source_target_pairs={{0,96},{32,128},{64,160},{96,192},{128,224},{160,0},{192,32},{224,... | collective-permute-start | bytes 98312 | tf_op jit(solution)/shard_map/ppermute | solution.py:25
  120.1 6.9 %collective-permute-start.27 = (f32[64,128]{1,0:T(8,128)S(1)}, f32[64,128]{1,0:T(8,128)S(1)}, u32[]{:S(2)}, u32[]{:S(2)}) collective-permute-start(f32[64,128]{1,0:T(8,128)S(1)} %get-tuple-element.64), channel_id=1, source_target_pairs={{0,160},{32,192},{64,224},{96,0},{128,32},{160,64},{192,96},{224,1... | collective-permute-start | bytes 98312 | tf_op jit(solution)/shard_map/ppermute | solution.py:25
  (14 other events, 117.1 us)

commit v2 on v1

--- a/solution.py
+++ b/solution.py
@@ -222,12 +222,6 @@
     return [pltpu.with_memory_space_constraint(b, pltpu.VMEM) for b in blocks]
 
 
-def owners():
-    x, c = lax.axis_index("x"), lax.axis_index("c")
-    for at in range(8):
-        yield 2 * lax.rem(x - at % 4 + 4, 4) + (c if at < 4 else 1 - c)
-
-
 def for_columns(body, channels):
     for at in range(0, channels, 2 * LANES):
         body(pl.ds(at, 2 * LANES))
@@ -246,26 +240,29 @@
 
 def output_kernel(*refs):
     u_refs, w_refs, own_ref, outs = refs[:8], refs[8:17], refs[17], refs[18:24]
-    u_all, w_all, total, sems = refs[24:]
+    w_all, total, sems = refs[24:]
     z, y = lax.axis_index("z"), lax.axis_index("y")
+    x, c = lax.axis_index("x"), lax.axis_index("c")
+
+    def piece(k):
+        owner = lax.rem(z - k + 8, 8)
+        step = lax.rem(x - owner // 2 + 4, 4)
+        return (step + 4 * lax.rem(owner + c, 2)) * LANES
+
+    pairs = []
+    for at, k in enumerate((0, 1, 2, 3, -1, -2, -3, 4, 4)):
+        count = w_refs[at].shape[0]
+        start = piece(k) + (count if at == 8 else 0)
+        start = pl.multiple_of(start, count)
+        pairs.append((w_refs[at], w_all.at[pl.ds(start, count)]))
+    run_copies(pairs, sems)
     rows = own_ref.shape[0]
     half = rows // 2
-    pairs = []
-    for u_ref, owner in zip(u_refs, owners()):
-        lanes = pl.ds(pl.multiple_of(owner * LANES, LANES), LANES)
-        pairs.append((u_ref, u_all.at[:, lanes]))
-    for at, k in enumerate((0, 1, 2, 3, -1, -2, -3)):
-        start = pl.multiple_of(lax.rem(z - k + 8, 8) * LANES, LANES)
-        pairs.append((w_refs[at], w_all.at[pl.ds(start, LANES)]))
-    far = pl.multiple_of(lax.rem(z + 4, 8) * LANES, LANES)
-    later = pl.multiple_of(far + LANES // 2, LANES // 2)
-    pairs.append((w_refs[7], w_all.at[pl.ds(far, LANES // 2)]))
-    pairs.append((w_refs[8], w_all.at[pl.ds(later, LANES // 2)]))
-    run_copies(pairs, sems)
     places = ((2, 0), (2, half), (1, half), (3, 0), (1, 0), (3, half))
 
     def body(lanes):
-        sums = jnp.dot(u_all[...], w_all[:, lanes], preferred_element_type=F32)
+        left = jnp.concatenate([u_ref[...] for u_ref in u_refs], axis=1)
+        sums = jnp.dot(left, w_all[:, lanes], preferred_element_type=F32)
         total[:, lanes] = sums.astype(BF16)
 
     for_columns(body, own_ref.shape[1])
@@ -279,20 +276,22 @@
     tokens, channels = features[0].shape[0], weights[0].shape[1]
     shape = jax.ShapeDtypeStruct((tokens // 4, channels), BF16)
     short = jax.ShapeDtypeStruct((tokens // 8, channels), BF16)
+    stored = (0, 1, 4)
+    spaces = [pltpu.HBM if at in stored else pltpu.VMEM for at in range(9)]
+    blocks = map(pltpu.with_memory_space_constraint, weights, spaces)
     return pl.pallas_call(
         output_kernel,
-        in_specs=[ANY] + [VMEM] * 7 + [ANY] + [VMEM] * 8,
+        in_specs=[VMEM] * 8 + [ANY if at in stored else VMEM for at in range(9)],
         out_specs=[VMEM] * 7,
         out_shape=[shape] + [short] * 6,
         scratch_shapes=[
-            pltpu.VMEM((tokens, 8 * LANES), BF16),
             pltpu.VMEM((8 * LANES, channels), BF16),
             pltpu.VMEM((tokens, channels), BF16),
-            pltpu.SemaphoreType.DMA((17,)),
+            pltpu.SemaphoreType.DMA((9,)),
         ],
         name="output_partials",
         compiler_params=LARGE,
-    )(features[0], *on_chip(features[1:]), weights[0], *on_chip(weights[1:]))
+    )(*on_chip(features), *blocks)
 
 
 HOPS = (3, -3, 2, -2, 1, -1, 0)
@@ -300,31 +299,35 @@
 
 def weight_kernel(*refs):
     u_refs, m_refs, far_refs, outs = refs[:8], refs[8:12], refs[13:15], refs[15:22]
-    u_all, m_all, flipped, sems = refs[22:]
+    flipped, total = refs[22:]
     z, y = lax.axis_index("z"), lax.axis_index("y")
-    pairs = []
-    for u_ref, owner in zip(u_refs, owners()):
-        start = pl.multiple_of(lax.rem(owner - z + 8, 8) * LANES, LANES)
-        pairs.append((u_ref, u_all.at[:, pl.ds(start, LANES)]))
+    x, c = lax.axis_index("x"), lax.axis_index("c")
     rows = m_refs[0].shape[0]
-    for d, m_ref in enumerate(m_refs):
+    for d in range(4):
         start = pl.multiple_of(lax.rem(y - d + 4, 4) * rows, rows)
-        pairs.append((m_ref, m_all.at[pl.ds(start, rows)]))
-    run_copies(pairs, sems)
-    flipped[...] = u_all[...].T
+        for at, u_ref in enumerate(u_refs):
+            block = u_ref[pl.ds(start, rows)]
+            flipped[at * LANES : (at + 1) * LANES, d * rows : (d + 1) * rows] = block.T
+
+    def body(lanes):
+        right = jnp.concatenate([m_ref[:, lanes] for m_ref in m_refs], axis=0)
+        sums = jnp.dot(flipped[...], right, preferred_element_type=F32)
+        total[:, lanes] = sums.astype(BF16)
+
+    for_columns(body, total.shape[1])
+
+    def block(hop):
+        owner = lax.rem(z + hop + 8, 8)
+        step = lax.rem(x - owner // 2 + 4, 4)
+        start = (step + 4 * lax.rem(owner + c, 2)) * LANES
+        return total[pl.ds(pl.multiple_of(start, LANES), LANES)]
+
+    far = block(4)
     half = LANES // 2
-
-    def body(lanes):
-        sums = jnp.dot(flipped[...], m_all[:, lanes], preferred_element_type=F32)
-        sums = sums.astype(BF16)
-        far = 4 * LANES
-        far_refs[0][:, lanes] = sums[far : far + half]
-        far_refs[1][:, lanes] = sums[far + half : far + LANES]
-        for out, hop in zip(outs, HOPS):
-            start = hop % 8 * LANES
-            out[:, lanes] = sums[start : start + LANES]
-
-    for_columns(body, m_all.shape[1])
+    far_refs[0][...] = far[:half]
+    far_refs[1][...] = far[half:]
+    for out, hop in zip(outs, HOPS):
+        out[...] = block(hop)
 
 
 def weight_partials(features, mixed, after):
@@ -333,18 +336,16 @@
     short = jax.ShapeDtypeStruct((LANES // 2, channels), BF16)
     return pl.pallas_call(
         weight_kernel,
-        in_specs=[ANY] + [VMEM] * 7 + [ANY] + [VMEM] * 3 + [ANY],
+        in_specs=[VMEM] * 12 + [ANY],
         out_specs=[VMEM] * 9,
         out_shape=[short] * 2 + [shape] * 7,
         scratch_shapes=[
-            pltpu.VMEM((tokens, 8 * LANES), BF16),
-            pltpu.VMEM((tokens, channels), BF16),
             pltpu.VMEM((8 * LANES, tokens), BF16),
-            pltpu.SemaphoreType.DMA((12,)),
+            pltpu.VMEM((8 * LANES, channels), BF16),
         ],
         name="weight_partials",
         compiler_params=LARGE,
-    )(features[0], *on_chip(features[1:]), mixed[0], *on_chip(mixed[1:]), after)
+    )(*on_chip(features), *on_chip(mixed), after)
 
 
 def add_kernel(ahead_ref, behind_ref, first_ref, last_ref, ahead_out, behind_out):
@@ -425,8 +426,8 @@
     below, above = shift(local, "z", 1), shift(local, "z", -1)
     pair = local + above
     local = pair + below
-    local = local + shift(local, "z", -3) + shift(pair, "z", 3)
-    grad_filter = local * factor
+    nearer, farther = shift(local, "z", -3), shift(pair, "z", 3)
+    grad_filter = (local + nearer + farther) * factor
     grad_input = conv_backward(d_conv, following, filters)
     return (grad_gate, grad_input, grad_filter, grad_weight)
 

time: 132 us -> 131 us (level)
  no operation moved by 1% of the time
where the time goes in v2:
time: 131 us; the launch traced here: 130 us
  starting transfers between devices  59.2 us (45%)
  waiting for transfers between devices  52.5 us (40%)
  Pallas kernels  14.3 us (11%)
  local copies, waits for them, and re-layouts  1.75 us (1%)
  other arithmetic  1.48 us (1%)
    ppermute x38, waiting for transfers between devices, shift(): return lax.ppermute(block, axis, route)  47.3 us
    ppermute x38, starting transfers between devices, shift(): return lax.ppermute(block, axis, route)  46.5 us
    ppermute x2, starting transfers between devices, from_behind(): return lax.ppermute(block, SEQ, route)  8.12 us
    all_to_all x1, starting transfers between devices, exchanged(): return lax.all_to_all(blocks, axis, split_axis=0, concat_axis=0, tiled=True)  4.59 us
    ppermute x2, waiting for transfers between devices, from_behind(): return lax.ppermute(block, SEQ, route)  4.52 us
    pallas_call x1, Pallas kernels, output_partials(): pl.pallas_call(output_kernel, in_specs=[VMEM] * 8 + [ANY if at in stored...  3.76 us
    pallas_call x1, Pallas kernels, output_gradients(): pl.pallas_call(gradient_kernel, grid=(channels // STEP,), in_specs=[tile(...  3.16 us
  transfers between devices with their start and end apart: 41, of which 19 were waited for; matrix products, arithmetic and copies ran while one was open for 1% of the time, Pallas kernels for 9%

profile of v2, /device:TPU:32, one launch (start us, length us, event | category | flops | bytes accessed | tf_op | source)
XLA Modules:
  0.0 130.1 jit_solution(358815915225885060)
XLA Ops:
  2.3 4.6 %all-to-all-start = ((bf16[4,256,128]{2,1,0:T(8,128)(2,1)}), bf16[4,256,128]{2,1,0:T(8,128)(2,1)S(1)}, u32[]{:S(2)}, u32[]{:S(2)}) async-start(bf16[4,256,128]{2,1,0:T(8,128)(2,1)} %bitcast_bitcast_fusion), calls=%async_computation | async-start | bytes 524288 | tf_op jit(solution)/shard_map/all_to_all | solution.py:29
  6.9 1.9 %collective-permute-start.7 = (bf16[128,1024]{1,0:T(8,128)(2,1)S(1)}, bf16[128,1024]{1,0:T(8,128)(2,1)S(1)}, u32[]{:S(2)}, u32[]{:S(2)}) collective-permute-start(bf16[128,1024]{1,0:T(8,128)(2,1)S(1)} %copy-done.4), channel_id=1, source_target_pairs={{0,32},{32,64},{64,96},{96,128},{128,160},{160,192},{192,224},{224... | collective-permute-start | bytes 786440 | tf_op jit(solution)/shard_map/ppermute | solution.py:25
  9.0 3.9 %collective-permute-start.21 = (bf16[128,1024]{1,0:T(8,128)(2,1)S(1)}, bf16[128,1024]{1,0:T(8,128)(2,1)S(1)}, u32[]{:S(2)}, u32[]{:S(2)}) collective-permute-start(bf16[128,1024]{1,0:T(8,128)(2,1)S(1)} %slice.11), channel_id=1, source_target_pairs={{0,8},{8,16},{16,24},{24,32},{32,40},{40,48},{48,56},{56,64},{64,7... | collective-permute-start | bytes 786440 | tf_op jit(solution)/shard_map/ppermute | solution.py:35
  13.6 2.8 %collective-permute-start.2 = (bf16[1024,128]{1,0:T(8,128)(2,1)S(1)}, bf16[1024,128]{1,0:T(8,128)(2,1)S(1)}, u32[]{:S(2)}, u32[]{:S(2)}) collective-permute-start(bf16[1024,128]{1,0:T(8,128)(2,1)S(1)} %bitcast.9), channel_id=1, source_target_pairs={{0,6},{2,0},{4,2},{6,4},{1,7},{3,1},{5,3},{7,5},{8,14},{10,8},{12,... | collective-permute-start | bytes 786440 | tf_op jit(solution)/shard_map/ppermute | solution.py:25
  16.4 1.9 %collective-permute-start.8 = (bf16[128,1024]{1,0:T(8,128)(2,1)S(1)}, bf16[128,1024]{1,0:T(8,128)(2,1)S(1)}, u32[]{:S(2)}, u32[]{:S(2)}) collective-permute-start(bf16[128,1024]{1,0:T(8,128)(2,1)S(1)} %collective-permute-done.7.refs_9_), channel_id=1, source_target_pairs={{0,32},{32,64},{64,96},{96,128},{128,160},{160,192},{192,224},{224... | collective-permute-start | bytes 786440 | tf_op jit(solution)/shard_map/ppermute | solution.py:25
  20.0 4.5 %collective-permute-done.21.prev_ref.refs_7_ = bf16[128,1024]{1,0:T(8,128)(2,1)S(1)} collective-permute-done((bf16[128,1024]{1,0:T(8,128)(2,1)S(1)}, bf16[128,1024]{1,0:T(8,128)(2,1)S(1)}, u32[]{:S(2)}, u32[]{:S(2)}) %collective-permute-start.21) | collective-permute-done | bytes 262176 | tf_op jit(solution)/shard_map/ppermute | solution.py:35
  24.5 3.2 %collective-permute-start.1 = (bf16[1024,128]{1,0:T(8,128)(2,1)S(1)}, bf16[1024,128]{1,0:T(8,128)(2,1)S(1)}, u32[]{:S(2)}, u32[]{:S(2)}) collective-permute-start(bf16[1024,128]{1,0:T(8,128)(2,1)S(1)} %bitcast.10), channel_id=1, source_target_pairs={{0,4},{2,6},{4,0},{6,2},{1,5},{3,7},{5,1},{7,3},{8,12},{10,14},{12... | collective-permute-start | bytes 786440 | tf_op jit(solution)/shard_map/ppermute | solution.py:25
  30.0 1.8 %collective-permute-start.12 = (bf16[128,1024]{1,0:T(8,128)(2,1)S(1)}, bf16[128,1024]{1,0:T(8,128)(2,1)S(1)}, u32[]{:S(2)}, u32[]{:S(2)}) collective-permute-start(bf16[128,1024]{1,0:T(8,128)(2,1)S(1)} %collective-permute-done.11.refs_13_), channel_id=1, source_target_pairs={{0,224},{32,0},{64,32},{96,64},{128,96},{160,128},{192,160},{224,1... | collective-permute-start | bytes 786440 | tf_op jit(solution)/shard_map/ppermute | solution.py:25
  31.8 2.1 %conv_forward.1 = (bf16[256,1024]{1,0:T(8,128)(2,1)S(1)}, f32[256,1024]{1,0:T(8,128)S(1)}) custom-call(bf16[128,1024]{1,0:T(8,128)(2,1)S(1)} %collective-permute-done.21.prev_ref.refs_7_, bf16[256,1024]{1,0:T(8,128)(2,1)S(1)} %copy-done.1, bf16[256,1024]{1,0:T(8,128)(2,1)S(1)} %copy-done.2, bf16[64,128]{1,0:T(8,128)(2,1)S(1)} %copy-done.3), custom_call_target="tpu_custom_call" | custom-call | tf_op jit(solution)/shard_map/conv_forward/pallas_call | solution.py:110
  40.2 2.4 %collective-permute-start.13 = (bf16[64,1024]{1,0:T(8,128)(2,1)S(1)}, bf16[64,1024]{1,0:T(8,128)(2,1)S(1)}, u32[]{:S(2)}, u32[]{:S(2)}) collective-permute-start(bf16[64,1024]{1,0:T(8,128)(2,1)S(1)} %slice.12), channel_id=1, source_target_pairs={{0,32},{32,64},{64,96},{96,128},{128,160},{160,192},{192,224},{224... | collective-permute-start | bytes 393224 | tf_op jit(solution)/shard_map/ppermute | solution.py:25
  43.6 3.4 %collective-permute-done.13.refs_15_ = bf16[64,1024]{1,0:T(8,128)(2,1)S(1)} collective-permute-done((bf16[64,1024]{1,0:T(8,128)(2,1)S(1)}, bf16[64,1024]{1,0:T(8,128)(2,1)S(1)}, u32[]{:S(2)}, u32[]{:S(2)}) %collective-permute-start.13) | collective-permute-done | bytes 131104 | tf_op jit(solution)/shard_map/ppermute | solution.py:25
  47.0 2.5 %collective-permute-done.14.refs_16_ = bf16[64,1024]{1,0:T(8,128)(2,1)S(1)} collective-permute-done((bf16[64,1024]{1,0:T(8,128)(2,1)S(1)}, bf16[64,1024]{1,0:T(8,128)(2,1)S(1)}, u32[]{:S(2)}, u32[]{:S(2)}) %collective-permute-start.14) | collective-permute-done | bytes 131104 | tf_op jit(solution)/shard_map/ppermute | solution.py:25
  49.5 3.8 %output_partials.1 = (bf16[256,1024]{1,0:T(8,128)(2,1)S(1)}, bf16[128,1024]{1,0:T(8,128)(2,1)S(1)}, bf16[128,1024]{1,0:T(8,128)(2,1)S(1)}, bf16[128,1024]{1,0:T(...) custom-call(bf16[1024,128]{1,0:T(8,128)(2,1)S(1)} %bitcast.12, ...), custom_call_target="tpu_custom_call" | custom-call | tf_op jit(solution)/shard_map/output_partials/pallas_call | solution.py:282
  53.3 8.8 %collective-permute-done.29.refs_9_ = bf16[256,1024]{1,0:T(8,128)(2,1)S(1)} collective-permute-done((bf16[256,1024]{1,0:T(8,128)(2,1)S(1)}, bf16[256,1024]{1,0:T(8,128)(2,1)S(1)}, u32[]{:S(2)}, u32[]{:S(2)}) %collective-permute-start.29) | collective-permute-done | bytes 524320 | tf_op jit(solution)/shard_map/ppermute | solution.py:25
  62.0 2.5 %weight_partials.1 = (bf16[64,1024]{1,0:T(8,128)(2,1)S(1)}, bf16[64,1024]{1,0:T(8,128)(2,1)S(1)}, bf16[128,1024]{1,0:T(8,128)(2,1)S(1)}, bf16[128,1024]{1,0:T(8,...) custom-call(bf16[1024,128]{1,0:T(8,128)(2,1)S(1)} %bitcast.13, ...), custom_call_target="tpu_custom_call" | custom-call | tf_op jit(solution)/shard_map/weight_partials/pallas_call | solution.py:337
  64.6 3.1 %collective-permute-start.32 = (bf16[64,1024]{1,0:T(8,128)(2,1)S(1)}, bf16[64,1024]{1,0:T(8,128)(2,1)S(1)}, u32[]{:S(2)}, u32[]{:S(2)}) collective-permute-start(bf16[64,1024]{1,0:T(8,128)(2,1)S(1)} %get-tuple-element.50), channel_id=1, source_target_pairs={{0,32},{32,64},{64,96},{96,128},{128,160},{160,192},{192,224},{224... | collective-permute-start | bytes 393224 | tf_op jit(solution)/shard_map/ppermute | solution.py:25
  68.5 2.3 %collective-permute-start.16 = (bf16[128,1024]{1,0:T(8,128)(2,1)S(1)}, bf16[128,1024]{1,0:T(8,128)(2,1)S(1)}, u32[]{:S(2)}, u32[]{:S(2)}) collective-permute-start(bf16[128,1024]{1,0:T(8,128)(2,1)S(1)} %get-tuple-element.36), channel_id=1, source_target_pairs={{0,24},{8,0},{16,8},{24,16},{1,25},{9,1},{17,9},{25,17},{2,26},{10... | collective-permute-start | bytes 786440 | tf_op jit(solution)/shard_map/ppermute | solution.py:25
  70.9 2.1 %collective-permute-done.33.behind_ref = bf16[64,1024]{1,0:T(8,128)(2,1)S(1)} collective-permute-done((bf16[64,1024]{1,0:T(8,128)(2,1)S(1)}, bf16[64,1024]{1,0:T(8,128)(2,1)S(1)}, u32[]{:S(2)}, u32[]{:S(2)}) %collective-permute-start.33) | collective-permute-done | bytes 131104 | tf_op jit(solution)/shard_map/ppermute | solution.py:25
  73.1 2.8 %collective-permute-start.34 = (bf16[128,1024]{1,0:T(8,128)(2,1)S(1)}, bf16[128,1024]{1,0:T(8,128)(2,1)S(1)}, u32[]{:S(2)}, u32[]{:S(2)}) collective-permute-start(bf16[128,1024]{1,0:T(8,128)(2,1)S(1)} %get-tuple-element.54), channel_id=1, source_target_pairs={{0,32},{32,64},{64,96},{96,128},{128,160},{160,192},{192,224},{224... | collective-permute-start | bytes 786440 | tf_op jit(solution)/shard_map/ppermute | solution.py:25
  78.1 2.6 %collective-permute-done.34.ahead_ref = bf16[128,1024]{1,0:T(8,128)(2,1)S(1)} collective-permute-done((bf16[128,1024]{1,0:T(8,128)(2,1)S(1)}, bf16[128,1024]{1,0:T(8,128)(2,1)S(1)}, u32[]{:S(2)}, u32[]{:S(2)}) %collective-permute-start.34) | collective-permute-done | bytes 262176 | tf_op jit(solution)/shard_map/ppermute | solution.py:25
  81.3 2.5 %collective-permute-done.35.behind_ref = bf16[128,1024]{1,0:T(8,128)(2,1)S(1)} collective-permute-done((bf16[128,1024]{1,0:T(8,128)(2,1)S(1)}, bf16[128,1024]{1,0:T(8,128)(2,1)S(1)}, u32[]{:S(2)}, u32[]{:S(2)}) %collective-permute-start.35) | collective-permute-done | bytes 262176 | tf_op jit(solution)/shard_map/ppermute | solution.py:25
  84.0 1.8 %collective-permute-start.36 = (bf16[128,1024]{1,0:T(8,128)(2,1)S(1)}, bf16[128,1024]{1,0:T(8,128)(2,1)S(1)}, u32[]{:S(2)}, u32[]{:S(2)}) collective-permute-start(bf16[128,1024]{1,0:T(8,128)(2,1)S(1)} %get-tuple-element.58), channel_id=1, source_target_pairs={{0,32},{32,64},{64,96},{96,128},{128,160},{160,192},{192,224},{224... | collective-permute-start | bytes 786440 | tf_op jit(solution)/shard_map/ppermute | solution.py:25
  87.0 3.3 %collective-permute-done.17.refs_1_ = bf16[128,1024]{1,0:T(8,128)(2,1)S(1)} collective-permute-done((bf16[128,1024]{1,0:T(8,128)(2,1)S(1)}, bf16[128,1024]{1,0:T(8,128)(2,1)S(1)}, u32[]{:S(2)}, u32[]{:S(2)}) %collective-permute-start.17) | collective-permute-done | bytes 262176 | tf_op jit(solution)/shard_map/ppermute | solution.py:25
  90.3 3.2 %output_gradients.1 = (bf16[256,1024]{1,0:T(8,128)(2,1)}, bf16[256,1024]{1,0:T(8,128)(2,1)S(1)}, bf16[128,1024]{1,0:T(8,128)(2,1)S(1)}, f32[64,128]{1,0:T(8,128)S(1)}) custom-call(bf16[256,1024]{1,0:T(8,128)(2,1)S(1)} %get-tuple-element.34.refs_0_.refs_12_, bf16[128,1024]{1,0:T(8,128)(2,1)S(1)} %collective-permute-done.17.refs_1_, ...), custom_call_target="tpu_custom_call" | custom-call | tf_op jit(solution)/shard_map/output_gradients/pallas_call | solution.py:200
  93.5 5.1 %collective-permute-done.23 = f32[64,128]{1,0:T(8,128)S(1)} collective-permute-done((f32[64,128]{1,0:T(8,128)S(1)}, f32[64,128]{1,0:T(8,128)S(1)}, u32[]{:S(2)}, u32[]{:S(2)}) %collective-permute-start.23) | collective-permute-done | bytes 32800 | tf_op jit(solution)/shard_map/ppermute | solution.py:25
  98.6 5.4 %collective-permute-done.24 = f32[64,128]{1,0:T(8,128)S(1)} collective-permute-done((f32[64,128]{1,0:T(8,128)S(1)}, f32[64,128]{1,0:T(8,128)S(1)}, u32[]{:S(2)}, u32[]{:S(2)}) %collective-permute-start.24) | collective-permute-done | bytes 32800 | tf_op jit(solution)/shard_map/ppermute | solution.py:25
  104.0 2.3 %collective-permute-start.26 = (f32[64,128]{1,0:T(8,128)S(1)}, f32[64,128]{1,0:T(8,128)S(1)}, u32[]{:S(2)}, u32[]{:S(2)}) collective-permute-start(f32[64,128]{1,0:T(8,128)S(1)} %add.25), channel_id=1, source_target_pairs={{0,32},{32,64},{64,96},{96,128},{128,160},{160,192},{192,224},{224... | collective-permute-start | bytes 98312 | tf_op jit(solution)/shard_map/ppermute | solution.py:25
  106.8 4.2 %collective-permute-start.22 = (bf16[128,1024]{1,0:T(8,128)(2,1)S(1)}, bf16[128,1024]{1,0:T(8,128)(2,1)S(1)}, u32[]{:S(2)}, u32[]{:S(2)}) collective-permute-start(bf16[128,1024]{1,0:T(8,128)(2,1)S(1)} %get-tuple-element.46), channel_id=1, source_target_pairs={{8,0},{16,8},{24,16},{32,24},{40,32},{48,40},{56,48},{64,56},{72,6... | collective-permute-start | bytes 786440 | tf_op jit(solution)/shard_map/ppermute | solution.py:35
  111.3 2.0 %collective-permute-start.39 = (bf16[128,1024]{1,0:T(8,128)(2,1)S(1)}, bf16[128,1024]{1,0:T(8,128)(2,1)S(1)}, u32[]{:S(2)}, u32[]{:S(2)}) collective-permute-start(bf16[128,1024]{1,0:T(8,128)(2,1)S(1)} %get-tuple-element.63), channel_id=1, source_target_pairs={{0,224},{32,0},{64,32},{96,64},{128,96},{160,128},{192,160},{224,1... | collective-permute-start | bytes 786440 | tf_op jit(solution)/shard_map/ppermute | solution.py:25
  113.3 6.1 %collective-permute-start.28 = (f32[64,128]{1,0:T(8,128)S(1)}, f32[64,128]{1,0:T(8,128)S(1)}, u32[]{:S(2)}, u32[]{:S(2)}) collective-permute-start(f32[64,128]{1,0:T(8,128)S(1)} %get-tuple-element.65), channel_id=1, source_target_pairs={{0,96},{32,128},{64,160},{96,192},{128,224},{160,0},{192,32},{224,... | collective-permute-start | bytes 98312 | tf_op jit(solution)/shard_map/ppermute | solution.py:25
  121.0 5.3 %collective-permute-done.27 = f32[64,128]{1,0:T(8,128)S(1)} collective-permute-done((f32[64,128]{1,0:T(8,128)S(1)}, f32[64,128]{1,0:T(8,128)S(1)}, u32[]{:S(2)}, u32[]{:S(2)}) %collective-permute-start.27) | collective-permute-done | bytes 32800 | tf_op jit(solution)/shard_map/ppermute | solution.py:25
  126.9 2.3 %conv_backward.1 = bf16[256,1024]{1,0:T(8,128)(2,1)} custom-call(bf16[256,1024]{1,0:T(8,128)(2,1)S(1)} %get-tuple-element.45.d_ref, bf16[128,1024]{1,0:T(8,128)(2,1)S(1)} %collective-permute-done.22.next_ref, bf16[64,128]{1,0:T(8,128)(2,1)S(1)} %copy-done.3), custom_call_target="tpu_custom_call" | custom-call | tf_op jit(solution)/shard_map/conv_backward/pallas_call | solution.py:143
  (82 shorter events, 22.7 us)
Async XLA Ops:
  2.3 11.3 %all-to-all-start = ((bf16[4,256,128]{2,1,0:T(8,128)(2,1)}), bf16[4,256,128]{2,1,0:T(8,128)(2,1)S(1)}, u32[]{:S(2)}, u32[]{:S(2)}) async-start(bf16[4,256,128]{2,1,0:T(8,128)(2,1)} %bitcast_bitcast_fusion), calls=%async_computation | async-start | bytes 524288 | tf_op jit(solution)/shard_map/all_to_all | solution.py:29
  6.9 9.4 %collective-permute-start.7 = (bf16[128,1024]{1,0:T(8,128)(2,1)S(1)}, bf16[128,1024]{1,0:T(8,128)(2,1)S(1)}, u32[]{:S(2)}, u32[]{:S(2)}) collective-permute-start(bf16[128,1024]{1,0:T(8,128)(2,1)S(1)} %copy-done.4), channel_id=1, source_target_pairs={{0,32},{32,64},{64,96},{96,128},{128,160},{160,192},{192,224},{224... | collective-permute-start | bytes 786440 | tf_op jit(solution)/shard_map/ppermute | solution.py:25
  8.9 9.4 %collective-permute-start.10 = (bf16[128,1024]{1,0:T(8,128)(2,1)S(1)}, bf16[128,1024]{1,0:T(8,128)(2,1)S(1)}, u32[]{:S(2)}, u32[]{:S(2)}) collective-permute-start(bf16[128,1024]{1,0:T(8,128)(2,1)S(1)} %copy-done.4), channel_id=1, source_target_pairs={{0,224},{32,0},{64,32},{96,64},{128,96},{160,128},{192,160},{224,1... | collective-permute-start | bytes 786440 | tf_op jit(solution)/shard_map/ppermute | solution.py:25
  9.0 15.5 %collective-permute-start.21 = (bf16[128,1024]{1,0:T(8,128)(2,1)S(1)}, bf16[128,1024]{1,0:T(8,128)(2,1)S(1)}, u32[]{:S(2)}, u32[]{:S(2)}) collective-permute-start(bf16[128,1024]{1,0:T(8,128)(2,1)S(1)} %slice.11), channel_id=1, source_target_pairs={{0,8},{8,16},{16,24},{24,32},{32,40},{40,48},{48,56},{56,64},{64,7... | collective-permute-start | bytes 786440 | tf_op jit(solution)/shard_map/ppermute | solution.py:35
  13.6 14.2 %collective-permute-start.3 = (bf16[1024,128]{1,0:T(8,128)(2,1)S(1)}, bf16[1024,128]{1,0:T(8,128)(2,1)S(1)}, u32[]{:S(2)}, u32[]{:S(2)}) collective-permute-start(bf16[1024,128]{1,0:T(8,128)(2,1)S(1)} %bitcast.8), channel_id=1, source_target_pairs={{0,1},{1,0},{2,3},{3,2},{4,5},{5,4},{6,7},{7,6},{8,9},{9,8},{10,11... | collective-permute-start | bytes 786440 | tf_op jit(solution)/shard_map/ppermute | solution.py:25
  13.6 14.7 %collective-permute-start.2 = (bf16[1024,128]{1,0:T(8,128)(2,1)S(1)}, bf16[1024,128]{1,0:T(8,128)(2,1)S(1)}, u32[]{:S(2)}, u32[]{:S(2)}) collective-permute-start(bf16[1024,128]{1,0:T(8,128)(2,1)S(1)} %bitcast.9), channel_id=1, source_target_pairs={{0,6},{2,0},{4,2},{6,4},{1,7},{3,1},{5,3},{7,5},{8,14},{10,8},{12,... | collective-permute-start | bytes 786440 | tf_op jit(solution)/shard_map/ppermute | solution.py:25
  16.4 12.0 %collective-permute-start.8 = (bf16[128,1024]{1,0:T(8,128)(2,1)S(1)}, bf16[128,1024]{1,0:T(8,128)(2,1)S(1)}, u32[]{:S(2)}, u32[]{:S(2)}) collective-permute-start(bf16[128,1024]{1,0:T(8,128)(2,1)S(1)} %collective-permute-done.7.refs_9_), channel_id=1, source_target_pairs={{0,32},{32,64},{64,96},{96,128},{128,160},{160,192},{192,224},{224... | collective-permute-start | bytes 786440 | tf_op jit(solution)/shard_map/ppermute | solution.py:25
  18.3 11.7 %collective-permute-start.11 = (bf16[128,1024]{1,0:T(8,128)(2,1)S(1)}, bf16[128,1024]{1,0:T(8,128)(2,1)S(1)}, u32[]{:S(2)}, u32[]{:S(2)}) collective-permute-start(bf16[128,1024]{1,0:T(8,128)(2,1)S(1)} %collective-permute-done.10.refs_12_), channel_id=1, source_target_pairs={{0,224},{32,0},{64,32},{96,64},{128,96},{160,128},{192,160},{224,1... | collective-permute-start | bytes 786440 | tf_op jit(solution)/shard_map/ppermute | solution.py:25
  24.5 9.5 %collective-permute-start.1 = (bf16[1024,128]{1,0:T(8,128)(2,1)S(1)}, bf16[1024,128]{1,0:T(8,128)(2,1)S(1)}, u32[]{:S(2)}, u32[]{:S(2)}) collective-permute-start(bf16[1024,128]{1,0:T(8,128)(2,1)S(1)} %bitcast.10), channel_id=1, source_target_pairs={{0,4},{2,6},{4,0},{6,2},{1,5},{3,7},{5,1},{7,3},{8,12},{10,14},{12... | collective-permute-start | bytes 786440 | tf_op jit(solution)/shard_map/ppermute | solution.py:25
  27.8 9.0 %collective-permute-start = (bf16[1024,128]{1,0:T(8,128)(2,1)S(1)}, bf16[1024,128]{1,0:T(8,128)(2,1)S(1)}, u32[]{:S(2)}, u32[]{:S(2)}) collective-permute-start(bf16[1024,128]{1,0:T(8,128)(2,1)S(1)} %bitcast.11), channel_id=1, source_target_pairs={{0,2},{2,4},{4,6},{6,0},{1,3},{3,5},{5,7},{7,1},{8,10},{10,12},{12... | collective-permute-start | bytes 786440 | tf_op jit(solution)/shard_map/ppermute | solution.py:25
  28.4 9.5 %collective-permute-start.6 = (bf16[1024,128]{1,0:T(8,128)(2,1)S(1)}, bf16[1024,128]{1,0:T(8,128)(2,1)S(1)}, u32[]{:S(2)}, u32[]{:S(2)}) collective-permute-start(bf16[1024,128]{1,0:T(8,128)(2,1)S(1)} %collective-permute-done.2.refs_3_), channel_id=1, source_target_pairs={{0,1},{1,0},{2,3},{3,2},{4,5},{5,4},{6,7},{7,6},{8,9},{9,8},{10,11... | collective-permute-start | bytes 786440 | tf_op jit(solution)/shard_map/ppermute | solution.py:25
  28.4 10.3 %collective-permute-start.9 = (bf16[128,1024]{1,0:T(8,128)(2,1)S(1)}, bf16[128,1024]{1,0:T(8,128)(2,1)S(1)}, u32[]{:S(2)}, u32[]{:S(2)}) collective-permute-start(bf16[128,1024]{1,0:T(8,128)(2,1)S(1)} %collective-permute-done.8.refs_10_), channel_id=1, source_target_pairs={{0,32},{32,64},{64,96},{96,128},{128,160},{160,192},{192,224},{224... | collective-permute-start | bytes 786440 | tf_op jit(solution)/shard_map/ppermute | solution.py:25
  30.0 8.7 %collective-permute-start.12 = (bf16[128,1024]{1,0:T(8,128)(2,1)S(1)}, bf16[128,1024]{1,0:T(8,128)(2,1)S(1)}, u32[]{:S(2)}, u32[]{:S(2)}) collective-permute-start(bf16[128,1024]{1,0:T(8,128)(2,1)S(1)} %collective-permute-done.11.refs_13_), channel_id=1, source_target_pairs={{0,224},{32,0},{64,32},{96,64},{128,96},{160,128},{192,160},{224,1... | collective-permute-start | bytes 786440 | tf_op jit(solution)/shard_map/ppermute | solution.py:25
  34.1 19.2 %collective-permute-start.31 = (bf16[256,1024]{1,0:T(8,128)(2,1)S(1)}, bf16[256,1024]{1,0:T(8,128)(2,1)S(1)}, u32[]{:S(2)}, u32[]{:S(2)}) collective-permute-start(bf16[256,1024]{1,0:T(8,128)(2,1)S(1)} %get-tuple-element.48.refs_8_), channel_id=1, source_target_pairs={{0,24},{8,0},{16,8},{24,16},{1,25},{9,1},{17,9},{25,17},{2,26},{10... | collective-permute-start | bytes 1572872 | tf_op jit(solution)/shard_map/ppermute | solution.py:25
  36.8 16.5 %collective-permute-start.30 = (bf16[256,1024]{1,0:T(8,128)(2,1)S(1)}, bf16[256,1024]{1,0:T(8,128)(2,1)S(1)}, u32[]{:S(2)}, u32[]{:S(2)}) collective-permute-start(bf16[256,1024]{1,0:T(8,128)(2,1)S(1)} %get-tuple-element.48.refs_8_), channel_id=1, source_target_pairs={{0,16},{8,24},{16,0},{24,8},{1,17},{9,25},{17,1},{25,9},{2,18},{10... | collective-permute-start | bytes 1572872 | tf_op jit(solution)/shard_map/ppermute | solution.py:25
  37.9 24.2 %collective-permute-start.29 = (bf16[256,1024]{1,0:T(8,128)(2,1)S(1)}, bf16[256,1024]{1,0:T(8,128)(2,1)S(1)}, u32[]{:S(2)}, u32[]{:S(2)}) collective-permute-start(bf16[256,1024]{1,0:T(8,128)(2,1)S(1)} %get-tuple-element.48.refs_8_), channel_id=1, source_target_pairs={{0,8},{8,16},{16,24},{24,0},{1,9},{9,17},{17,25},{25,1},{2,10},{10... | collective-permute-start | bytes 1572872 | tf_op jit(solution)/shard_map/ppermute | solution.py:25
  67.7 8.9 %collective-permute-start.15 = (bf16[128,1024]{1,0:T(8,128)(2,1)S(1)}, bf16[128,1024]{1,0:T(8,128)(2,1)S(1)}, u32[]{:S(2)}, u32[]{:S(2)}) collective-permute-start(bf16[128,1024]{1,0:T(8,128)(2,1)S(1)} %get-tuple-element.35), channel_id=1, source_target_pairs={{0,8},{8,16},{16,24},{24,0},{1,9},{9,17},{17,25},{25,1},{2,10},{10... | collective-permute-start | bytes 786440 | tf_op jit(solution)/shard_map/ppermute | solution.py:25
  68.5 9.3 %collective-permute-start.16 = (bf16[128,1024]{1,0:T(8,128)(2,1)S(1)}, bf16[128,1024]{1,0:T(8,128)(2,1)S(1)}, u32[]{:S(2)}, u32[]{:S(2)}) collective-permute-start(bf16[128,1024]{1,0:T(8,128)(2,1)S(1)} %get-tuple-element.36), channel_id=1, source_target_pairs={{0,24},{8,0},{16,8},{24,16},{1,25},{9,1},{17,9},{25,17},{2,26},{10... | collective-permute-start | bytes 786440 | tf_op jit(solution)/shard_map/ppermute | solution.py:25
  73.1 7.7 %collective-permute-start.34 = (bf16[128,1024]{1,0:T(8,128)(2,1)S(1)}, bf16[128,1024]{1,0:T(8,128)(2,1)S(1)}, u32[]{:S(2)}, u32[]{:S(2)}) collective-permute-start(bf16[128,1024]{1,0:T(8,128)(2,1)S(1)} %get-tuple-element.54), channel_id=1, source_target_pairs={{0,32},{32,64},{64,96},{96,128},{128,160},{160,192},{192,224},{224... | collective-permute-start | bytes 786440 | tf_op jit(solution)/shard_map/ppermute | solution.py:25
  75.8 8.0 %collective-permute-start.35 = (bf16[128,1024]{1,0:T(8,128)(2,1)S(1)}, bf16[128,1024]{1,0:T(8,128)(2,1)S(1)}, u32[]{:S(2)}, u32[]{:S(2)}) collective-permute-start(bf16[128,1024]{1,0:T(8,128)(2,1)S(1)} %get-tuple-element.55), channel_id=1, source_target_pairs={{0,224},{32,0},{64,32},{96,64},{128,96},{160,128},{192,160},{224,1... | collective-permute-start | bytes 786440 | tf_op jit(solution)/shard_map/ppermute | solution.py:25
  75.8 10.0 %collective-permute-start.18 = (bf16[128,1024]{1,0:T(8,128)(2,1)S(1)}, bf16[128,1024]{1,0:T(8,128)(2,1)S(1)}, u32[]{:S(2)}, u32[]{:S(2)}) collective-permute-start(bf16[128,1024]{1,0:T(8,128)(2,1)S(1)} %get-tuple-element.40), channel_id=1, source_target_pairs={{0,24},{8,0},{16,8},{24,16},{1,25},{9,1},{17,9},{25,17},{2,26},{10... | collective-permute-start | bytes 786440 | tf_op jit(solution)/shard_map/ppermute | solution.py:25
  76.6 10.4 %collective-permute-start.19 = (bf16[128,1024]{1,0:T(8,128)(2,1)S(1)}, bf16[128,1024]{1,0:T(8,128)(2,1)S(1)}, u32[]{:S(2)}, u32[]{:S(2)}) collective-permute-start(bf16[128,1024]{1,0:T(8,128)(2,1)S(1)} %get-tuple-element.41), channel_id=1, source_target_pairs={{0,8},{8,16},{16,24},{24,0},{1,9},{9,17},{17,25},{25,1},{2,10},{10... | collective-permute-start | bytes 786440 | tf_op jit(solution)/shard_map/ppermute | solution.py:25
  78.0 12.3 %collective-permute-start.17 = (bf16[128,1024]{1,0:T(8,128)(2,1)S(1)}, bf16[128,1024]{1,0:T(8,128)(2,1)S(1)}, u32[]{:S(2)}, u32[]{:S(2)}) collective-permute-start(bf16[128,1024]{1,0:T(8,128)(2,1)S(1)} %get-tuple-element.39), channel_id=1, source_target_pairs={{0,8},{8,16},{16,24},{24,0},{1,9},{9,17},{17,25},{25,1},{2,10},{10... | collective-permute-start | bytes 786440 | tf_op jit(solution)/shard_map/ppermute | solution.py:25
  80.7 9.6 %collective-permute-start.20 = (bf16[128,1024]{1,0:T(8,128)(2,1)S(1)}, bf16[128,1024]{1,0:T(8,128)(2,1)S(1)}, u32[]{:S(2)}, u32[]{:S(2)}) collective-permute-start(bf16[128,1024]{1,0:T(8,128)(2,1)S(1)} %get-tuple-element.42), channel_id=1, source_target_pairs={{0,24},{8,0},{16,8},{24,16},{1,25},{9,1},{17,9},{25,17},{2,26},{10... | collective-permute-start | bytes 786440 | tf_op jit(solution)/shard_map/ppermute | solution.py:25
  84.0 27.1 %collective-permute-start.36 = (bf16[128,1024]{1,0:T(8,128)(2,1)S(1)}, bf16[128,1024]{1,0:T(8,128)(2,1)S(1)}, u32[]{:S(2)}, u32[]{:S(2)}) collective-permute-start(bf16[128,1024]{1,0:T(8,128)(2,1)S(1)} %get-tuple-element.58), channel_id=1, source_target_pairs={{0,32},{32,64},{64,96},{96,128},{128,160},{160,192},{192,224},{224... | collective-permute-start | bytes 786440 | tf_op jit(solution)/shard_map/ppermute | solution.py:25
  85.8 25.2 %collective-permute-start.37 = (bf16[128,1024]{1,0:T(8,128)(2,1)S(1)}, bf16[128,1024]{1,0:T(8,128)(2,1)S(1)}, u32[]{:S(2)}, u32[]{:S(2)}) collective-permute-start(bf16[128,1024]{1,0:T(8,128)(2,1)S(1)} %get-tuple-element.59), channel_id=1, source_target_pairs={{0,224},{32,0},{64,32},{96,64},{128,96},{160,128},{192,160},{224,1... | collective-permute-start | bytes 786440 | tf_op jit(solution)/shard_map/ppermute | solution.py:25
  104.0 9.2 %collective-permute-start.26 = (f32[64,128]{1,0:T(8,128)S(1)}, f32[64,128]{1,0:T(8,128)S(1)}, u32[]{:S(2)}, u32[]{:S(2)}) collective-permute-start(f32[64,128]{1,0:T(8,128)S(1)} %add.25), channel_id=1, source_target_pairs={{0,32},{32,64},{64,96},{96,128},{128,160},{160,192},{192,224},{224... | collective-permute-start | bytes 98312 | tf_op jit(solution)/shard_map/ppermute | solution.py:25
  106.3 7.0 %collective-permute-start.25 = (f32[64,128]{1,0:T(8,128)S(1)}, f32[64,128]{1,0:T(8,128)S(1)}, u32[]{:S(2)}, u32[]{:S(2)}) collective-permute-start(f32[64,128]{1,0:T(8,128)S(1)} %add.25), channel_id=1, source_target_pairs={{0,224},{32,0},{64,32},{96,64},{128,96},{160,128},{192,160},{224,1... | collective-permute-start | bytes 98312 | tf_op jit(solution)/shard_map/ppermute | solution.py:25
  106.8 20.1 %collective-permute-start.22 = (bf16[128,1024]{1,0:T(8,128)(2,1)S(1)}, bf16[128,1024]{1,0:T(8,128)(2,1)S(1)}, u32[]{:S(2)}, u32[]{:S(2)}) collective-permute-start(bf16[128,1024]{1,0:T(8,128)(2,1)S(1)} %get-tuple-element.46), channel_id=1, source_target_pairs={{8,0},{16,8},{24,16},{32,24},{40,32},{48,40},{56,48},{64,56},{72,6... | collective-permute-start | bytes 786440 | tf_op jit(solution)/shard_map/ppermute | solution.py:35
  111.2 18.1 %collective-permute-start.38 = (bf16[128,1024]{1,0:T(8,128)(2,1)S(1)}, bf16[128,1024]{1,0:T(8,128)(2,1)S(1)}, u32[]{:S(2)}, u32[]{:S(2)}) collective-permute-start(bf16[128,1024]{1,0:T(8,128)(2,1)S(1)} %get-tuple-element.62), channel_id=1, source_target_pairs={{0,32},{32,64},{64,96},{96,128},{128,160},{160,192},{192,224},{224... | collective-permute-start | bytes 786440 | tf_op jit(solution)/shard_map/ppermute | solution.py:25
  111.3 18.0 %collective-permute-start.39 = (bf16[128,1024]{1,0:T(8,128)(2,1)S(1)}, bf16[128,1024]{1,0:T(8,128)(2,1)S(1)}, u32[]{:S(2)}, u32[]{:S(2)}) collective-permute-start(bf16[128,1024]{1,0:T(8,128)(2,1)S(1)} %get-tuple-element.63), channel_id=1, source_target_pairs={{0,224},{32,0},{64,32},{96,64},{128,96},{160,128},{192,160},{224,1... | collective-permute-start | bytes 786440 | tf_op jit(solution)/shard_map/ppermute | solution.py:25
  113.3 7.7 %collective-permute-start.28 = (f32[64,128]{1,0:T(8,128)S(1)}, f32[64,128]{1,0:T(8,128)S(1)}, u32[]{:S(2)}, u32[]{:S(2)}) collective-permute-start(f32[64,128]{1,0:T(8,128)S(1)} %get-tuple-element.65), channel_id=1, source_target_pairs={{0,96},{32,128},{64,160},{96,192},{128,224},{160,0},{192,32},{224,... | collective-permute-start | bytes 98312 | tf_op jit(solution)/shard_map/ppermute | solution.py:25
  (16 other events, 150.4 us)

commit v3 on v2

--- a/solution.py
+++ b/solution.py
@@ -238,9 +238,9 @@
         copy.wait()
 
 
-def output_kernel(*refs):
-    u_refs, w_refs, own_ref, outs = refs[:8], refs[8:17], refs[17], refs[18:24]
-    w_all, total, sems = refs[24:]
+def output_kernel(places, *refs):
+    u_refs, w_refs, outs = refs[:8], refs[8:17], refs[17:-2]
+    w_all, sems = refs[-2:]
     z, y = lax.axis_index("z"), lax.axis_index("y")
     x, c = lax.axis_index("x"), lax.axis_index("c")
 
@@ -256,40 +256,48 @@
         start = pl.multiple_of(start, count)
         pairs.append((w_refs[at], w_all.at[pl.ds(start, count)]))
     run_copies(pairs, sems)
-    rows = own_ref.shape[0]
-    half = rows // 2
-    places = ((2, 0), (2, half), (1, half), (3, 0), (1, 0), (3, half))
+    rows = u_refs[0].shape[0] // 4
+    ahead = []
+    for d, *_ in places:
+        if d not in ahead:
+            ahead.append(d)
+    bands = []
+    for d in ahead:
+        band = pl.ds(pl.multiple_of(lax.rem(y + d, 4) * rows, rows), rows)
+        bands.append(jnp.concatenate([u_ref[band] for u_ref in u_refs], axis=1))
+    left = jnp.concatenate(bands, axis=0)
 
     def body(lanes):
-        left = jnp.concatenate([u_ref[...] for u_ref in u_refs], axis=1)
         sums = jnp.dot(left, w_all[:, lanes], preferred_element_type=F32)
-        total[:, lanes] = sums.astype(BF16)
-
-    for_columns(body, own_ref.shape[1])
-    own_ref[...] = total[pl.ds(pl.multiple_of(y * rows, rows), rows)]
-    for out, (d, at) in zip(outs, places):
-        start = pl.multiple_of(lax.rem(y + d, 4) * rows + at, half)
-        out[...] = total[pl.ds(start, half)]
-
-
-def output_partials(features, weights):
-    tokens, channels = features[0].shape[0], weights[0].shape[1]
-    shape = jax.ShapeDtypeStruct((tokens // 4, channels), BF16)
-    short = jax.ShapeDtypeStruct((tokens // 8, channels), BF16)
+        sums = sums.astype(BF16)
+        for out, (d, first, last) in zip(outs, places):
+            start = ahead.index(d) * rows
+            out[:, lanes] = sums[start + first : start + last]
+
+    for_columns(body, w_all.shape[1])
+
+
+def output_partials(features, weights, places):
+    channels = weights[0].shape[1]
     stored = (0, 1, 4)
     spaces = [pltpu.HBM if at in stored else pltpu.VMEM for at in range(9)]
     blocks = map(pltpu.with_memory_space_constraint, weights, spaces)
-    return pl.pallas_call(
-        output_kernel,
+
+    def kernel(*refs):
+        output_kernel(places, *refs)
+
+    return pl.pallas_call(
+        kernel,
         in_specs=[VMEM] * 8 + [ANY if at in stored else VMEM for at in range(9)],
-        out_specs=[VMEM] * 7,
-        out_shape=[shape] + [short] * 6,
+        out_specs=[VMEM] * len(places),
+        out_shape=[
+            jax.ShapeDtypeStruct((last - first, channels), BF16)
+            for _, first, last in places
+        ],
         scratch_shapes=[
             pltpu.VMEM((8 * LANES, channels), BF16),
-            pltpu.VMEM((tokens, channels), BF16),
             pltpu.SemaphoreType.DMA((9,)),
         ],
-        name="output_partials",
         compiler_params=LARGE,
     )(*on_chip(features), *blocks)
 
@@ -397,8 +405,11 @@
     mixed, conv_out = conv_forward(prior, conv_input, gate, filters)
     mixed = [mixed] + [shift(mixed, "y", d) for d in (1, 2, 3)]
 
-    own_sum, far_top, far_low, up_low, down_top, up_top, down_low = output_partials(
-        features, weights
+    mid = rows // 2
+    places = (2, 0, mid), (2, mid, rows), (1, mid, rows), (3, 0, mid)
+    places += (1, 0, mid), (3, mid, rows), (0, 0, rows)
+    far_top, far_low, up_low, down_top, up_top, down_low, own_sum = output_partials(
+        features, weights, places
     )
     top, low = shift(far_top, "y", 1), shift(far_low, "y", -1)
     from_below, from_above = shift(up_low, "y", 1), shift(down_top, "y", -1)

time: 131 us -> 131 us (level)
  transfers between devices with their start and end apart: 41 -> 41, of which waited for: 19 -> 20; matrix products, arithmetic and copies ran while one was open for 1% -> 1% of each run, Pallas kernels for 9% -> 9%
where the time goes in v3:
time: 131 us; the launch traced here: 130 us
  starting transfers between devices  59.2 us (45%)
  waiting for transfers between devices  52.7 us (40%)
  Pallas kernels  14.1 us (11%)
  local copies, waits for them, and re-layouts  1.75 us (1%)
  other arithmetic  1.48 us (1%)
    ppermute x38, waiting for transfers between devices, shift(): return lax.ppermute(block, axis, route)  47.5 us
    ppermute x38, starting transfers between devices, shift(): return lax.ppermute(block, axis, route)  46.5 us
    ppermute x2, starting transfers between devices, from_behind(): return lax.ppermute(block, SEQ, route)  8.12 us
    all_to_all x1, starting transfers between devices, exchanged(): return lax.all_to_all(blocks, axis, split_axis=0, concat_axis=0, tiled=True)  4.59 us
    ppermute x2, waiting for transfers between devices, from_behind(): return lax.ppermute(block, SEQ, route)  4.52 us
    pallas_call x1, Pallas kernels, output_partials(): pl.pallas_call(kernel, in_specs=[VMEM] * 8 + [ANY if at in stored else VM...  3.54 us
    pallas_call x1, Pallas kernels, output_gradients(): pl.pallas_call(gradient_kernel, grid=(channels // STEP,), in_specs=[tile(...  3.16 us
  transfers between devices with their start and end apart: 41, of which 20 were waited for; matrix products, arithmetic and copies ran while one was open for 1% of the time, Pallas kernels for 9%

profile of v3, /device:TPU:32, one launch (start us, length us, event | category | flops | bytes accessed | tf_op | source)
XLA Modules:
  0.0 130.1 jit_solution(5535376602519136372)
XLA Ops:
  2.3 4.6 %all-to-all-start = ((bf16[4,256,128]{2,1,0:T(8,128)(2,1)}), bf16[4,256,128]{2,1,0:T(8,128)(2,1)S(1)}, u32[]{:S(2)}, u32[]{:S(2)}) async-start(bf16[4,256,128]{2,1,0:T(8,128)(2,1)} %bitcast_bitcast_fusion), calls=%async_computation | async-start | bytes 524288 | tf_op jit(solution)/shard_map/all_to_all | solution.py:29
  6.9 1.9 %collective-permute-start.7 = (bf16[128,1024]{1,0:T(8,128)(2,1)S(1)}, bf16[128,1024]{1,0:T(8,128)(2,1)S(1)}, u32[]{:S(2)}, u32[]{:S(2)}) collective-permute-start(bf16[128,1024]{1,0:T(8,128)(2,1)S(1)} %copy-done.4), channel_id=1, source_target_pairs={{0,32},{32,64},{64,96},{96,128},{128,160},{160,192},{192,224},{224... | collective-permute-start | bytes 786440 | tf_op jit(solution)/shard_map/ppermute | solution.py:25
  9.0 3.9 %collective-permute-start.21 = (bf16[128,1024]{1,0:T(8,128)(2,1)S(1)}, bf16[128,1024]{1,0:T(8,128)(2,1)S(1)}, u32[]{:S(2)}, u32[]{:S(2)}) collective-permute-start(bf16[128,1024]{1,0:T(8,128)(2,1)S(1)} %slice.11), channel_id=1, source_target_pairs={{0,8},{8,16},{16,24},{24,32},{32,40},{40,48},{48,56},{56,64},{64,7... | collective-permute-start | bytes 786440 | tf_op jit(solution)/shard_map/ppermute | solution.py:35
  13.6 2.8 %collective-permute-start.2 = (bf16[1024,128]{1,0:T(8,128)(2,1)S(1)}, bf16[1024,128]{1,0:T(8,128)(2,1)S(1)}, u32[]{:S(2)}, u32[]{:S(2)}) collective-permute-start(bf16[1024,128]{1,0:T(8,128)(2,1)S(1)} %bitcast.9), channel_id=1, source_target_pairs={{0,6},{2,0},{4,2},{6,4},{1,7},{3,1},{5,3},{7,5},{8,14},{10,8},{12,... | collective-permute-start | bytes 786440 | tf_op jit(solution)/shard_map/ppermute | solution.py:25
  16.4 1.9 %collective-permute-start.8 = (bf16[128,1024]{1,0:T(8,128)(2,1)S(1)}, bf16[128,1024]{1,0:T(8,128)(2,1)S(1)}, u32[]{:S(2)}, u32[]{:S(2)}) collective-permute-start(bf16[128,1024]{1,0:T(8,128)(2,1)S(1)} %collective-permute-done.7.refs_9_), channel_id=1, source_target_pairs={{0,32},{32,64},{64,96},{96,128},{128,160},{160,192},{192,224},{224... | collective-permute-start | bytes 786440 | tf_op jit(solution)/shard_map/ppermute | solution.py:25
  20.0 4.5 %collective-permute-done.21.prev_ref.refs_7_ = bf16[128,1024]{1,0:T(8,128)(2,1)S(1)} collective-permute-done((bf16[128,1024]{1,0:T(8,128)(2,1)S(1)}, bf16[128,1024]{1,0:T(8,128)(2,1)S(1)}, u32[]{:S(2)}, u32[]{:S(2)}) %collective-permute-start.21) | collective-permute-done | bytes 262176 | tf_op jit(solution)/shard_map/ppermute | solution.py:35
  24.5 3.2 %collective-permute-start.1 = (bf16[1024,128]{1,0:T(8,128)(2,1)S(1)}, bf16[1024,128]{1,0:T(8,128)(2,1)S(1)}, u32[]{:S(2)}, u32[]{:S(2)}) collective-permute-start(bf16[1024,128]{1,0:T(8,128)(2,1)S(1)} %bitcast.10), channel_id=1, source_target_pairs={{0,4},{2,6},{4,0},{6,2},{1,5},{3,7},{5,1},{7,3},{8,12},{10,14},{12... | collective-permute-start | bytes 786440 | tf_op jit(solution)/shard_map/ppermute | solution.py:25
  30.0 1.8 %collective-permute-start.12 = (bf16[128,1024]{1,0:T(8,128)(2,1)S(1)}, bf16[128,1024]{1,0:T(8,128)(2,1)S(1)}, u32[]{:S(2)}, u32[]{:S(2)}) collective-permute-start(bf16[128,1024]{1,0:T(8,128)(2,1)S(1)} %collective-permute-done.11.refs_13_), channel_id=1, source_target_pairs={{0,224},{32,0},{64,32},{96,64},{128,96},{160,128},{192,160},{224,1... | collective-permute-start | bytes 786440 | tf_op jit(solution)/shard_map/ppermute | solution.py:25
  31.8 2.1 %conv_forward.1 = (bf16[256,1024]{1,0:T(8,128)(2,1)S(1)}, f32[256,1024]{1,0:T(8,128)S(1)}) custom-call(bf16[128,1024]{1,0:T(8,128)(2,1)S(1)} %collective-permute-done.21.prev_ref.refs_7_, bf16[256,1024]{1,0:T(8,128)(2,1)S(1)} %copy-done.1, bf16[256,1024]{1,0:T(8,128)(2,1)S(1)} %copy-done.2, bf16[64,128]{1,0:T(8,128)(2,1)S(1)} %copy-done.3), custom_call_target="tpu_custom_call" | custom-call | tf_op jit(solution)/shard_map/conv_forward/pallas_call | solution.py:110
  40.2 2.4 %collective-permute-start.13 = (bf16[64,1024]{1,0:T(8,128)(2,1)S(1)}, bf16[64,1024]{1,0:T(8,128)(2,1)S(1)}, u32[]{:S(2)}, u32[]{:S(2)}) collective-permute-start(bf16[64,1024]{1,0:T(8,128)(2,1)S(1)} %slice.12), channel_id=1, source_target_pairs={{0,32},{32,64},{64,96},{96,128},{128,160},{160,192},{192,224},{224... | collective-permute-start | bytes 393224 | tf_op jit(solution)/shard_map/ppermute | solution.py:25
  43.6 3.4 %collective-permute-done.13.refs_15_ = bf16[64,1024]{1,0:T(8,128)(2,1)S(1)} collective-permute-done((bf16[64,1024]{1,0:T(8,128)(2,1)S(1)}, bf16[64,1024]{1,0:T(8,128)(2,1)S(1)}, u32[]{:S(2)}, u32[]{:S(2)}) %collective-permute-start.13) | collective-permute-done | bytes 131104 | tf_op jit(solution)/shard_map/ppermute | solution.py:25
  47.0 2.5 %collective-permute-done.14.refs_16_ = bf16[64,1024]{1,0:T(8,128)(2,1)S(1)} collective-permute-done((bf16[64,1024]{1,0:T(8,128)(2,1)S(1)}, bf16[64,1024]{1,0:T(8,128)(2,1)S(1)}, u32[]{:S(2)}, u32[]{:S(2)}) %collective-permute-start.14) | collective-permute-done | bytes 131104 | tf_op jit(solution)/shard_map/ppermute | solution.py:25
  49.5 3.5 %shard_map.84 = (bf16[128,1024]{1,0:T(8,128)(2,1)S(1)}, bf16[128,1024]{1,0:T(8,128)(2,1)S(1)}, bf16[128,1024]{1,0:T(8,128)(2,1)S(1)}, bf16[128,1024]{1,0:T(8,128...) custom-call(bf16[1024,128]{1,0:T(8,128)(2,1)S(1)} %bitcast.12, ...), custom_call_target="tpu_custom_call" | custom-call | tf_op jit(solution)/shard_map/pallas_call | solution.py:289
  53.1 8.9 %collective-permute-done.29.refs_9_ = bf16[256,1024]{1,0:T(8,128)(2,1)S(1)} collective-permute-done((bf16[256,1024]{1,0:T(8,128)(2,1)S(1)}, bf16[256,1024]{1,0:T(8,128)(2,1)S(1)}, u32[]{:S(2)}, u32[]{:S(2)}) %collective-permute-start.29) | collective-permute-done | bytes 524320 | tf_op jit(solution)/shard_map/ppermute | solution.py:25
  62.0 2.5 %weight_partials.1 = (bf16[64,1024]{1,0:T(8,128)(2,1)S(1)}, bf16[64,1024]{1,0:T(8,128)(2,1)S(1)}, bf16[128,1024]{1,0:T(8,128)(2,1)S(1)}, bf16[128,1024]{1,0:T(8,...) custom-call(bf16[1024,128]{1,0:T(8,128)(2,1)S(1)} %bitcast.13, ...), custom_call_target="tpu_custom_call" | custom-call | tf_op jit(solution)/shard_map/weight_partials/pallas_call | solution.py:345
  64.6 3.1 %collective-permute-start.32 = (bf16[64,1024]{1,0:T(8,128)(2,1)S(1)}, bf16[64,1024]{1,0:T(8,128)(2,1)S(1)}, u32[]{:S(2)}, u32[]{:S(2)}) collective-permute-start(bf16[64,1024]{1,0:T(8,128)(2,1)S(1)} %get-tuple-element.50), channel_id=1, source_target_pairs={{0,32},{32,64},{64,96},{96,128},{128,160},{160,192},{192,224},{224... | collective-permute-start | bytes 393224 | tf_op jit(solution)/shard_map/ppermute | solution.py:25
  68.5 2.3 %collective-permute-start.16 = (bf16[128,1024]{1,0:T(8,128)(2,1)S(1)}, bf16[128,1024]{1,0:T(8,128)(2,1)S(1)}, u32[]{:S(2)}, u32[]{:S(2)}) collective-permute-start(bf16[128,1024]{1,0:T(8,128)(2,1)S(1)} %get-tuple-element.36), channel_id=1, source_target_pairs={{0,24},{8,0},{16,8},{24,16},{1,25},{9,1},{17,9},{25,17},{2,26},{10... | collective-permute-start | bytes 786440 | tf_op jit(solution)/shard_map/ppermute | solution.py:25
  70.9 2.1 %collective-permute-done.33.behind_ref = bf16[64,1024]{1,0:T(8,128)(2,1)S(1)} collective-permute-done((bf16[64,1024]{1,0:T(8,128)(2,1)S(1)}, bf16[64,1024]{1,0:T(8,128)(2,1)S(1)}, u32[]{:S(2)}, u32[]{:S(2)}) %collective-permute-start.33) | collective-permute-done | bytes 131104 | tf_op jit(solution)/shard_map/ppermute | solution.py:25
  73.1 2.8 %collective-permute-start.34 = (bf16[128,1024]{1,0:T(8,128)(2,1)S(1)}, bf16[128,1024]{1,0:T(8,128)(2,1)S(1)}, u32[]{:S(2)}, u32[]{:S(2)}) collective-permute-start(bf16[128,1024]{1,0:T(8,128)(2,1)S(1)} %get-tuple-element.54), channel_id=1, source_target_pairs={{0,32},{32,64},{64,96},{96,128},{128,160},{160,192},{192,224},{224... | collective-permute-start | bytes 786440 | tf_op jit(solution)/shard_map/ppermute | solution.py:25
  78.1 2.6 %collective-permute-done.34.ahead_ref = bf16[128,1024]{1,0:T(8,128)(2,1)S(1)} collective-permute-done((bf16[128,1024]{1,0:T(8,128)(2,1)S(1)}, bf16[128,1024]{1,0:T(8,128)(2,1)S(1)}, u32[]{:S(2)}, u32[]{:S(2)}) %collective-permute-start.34) | collective-permute-done | bytes 262176 | tf_op jit(solution)/shard_map/ppermute | solution.py:25
  81.3 2.5 %collective-permute-done.35.behind_ref = bf16[128,1024]{1,0:T(8,128)(2,1)S(1)} collective-permute-done((bf16[128,1024]{1,0:T(8,128)(2,1)S(1)}, bf16[128,1024]{1,0:T(8,128)(2,1)S(1)}, u32[]{:S(2)}, u32[]{:S(2)}) %collective-permute-start.35) | collective-permute-done | bytes 262176 | tf_op jit(solution)/shard_map/ppermute | solution.py:25
  84.0 1.8 %collective-permute-start.36 = (bf16[128,1024]{1,0:T(8,128)(2,1)S(1)}, bf16[128,1024]{1,0:T(8,128)(2,1)S(1)}, u32[]{:S(2)}, u32[]{:S(2)}) collective-permute-start(bf16[128,1024]{1,0:T(8,128)(2,1)S(1)} %get-tuple-element.58), channel_id=1, source_target_pairs={{0,32},{32,64},{64,96},{96,128},{128,160},{160,192},{192,224},{224... | collective-permute-start | bytes 786440 | tf_op jit(solution)/shard_map/ppermute | solution.py:25
  87.0 3.3 %collective-permute-done.17.refs_1_ = bf16[128,1024]{1,0:T(8,128)(2,1)S(1)} collective-permute-done((bf16[128,1024]{1,0:T(8,128)(2,1)S(1)}, bf16[128,1024]{1,0:T(8,128)(2,1)S(1)}, u32[]{:S(2)}, u32[]{:S(2)}) %collective-permute-start.17) | collective-permute-done | bytes 262176 | tf_op jit(solution)/shard_map/ppermute | solution.py:25
  90.3 3.2 %output_gradients.1 = (bf16[256,1024]{1,0:T(8,128)(2,1)}, bf16[256,1024]{1,0:T(8,128)(2,1)S(1)}, bf16[128,1024]{1,0:T(8,128)(2,1)S(1)}, f32[64,128]{1,0:T(8,128)S(1)}) custom-call(bf16[256,1024]{1,0:T(8,128)(2,1)S(1)} %get-tuple-element.34.refs_0_.refs_12_, bf16[128,1024]{1,0:T(8,128)(2,1)S(1)} %collective-permute-done.17.refs_1_, ...), custom_call_target="tpu_custom_call" | custom-call | tf_op jit(solution)/shard_map/output_gradients/pallas_call | solution.py:200
  93.5 5.1 %collective-permute-done.23 = f32[64,128]{1,0:T(8,128)S(1)} collective-permute-done((f32[64,128]{1,0:T(8,128)S(1)}, f32[64,128]{1,0:T(8,128)S(1)}, u32[]{:S(2)}, u32[]{:S(2)}) %collective-permute-start.23) | collective-permute-done | bytes 32800 | tf_op jit(solution)/shard_map/ppermute | solution.py:25
  98.6 5.4 %collective-permute-done.24 = f32[64,128]{1,0:T(8,128)S(1)} collective-permute-done((f32[64,128]{1,0:T(8,128)S(1)}, f32[64,128]{1,0:T(8,128)S(1)}, u32[]{:S(2)}, u32[]{:S(2)}) %collective-permute-start.24) | collective-permute-done | bytes 32800 | tf_op jit(solution)/shard_map/ppermute | solution.py:25
  104.0 2.3 %collective-permute-start.26 = (f32[64,128]{1,0:T(8,128)S(1)}, f32[64,128]{1,0:T(8,128)S(1)}, u32[]{:S(2)}, u32[]{:S(2)}) collective-permute-start(f32[64,128]{1,0:T(8,128)S(1)} %add.25), channel_id=1, source_target_pairs={{0,32},{32,64},{64,96},{96,128},{128,160},{160,192},{192,224},{224... | collective-permute-start | bytes 98312 | tf_op jit(solution)/shard_map/ppermute | solution.py:25
  106.8 4.2 %collective-permute-start.22 = (bf16[128,1024]{1,0:T(8,128)(2,1)S(1)}, bf16[128,1024]{1,0:T(8,128)(2,1)S(1)}, u32[]{:S(2)}, u32[]{:S(2)}) collective-permute-start(bf16[128,1024]{1,0:T(8,128)(2,1)S(1)} %get-tuple-element.46), channel_id=1, source_target_pairs={{8,0},{16,8},{24,16},{32,24},{40,32},{48,40},{56,48},{64,56},{72,6... | collective-permute-start | bytes 786440 | tf_op jit(solution)/shard_map/ppermute | solution.py:35
  111.3 2.0 %collective-permute-start.39 = (bf16[128,1024]{1,0:T(8,128)(2,1)S(1)}, bf16[128,1024]{1,0:T(8,128)(2,1)S(1)}, u32[]{:S(2)}, u32[]{:S(2)}) collective-permute-start(bf16[128,1024]{1,0:T(8,128)(2,1)S(1)} %get-tuple-element.63), channel_id=1, source_target_pairs={{0,224},{32,0},{64,32},{96,64},{128,96},{160,128},{192,160},{224,1... | collective-permute-start | bytes 786440 | tf_op jit(solution)/shard_map/ppermute | solution.py:25
  113.3 6.1 %collective-permute-start.28 = (f32[64,128]{1,0:T(8,128)S(1)}, f32[64,128]{1,0:T(8,128)S(1)}, u32[]{:S(2)}, u32[]{:S(2)}) collective-permute-start(f32[64,128]{1,0:T(8,128)S(1)} %get-tuple-element.65), channel_id=1, source_target_pairs={{0,96},{32,128},{64,160},{96,192},{128,224},{160,0},{192,32},{224,... | collective-permute-start | bytes 98312 | tf_op jit(solution)/shard_map/ppermute | solution.py:25
  121.0 5.3 %collective-permute-done.27 = f32[64,128]{1,0:T(8,128)S(1)} collective-permute-done((f32[64,128]{1,0:T(8,128)S(1)}, f32[64,128]{1,0:T(8,128)S(1)}, u32[]{:S(2)}, u32[]{:S(2)}) %collective-permute-start.27) | collective-permute-done | bytes 32800 | tf_op jit(solution)/shard_map/ppermute | solution.py:25
  126.9 2.3 %conv_backward.1 = bf16[256,1024]{1,0:T(8,128)(2,1)} custom-call(bf16[256,1024]{1,0:T(8,128)(2,1)S(1)} %get-tuple-element.45.d_ref, bf16[128,1024]{1,0:T(8,128)(2,1)S(1)} %collective-permute-done.22.next_ref, bf16[64,128]{1,0:T(8,128)(2,1)S(1)} %copy-done.3), custom_call_target="tpu_custom_call" | custom-call | tf_op jit(solution)/shard_map/conv_backward/pallas_call | solution.py:143
  (82 shorter events, 22.8 us)
Async XLA Ops:
  2.3 11.3 %all-to-all-start = ((bf16[4,256,128]{2,1,0:T(8,128)(2,1)}), bf16[4,256,128]{2,1,0:T(8,128)(2,1)S(1)}, u32[]{:S(2)}, u32[]{:S(2)}) async-start(bf16[4,256,128]{2,1,0:T(8,128)(2,1)} %bitcast_bitcast_fusion), calls=%async_computation | async-start | bytes 524288 | tf_op jit(solution)/shard_map/all_to_all | solution.py:29
  6.9 9.4 %collective-permute-start.7 = (bf16[128,1024]{1,0:T(8,128)(2,1)S(1)}, bf16[128,1024]{1,0:T(8,128)(2,1)S(1)}, u32[]{:S(2)}, u32[]{:S(2)}) collective-permute-start(bf16[128,1024]{1,0:T(8,128)(2,1)S(1)} %copy-done.4), channel_id=1, source_target_pairs={{0,32},{32,64},{64,96},{96,128},{128,160},{160,192},{192,224},{224... | collective-permute-start | bytes 786440 | tf_op jit(solution)/shard_map/ppermute | solution.py:25
  8.9 9.4 %collective-permute-start.10 = (bf16[128,1024]{1,0:T(8,128)(2,1)S(1)}, bf16[128,1024]{1,0:T(8,128)(2,1)S(1)}, u32[]{:S(2)}, u32[]{:S(2)}) collective-permute-start(bf16[128,1024]{1,0:T(8,128)(2,1)S(1)} %copy-done.4), channel_id=1, source_target_pairs={{0,224},{32,0},{64,32},{96,64},{128,96},{160,128},{192,160},{224,1... | collective-permute-start | bytes 786440 | tf_op jit(solution)/shard_map/ppermute | solution.py:25
  9.0 15.5 %collective-permute-start.21 = (bf16[128,1024]{1,0:T(8,128)(2,1)S(1)}, bf16[128,1024]{1,0:T(8,128)(2,1)S(1)}, u32[]{:S(2)}, u32[]{:S(2)}) collective-permute-start(bf16[128,1024]{1,0:T(8,128)(2,1)S(1)} %slice.11), channel_id=1, source_target_pairs={{0,8},{8,16},{16,24},{24,32},{32,40},{40,48},{48,56},{56,64},{64,7... | collective-permute-start | bytes 786440 | tf_op jit(solution)/shard_map/ppermute | solution.py:35
  13.6 14.2 %collective-permute-start.3 = (bf16[1024,128]{1,0:T(8,128)(2,1)S(1)}, bf16[1024,128]{1,0:T(8,128)(2,1)S(1)}, u32[]{:S(2)}, u32[]{:S(2)}) collective-permute-start(bf16[1024,128]{1,0:T(8,128)(2,1)S(1)} %bitcast.8), channel_id=1, source_target_pairs={{0,1},{1,0},{2,3},{3,2},{4,5},{5,4},{6,7},{7,6},{8,9},{9,8},{10,11... | collective-permute-start | bytes 786440 | tf_op jit(solution)/shard_map/ppermute | solution.py:25
  13.6 14.7 %collective-permute-start.2 = (bf16[1024,128]{1,0:T(8,128)(2,1)S(1)}, bf16[1024,128]{1,0:T(8,128)(2,1)S(1)}, u32[]{:S(2)}, u32[]{:S(2)}) collective-permute-start(bf16[1024,128]{1,0:T(8,128)(2,1)S(1)} %bitcast.9), channel_id=1, source_target_pairs={{0,6},{2,0},{4,2},{6,4},{1,7},{3,1},{5,3},{7,5},{8,14},{10,8},{12,... | collective-permute-start | bytes 786440 | tf_op jit(solution)/shard_map/ppermute | solution.py:25
  16.4 12.0 %collective-permute-start.8 = (bf16[128,1024]{1,0:T(8,128)(2,1)S(1)}, bf16[128,1024]{1,0:T(8,128)(2,1)S(1)}, u32[]{:S(2)}, u32[]{:S(2)}) collective-permute-start(bf16[128,1024]{1,0:T(8,128)(2,1)S(1)} %collective-permute-done.7.refs_9_), channel_id=1, source_target_pairs={{0,32},{32,64},{64,96},{96,128},{128,160},{160,192},{192,224},{224... | collective-permute-start | bytes 786440 | tf_op jit(solution)/shard_map/ppermute | solution.py:25
  18.3 11.7 %collective-permute-start.11 = (bf16[128,1024]{1,0:T(8,128)(2,1)S(1)}, bf16[128,1024]{1,0:T(8,128)(2,1)S(1)}, u32[]{:S(2)}, u32[]{:S(2)}) collective-permute-start(bf16[128,1024]{1,0:T(8,128)(2,1)S(1)} %collective-permute-done.10.refs_12_), channel_id=1, source_target_pairs={{0,224},{32,0},{64,32},{96,64},{128,96},{160,128},{192,160},{224,1... | collective-permute-start | bytes 786440 | tf_op jit(solution)/shard_map/ppermute | solution.py:25
  24.5 9.5 %collective-permute-start.1 = (bf16[1024,128]{1,0:T(8,128)(2,1)S(1)}, bf16[1024,128]{1,0:T(8,128)(2,1)S(1)}, u32[]{:S(2)}, u32[]{:S(2)}) collective-permute-start(bf16[1024,128]{1,0:T(8,128)(2,1)S(1)} %bitcast.10), channel_id=1, source_target_pairs={{0,4},{2,6},{4,0},{6,2},{1,5},{3,7},{5,1},{7,3},{8,12},{10,14},{12... | collective-permute-start | bytes 786440 | tf_op jit(solution)/shard_map/ppermute | solution.py:25
  27.8 9.0 %collective-permute-start = (bf16[1024,128]{1,0:T(8,128)(2,1)S(1)}, bf16[1024,128]{1,0:T(8,128)(2,1)S(1)}, u32[]{:S(2)}, u32[]{:S(2)}) collective-permute-start(bf16[1024,128]{1,0:T(8,128)(2,1)S(1)} %bitcast.11), channel_id=1, source_target_pairs={{0,2},{2,4},{4,6},{6,0},{1,3},{3,5},{5,7},{7,1},{8,10},{10,12},{12... | collective-permute-start | bytes 786440 | tf_op jit(solution)/shard_map/ppermute | solution.py:25
  28.4 9.5 %collective-permute-start.6 = (bf16[1024,128]{1,0:T(8,128)(2,1)S(1)}, bf16[1024,128]{1,0:T(8,128)(2,1)S(1)}, u32[]{:S(2)}, u32[]{:S(2)}) collective-permute-start(bf16[1024,128]{1,0:T(8,128)(2,1)S(1)} %collective-permute-done.2.refs_3_), channel_id=1, source_target_pairs={{0,1},{1,0},{2,3},{3,2},{4,5},{5,4},{6,7},{7,6},{8,9},{9,8},{10,11... | collective-permute-start | bytes 786440 | tf_op jit(solution)/shard_map/ppermute | solution.py:25
  28.4 10.3 %collective-permute-start.9 = (bf16[128,1024]{1,0:T(8,128)(2,1)S(1)}, bf16[128,1024]{1,0:T(8,128)(2,1)S(1)}, u32[]{:S(2)}, u32[]{:S(2)}) collective-permute-start(bf16[128,1024]{1,0:T(8,128)(2,1)S(1)} %collective-permute-done.8.refs_10_), channel_id=1, source_target_pairs={{0,32},{32,64},{64,96},{96,128},{128,160},{160,192},{192,224},{224... | collective-permute-start | bytes 786440 | tf_op jit(solution)/shard_map/ppermute | solution.py:25
  30.0 8.7 %collective-permute-start.12 = (bf16[128,1024]{1,0:T(8,128)(2,1)S(1)}, bf16[128,1024]{1,0:T(8,128)(2,1)S(1)}, u32[]{:S(2)}, u32[]{:S(2)}) collective-permute-start(bf16[128,1024]{1,0:T(8,128)(2,1)S(1)} %collective-permute-done.11.refs_13_), channel_id=1, source_target_pairs={{0,224},{32,0},{64,32},{96,64},{128,96},{160,128},{192,160},{224,1... | collective-permute-start | bytes 786440 | tf_op jit(solution)/shard_map/ppermute | solution.py:25
  34.1 18.9 %collective-permute-start.31 = (bf16[256,1024]{1,0:T(8,128)(2,1)S(1)}, bf16[256,1024]{1,0:T(8,128)(2,1)S(1)}, u32[]{:S(2)}, u32[]{:S(2)}) collective-permute-start(bf16[256,1024]{1,0:T(8,128)(2,1)S(1)} %get-tuple-element.48.refs_8_), channel_id=1, source_target_pairs={{0,24},{8,0},{16,8},{24,16},{1,25},{9,1},{17,9},{25,17},{2,26},{10... | collective-permute-start | bytes 1572872 | tf_op jit(solution)/shard_map/ppermute | solution.py:25
  36.8 16.3 %collective-permute-start.30 = (bf16[256,1024]{1,0:T(8,128)(2,1)S(1)}, bf16[256,1024]{1,0:T(8,128)(2,1)S(1)}, u32[]{:S(2)}, u32[]{:S(2)}) collective-permute-start(bf16[256,1024]{1,0:T(8,128)(2,1)S(1)} %get-tuple-element.48.refs_8_), channel_id=1, source_target_pairs={{0,16},{8,24},{16,0},{24,8},{1,17},{9,25},{17,1},{25,9},{2,18},{10... | collective-permute-start | bytes 1572872 | tf_op jit(solution)/shard_map/ppermute | solution.py:25
  37.9 24.2 %collective-permute-start.29 = (bf16[256,1024]{1,0:T(8,128)(2,1)S(1)}, bf16[256,1024]{1,0:T(8,128)(2,1)S(1)}, u32[]{:S(2)}, u32[]{:S(2)}) collective-permute-start(bf16[256,1024]{1,0:T(8,128)(2,1)S(1)} %get-tuple-element.48.refs_8_), channel_id=1, source_target_pairs={{0,8},{8,16},{16,24},{24,0},{1,9},{9,17},{17,25},{25,1},{2,10},{10... | collective-permute-start | bytes 1572872 | tf_op jit(solution)/shard_map/ppermute | solution.py:25
  67.7 8.9 %collective-permute-start.15 = (bf16[128,1024]{1,0:T(8,128)(2,1)S(1)}, bf16[128,1024]{1,0:T(8,128)(2,1)S(1)}, u32[]{:S(2)}, u32[]{:S(2)}) collective-permute-start(bf16[128,1024]{1,0:T(8,128)(2,1)S(1)} %get-tuple-element.35), channel_id=1, source_target_pairs={{0,8},{8,16},{16,24},{24,0},{1,9},{9,17},{17,25},{25,1},{2,10},{10... | collective-permute-start | bytes 786440 | tf_op jit(solution)/shard_map/ppermute | solution.py:25
  68.5 9.3 %collective-permute-start.16 = (bf16[128,1024]{1,0:T(8,128)(2,1)S(1)}, bf16[128,1024]{1,0:T(8,128)(2,1)S(1)}, u32[]{:S(2)}, u32[]{:S(2)}) collective-permute-start(bf16[128,1024]{1,0:T(8,128)(2,1)S(1)} %get-tuple-element.36), channel_id=1, source_target_pairs={{0,24},{8,0},{16,8},{24,16},{1,25},{9,1},{17,9},{25,17},{2,26},{10... | collective-permute-start | bytes 786440 | tf_op jit(solution)/shard_map/ppermute | solution.py:25
  73.1 7.7 %collective-permute-start.34 = (bf16[128,1024]{1,0:T(8,128)(2,1)S(1)}, bf16[128,1024]{1,0:T(8,128)(2,1)S(1)}, u32[]{:S(2)}, u32[]{:S(2)}) collective-permute-start(bf16[128,1024]{1,0:T(8,128)(2,1)S(1)} %get-tuple-element.54), channel_id=1, source_target_pairs={{0,32},{32,64},{64,96},{96,128},{128,160},{160,192},{192,224},{224... | collective-permute-start | bytes 786440 | tf_op jit(solution)/shard_map/ppermute | solution.py:25
  75.8 8.0 %collective-permute-start.35 = (bf16[128,1024]{1,0:T(8,128)(2,1)S(1)}, bf16[128,1024]{1,0:T(8,128)(2,1)S(1)}, u32[]{:S(2)}, u32[]{:S(2)}) collective-permute-start(bf16[128,1024]{1,0:T(8,128)(2,1)S(1)} %get-tuple-element.55), channel_id=1, source_target_pairs={{0,224},{32,0},{64,32},{96,64},{128,96},{160,128},{192,160},{224,1... | collective-permute-start | bytes 786440 | tf_op jit(solution)/shard_map/ppermute | solution.py:25
  75.8 10.0 %collective-permute-start.18 = (bf16[128,1024]{1,0:T(8,128)(2,1)S(1)}, bf16[128,1024]{1,0:T(8,128)(2,1)S(1)}, u32[]{:S(2)}, u32[]{:S(2)}) collective-permute-start(bf16[128,1024]{1,0:T(8,128)(2,1)S(1)} %get-tuple-element.40), channel_id=1, source_target_pairs={{0,24},{8,0},{16,8},{24,16},{1,25},{9,1},{17,9},{25,17},{2,26},{10... | collective-permute-start | bytes 786440 | tf_op jit(solution)/shard_map/ppermute | solution.py:25
  76.6 10.4 %collective-permute-start.19 = (bf16[128,1024]{1,0:T(8,128)(2,1)S(1)}, bf16[128,1024]{1,0:T(8,128)(2,1)S(1)}, u32[]{:S(2)}, u32[]{:S(2)}) collective-permute-start(bf16[128,1024]{1,0:T(8,128)(2,1)S(1)} %get-tuple-element.41), channel_id=1, source_target_pairs={{0,8},{8,16},{16,24},{24,0},{1,9},{9,17},{17,25},{25,1},{2,10},{10... | collective-permute-start | bytes 786440 | tf_op jit(solution)/shard_map/ppermute | solution.py:25
  78.0 12.3 %collective-permute-start.17 = (bf16[128,1024]{1,0:T(8,128)(2,1)S(1)}, bf16[128,1024]{1,0:T(8,128)(2,1)S(1)}, u32[]{:S(2)}, u32[]{:S(2)}) collective-permute-start(bf16[128,1024]{1,0:T(8,128)(2,1)S(1)} %get-tuple-element.39), channel_id=1, source_target_pairs={{0,8},{8,16},{16,24},{24,0},{1,9},{9,17},{17,25},{25,1},{2,10},{10... | collective-permute-start | bytes 786440 | tf_op jit(solution)/shard_map/ppermute | solution.py:25
  80.7 9.6 %collective-permute-start.20 = (bf16[128,1024]{1,0:T(8,128)(2,1)S(1)}, bf16[128,1024]{1,0:T(8,128)(2,1)S(1)}, u32[]{:S(2)}, u32[]{:S(2)}) collective-permute-start(bf16[128,1024]{1,0:T(8,128)(2,1)S(1)} %get-tuple-element.42), channel_id=1, source_target_pairs={{0,24},{8,0},{16,8},{24,16},{1,25},{9,1},{17,9},{25,17},{2,26},{10... | collective-permute-start | bytes 786440 | tf_op jit(solution)/shard_map/ppermute | solution.py:25
  84.0 27.1 %collective-permute-start.36 = (bf16[128,1024]{1,0:T(8,128)(2,1)S(1)}, bf16[128,1024]{1,0:T(8,128)(2,1)S(1)}, u32[]{:S(2)}, u32[]{:S(2)}) collective-permute-start(bf16[128,1024]{1,0:T(8,128)(2,1)S(1)} %get-tuple-element.58), channel_id=1, source_target_pairs={{0,32},{32,64},{64,96},{96,128},{128,160},{160,192},{192,224},{224... | collective-permute-start | bytes 786440 | tf_op jit(solution)/shard_map/ppermute | solution.py:25
  85.8 25.2 %collective-permute-start.37 = (bf16[128,1024]{1,0:T(8,128)(2,1)S(1)}, bf16[128,1024]{1,0:T(8,128)(2,1)S(1)}, u32[]{:S(2)}, u32[]{:S(2)}) collective-permute-start(bf16[128,1024]{1,0:T(8,128)(2,1)S(1)} %get-tuple-element.59), channel_id=1, source_target_pairs={{0,224},{32,0},{64,32},{96,64},{128,96},{160,128},{192,160},{224,1... | collective-permute-start | bytes 786440 | tf_op jit(solution)/shard_map/ppermute | solution.py:25
  104.0 9.2 %collective-permute-start.26 = (f32[64,128]{1,0:T(8,128)S(1)}, f32[64,128]{1,0:T(8,128)S(1)}, u32[]{:S(2)}, u32[]{:S(2)}) collective-permute-start(f32[64,128]{1,0:T(8,128)S(1)} %add.25), channel_id=1, source_target_pairs={{0,32},{32,64},{64,96},{96,128},{128,160},{160,192},{192,224},{224... | collective-permute-start | bytes 98312 | tf_op jit(solution)/shard_map/ppermute | solution.py:25
  106.3 7.0 %collective-permute-start.25 = (f32[64,128]{1,0:T(8,128)S(1)}, f32[64,128]{1,0:T(8,128)S(1)}, u32[]{:S(2)}, u32[]{:S(2)}) collective-permute-start(f32[64,128]{1,0:T(8,128)S(1)} %add.25), channel_id=1, source_target_pairs={{0,224},{32,0},{64,32},{96,64},{128,96},{160,128},{192,160},{224,1... | collective-permute-start | bytes 98312 | tf_op jit(solution)/shard_map/ppermute | solution.py:25
  106.8 20.1 %collective-permute-start.22 = (bf16[128,1024]{1,0:T(8,128)(2,1)S(1)}, bf16[128,1024]{1,0:T(8,128)(2,1)S(1)}, u32[]{:S(2)}, u32[]{:S(2)}) collective-permute-start(bf16[128,1024]{1,0:T(8,128)(2,1)S(1)} %get-tuple-element.46), channel_id=1, source_target_pairs={{8,0},{16,8},{24,16},{32,24},{40,32},{48,40},{56,48},{64,56},{72,6... | collective-permute-start | bytes 786440 | tf_op jit(solution)/shard_map/ppermute | solution.py:35
  111.2 18.1 %collective-permute-start.38 = (bf16[128,1024]{1,0:T(8,128)(2,1)S(1)}, bf16[128,1024]{1,0:T(8,128)(2,1)S(1)}, u32[]{:S(2)}, u32[]{:S(2)}) collective-permute-start(bf16[128,1024]{1,0:T(8,128)(2,1)S(1)} %get-tuple-element.62), channel_id=1, source_target_pairs={{0,32},{32,64},{64,96},{96,128},{128,160},{160,192},{192,224},{224... | collective-permute-start | bytes 786440 | tf_op jit(solution)/shard_map/ppermute | solution.py:25
  111.3 18.0 %collective-permute-start.39 = (bf16[128,1024]{1,0:T(8,128)(2,1)S(1)}, bf16[128,1024]{1,0:T(8,128)(2,1)S(1)}, u32[]{:S(2)}, u32[]{:S(2)}) collective-permute-start(bf16[128,1024]{1,0:T(8,128)(2,1)S(1)} %get-tuple-element.63), channel_id=1, source_target_pairs={{0,224},{32,0},{64,32},{96,64},{128,96},{160,128},{192,160},{224,1... | collective-permute-start | bytes 786440 | tf_op jit(solution)/shard_map/ppermute | solution.py:25
  113.3 7.7 %collective-permute-start.28 = (f32[64,128]{1,0:T(8,128)S(1)}, f32[64,128]{1,0:T(8,128)S(1)}, u32[]{:S(2)}, u32[]{:S(2)}) collective-permute-start(f32[64,128]{1,0:T(8,128)S(1)} %get-tuple-element.65), channel_id=1, source_target_pairs={{0,96},{32,128},{64,160},{96,192},{128,224},{160,0},{192,32},{224,... | collective-permute-start | bytes 98312 | tf_op jit(solution)/shard_map/ppermute | solution.py:25
  (16 other events, 150.4 us)
